TPU v7x, 256 devices: a whole 4x4x8 slice. The times are simulated.
256 devices in a mesh: segment: 2 (over core), expert: 128 (over z, y, x).
Axes of the slice: x: 4, y: 4, z: 8, core: 2. Of those that a mesh axis runs over, the one named last changes fastest.
Arguments:
- saved_input: bfloat16 [2, 2, 8192, 2048], P('segment', None, 'expert'), may hold values from -6 to 6
- out_grad: bfloat16 [2, 8192, 2048], P(None, 'expert'), may hold values from -6 to 6
- expert_ids: int32 [2, 2, 8192, 2], P('segment', None, 'expert'), may hold values from 0 to 127, all different within a row; in each aligned block of 64 rows (0 to 63, 64 to 127, ..., all dimensions but the last counted through in order) at most 2 rows name the same one
- router_weights: float32 [2, 2, 8192, 2], P('segment', None, 'expert'), may hold values from 0.1 to 0.9
- w_gate: bfloat16 [2, 128, 2048, 384], P('segment', 'expert'), may hold values from -0.125 to 0.125
- w_up: bfloat16 [2, 128, 2048, 384], P('segment', 'expert'), may hold values from -0.125 to 0.125
- w_down: bfloat16 [2, 128, 384, 2048], P('segment', 'expert'), may hold values from -0.3125 to 0.3125
- eigenbasis: bfloat16 [2, 128, 384, 384], P('segment', 'expert'), may hold values from -0.3125 to 0.3125
Outputs:
- input_grad: bfloat16 [2, 2, 8192, 2048], P('segment', None, 'expert')
- rotated_grad: bfloat16 [2, 128, 384, 2048], P('segment', 'expert')
- ekfac_scales: float32 [2, 128, 384, 2048], P('segment', 'expert')
Inputs may be any that keep to these rules, and one draw needn't show every extreme that they name: `expert_ids`: the two experts of a token differ. In each layer and micro-batch, at most 2 rows of one block of 64 tokens choose the same expert, and some block reaches 2.
All inputs are finite; a program needn't handle non-finite values.
Results may differ from a plain program's by a relative error of at most 0.0085.
Values may be sent and summed in bfloat16 or wider, within the bound.
No kernel may reach another device: no remote copies, remote signals or barrier semaphores. Data moves between devices by JAX's collectives and lax.ppermute only.
A program may use at most 128 MiB of HBM per device.

v0:
```python
import functools
import jax
import jax.numpy as jnp
from jax import lax
from jax.experimental import pallas as pl
from jax.experimental.pallas import tpu as pltpu
from jax.sharding import PartitionSpec as P

LANES = 128
CAP = 2
F32 = jnp.float32
BF16 = jnp.bfloat16
SMEM = pl.BlockSpec(memory_space=pltpu.SMEM)
VMEM = pl.BlockSpec(memory_space=pltpu.VMEM)


def rows_to_tiles(rows, tiles, count, depth):
    for j in range(depth):
        tiles[pl.ds(j, count, stride=depth), :] = rows[:, j * LANES : (j + 1) * LANES]


def tiles_to_rows(tiles, rows, count, depth):
    for j in range(depth):
        rows[:, j * LANES : (j + 1) * LANES] = tiles[pl.ds(j, count, stride=depth), :].astype(
            rows.dtype
        )


def clear(send, experts):
    zero = jnp.zeros(send.shape[1:], send.dtype)

    def one(e, carry):
        send[e] = zero
        return carry

    lax.fori_loop(0, experts, one, 0, unroll=4)


def dispatch_kernel(
    here, own_ids, other_ids, own_w, other_w, own_x, other_x, grad, send, slots, grad_tiles,
    x_upper, x_lower, g_tiles, counts,
):
    tokens, width = grad.shape
    depth = width // LANES
    experts = send.shape[0]
    upper = here[0] == 1
    own = own_x[...].astype(F32)
    other = other_x[...].astype(F32)
    rows_to_tiles(jnp.where(upper, own, other), x_upper, tokens, depth)
    rows_to_tiles(jnp.where(upper, other, own), x_lower, tokens, depth)
    rows_to_tiles(grad[...].astype(F32), g_tiles, tokens, depth)
    clear(send, experts)

    def reset(e, carry):
        counts[0, e] = 0
        counts[1, e] = 0
        return carry

    lax.fori_loop(0, experts, reset, 0, unroll=8)

    def token(t, carry):
        at = pl.ds(pl.multiple_of(t * depth, depth), depth)
        up = x_upper[at, :].astype(BF16)
        low = x_lower[at, :].astype(BF16)
        g = g_tiles[at, :]
        grad_tiles[t] = g.astype(BF16)
        for k in range(2):
            p = 2 * t + k
            mine, theirs = own_ids[p], other_ids[p]
            e1 = jnp.where(upper, mine, theirs)
            e0 = jnp.where(upper, theirs, mine)
            c1 = jnp.minimum(counts[0, e1], CAP - 1)
            c0 = jnp.minimum(counts[1, e0], CAP - 1)
            counts[0, e1] = c1 + 1
            counts[1, e0] = c0 + 1
            slots[0, p] = e0 * CAP + c0
            slots[1, p] = e1 * CAP + c1
            weight = jnp.where(upper, own_w[p], other_w[p])
            send[e1, c1] = up
            send[e1, CAP + c1] = (weight * g).astype(BF16)
            send[e0, 2 * CAP + c0] = low
        return carry

    lax.fori_loop(0, tokens, token, 0)


def relay_kernel(here, slots, own_w, other_w, back, upstream, send, grad_out):
    tokens = upstream.shape[0]
    experts = send.shape[0]
    upper = here[0] == 1
    clear(send, experts)

    def token(t, carry):
        total = upstream[t].astype(F32)
        for k in range(2):
            s = slots[1, 2 * t + k]
            total = total + back[s // CAP, s % CAP].astype(F32)
        rounded = total.astype(BF16)
        grad_out[t] = rounded
        g = rounded.astype(F32)
        for k in range(2):
            p = 2 * t + k
            s = slots[0, p]
            weight = jnp.where(upper, other_w[p], own_w[p])
            send[s // CAP, s % CAP] = (weight * g).astype(BF16)
        return carry

    lax.fori_loop(0, tokens, token, 0)


def finish_kernel(here, slots, back, upstream, keep, away, low, up):
    tokens, depth = upstream.shape[0], upstream.shape[1]
    upper = here[0] == 1

    def token(t, carry):
        at = pl.ds(pl.multiple_of(t * depth, depth), depth)
        g = upstream[t].astype(F32)
        up[at, :] = g
        total = g
        for k in range(2):
            s = slots[0, 2 * t + k]
            total = total + back[s // CAP, s % CAP].astype(F32)
        low[at, :] = total
        return carry

    lax.fori_loop(0, tokens, token, 0)
    for j in range(depth):
        columns = slice(j * LANES, (j + 1) * LANES)
        high = up[pl.ds(j, tokens, stride=depth), :]
        down = low[pl.ds(j, tokens, stride=depth), :]
        keep[:, columns] = jnp.where(upper, high, down).astype(BF16)
        away[:, columns] = jnp.where(upper, down, high).astype(BF16)


def untile(block, tiles, rows):
    experts, cap, depth, lanes = block.shape
    count = experts * cap
    tiles[...] = block[...].astype(F32).reshape(count * depth, lanes)
    tiles_to_rows(tiles, rows, count, depth)


def forward_parts(rows, gate_up):
    hidden = jnp.dot(rows, gate_up, preferred_element_type=F32)
    half = hidden.shape[1] // 2
    gate, up = hidden[:, :half], hidden[:, half:]
    sigma = 1.0 / (1.0 + jnp.exp(-gate))
    act = gate * sigma
    dact = sigma * (1.0 + gate * (1.0 - sigma))
    return act, up * dact, (act * up).astype(BF16)


def backward_parts(act, slope, dy_rows, down_t, gate_up_t, tiles, send):
    experts, cap, depth, lanes = send.shape
    count = experts * cap
    grad_act = jnp.dot(dy_rows[...], down_t[...], preferred_element_type=F32)
    both = jnp.concatenate(
        [(grad_act * slope).astype(BF16), (grad_act * act).astype(BF16)], axis=1
    )
    dx = jnp.dot(both, gate_up_t[...], preferred_element_type=F32)
    rows_to_tiles(dx, tiles, count, depth)
    send[...] = tiles[...].reshape(experts, cap, depth, lanes).astype(BF16)


def upper_kernel(x, dy, gate_up, down_t, gate_up_t, send, dy_rows, activ, tiles, x_rows):
    untile(x, tiles, x_rows)
    act, slope, rounded = forward_parts(x_rows[...], gate_up[...])
    activ[...] = rounded
    untile(dy, tiles, dy_rows)
    backward_parts(act, slope, dy_rows, down_t, gate_up_t, tiles, send)


def forward_kernel(x, gate_up, act_out, slope_out, activ, tiles, x_rows):
    untile(x, tiles, x_rows)
    act, slope, rounded = forward_parts(x_rows[...], gate_up[...])
    act_out[...] = act
    slope_out[...] = slope
    activ[...] = rounded


def lower_kernel(dy, act, slope, down_t, gate_up_t, send, dy_rows, tiles):
    untile(dy, tiles, dy_rows)
    backward_parts(act[...], slope[...], dy_rows, down_t, gate_up_t, tiles, send)


def whole(block, at):
    return pl.BlockSpec(block, lambda i: at)


def call(kernel, args, in_specs, out_shape, out_specs, scratch, flops, moved):
    return pl.pallas_call(
        kernel,
        grid=(1,),
        in_specs=in_specs,
        out_shape=out_shape,
        out_specs=out_specs,
        scratch_shapes=scratch,
        compiler_params=pltpu.CompilerParams(vmem_limit_bytes=48 * 1024 * 1024),
        cost_estimate=pl.CostEstimate(flops=flops, bytes_accessed=moved, transcendentals=0),
    )(*args)


def swapped(block):
    return lax.ppermute(block, "segment", [(0, 1), (1, 0)])


def exchanged(block):
    return lax.all_to_all(block, "expert", split_axis=0, concat_axis=0, tiled=True)


def shape(dims, kind=BF16):
    return jax.ShapeDtypeStruct(dims, kind)


def shards(saved_input, out_grad, expert_ids, router_weights, w_gate, w_up, w_down, eigenbasis):
    experts = lax.axis_size("expert")
    segment = lax.axis_index("segment")
    upper = segment == 1
    micros, tokens, width = saved_input.shape[1:]
    hidden = w_gate.shape[-1]
    depth = width // LANES
    count = experts * CAP
    here = segment.astype(jnp.int32).reshape(1)

    ids = expert_ids[0].reshape(micros, tokens * 2)
    weights = router_weights[0].reshape(micros, tokens * 2)
    mine = functools.partial(lax.dynamic_index_in_dim, index=segment, axis=0, keepdims=False)
    theirs = functools.partial(lax.dynamic_index_in_dim, index=1 - segment, axis=0, keepdims=False)
    own_ids, other_ids = mine(ids), swapped(theirs(ids))
    own_w, other_w = mine(weights), swapped(theirs(weights))
    own_x, other_x = mine(saved_input[0]), swapped(theirs(saved_input[0]))
    grad = mine(out_grad)

    tile_rows = tokens * depth
    send, slots, grad_tiles = call(
        dispatch_kernel,
        (here, own_ids, other_ids, own_w, other_w, own_x, other_x, grad),
        [SMEM] * 5 + [VMEM] * 3,
        (
            shape((experts, 3 * CAP, depth, LANES)),
            shape((2, tokens * 2), jnp.int32),
            shape((tokens, depth, LANES)),
        ),
        (VMEM, SMEM, VMEM),
        [pltpu.VMEM((tile_rows, LANES), F32)] * 3 + [pltpu.SMEM((2, experts), jnp.int32)],
        1_000_000,
        5_000_000,
    )
    arrived = exchanged(send)

    other_gate, other_up = swapped(w_gate[0, 0]), swapped(w_up[0, 0])
    other_down, other_basis = swapped(w_down[0, 0]), swapped(eigenbasis[0, 0])

    def of_layer(layer):
        here_now = segment == layer
        gate = jnp.where(here_now, w_gate[0, 0], other_gate)
        up = jnp.where(here_now, w_up[0, 0], other_up)
        down = jnp.where(here_now, w_down[0, 0], other_down)
        basis = jnp.where(here_now, eigenbasis[0, 0], other_basis)
        gate_up = jnp.concatenate([gate, up], axis=1)
        return gate_up, down.T, gate_up.T, basis

    gate_up1, down_t1, gate_up_t1, basis1 = of_layer(1)
    gate_up0, down_t0, gate_up_t0, basis0 = of_layer(0)

    part = (experts, CAP, depth, LANES)
    tiles = pltpu.VMEM((count * depth, LANES), F32)
    rows = pltpu.VMEM((count, width), BF16)
    mat = 2 * count * width * hidden
    back_send, dy_rows1, activ1 = call(
        upper_kernel,
        (arrived, arrived, gate_up1, down_t1, gate_up_t1),
        [whole(part, (0, 0, 0, 0)), whole(part, (0, 1, 0, 0))] + [VMEM] * 3,
        (shape(part), shape((count, width)), shape((count, hidden))),
        (VMEM,) * 3,
        [tiles, rows],
        5 * mat,
        9_000_000,
    )
    back = exchanged(back_send)
    act0, slope0, activ0 = call(
        forward_kernel,
        (arrived, gate_up0),
        [whole(part, (0, 2, 0, 0)), VMEM],
        (shape((count, hidden), F32), shape((count, hidden), F32), shape((count, hidden))),
        (VMEM,) * 3,
        [tiles, rows],
        2 * mat,
        5_000_000,
    )
    rotated1 = jnp.dot(activ1, basis1, preferred_element_type=F32).astype(BF16)
    rotated0 = jnp.dot(activ0, basis0, preferred_element_type=F32).astype(BF16)

    dy_send, grad1 = call(
        relay_kernel,
        (here, slots, own_w, other_w, back, grad_tiles),
        [SMEM] * 4 + [VMEM] * 2,
        (shape(part), shape((tokens, depth, LANES))),
        (VMEM,) * 2,
        [],
        1_000_000,
        3_000_000,
    )
    dy = exchanged(dy_send)
    back_send0, dy_rows0 = call(
        lower_kernel,
        (dy, act0, slope0, down_t0, gate_up_t0),
        [VMEM] * 5,
        (shape(part), shape((count, width))),
        (VMEM,) * 2,
        [tiles],
        3 * mat,
        8_000_000,
    )
    back0 = exchanged(back_send0)

    all_rotated = jnp.concatenate(
        [
            jnp.where(upper, rotated1, rotated0),
            swapped(jnp.where(upper, rotated0, rotated1)),
        ],
        axis=0,
    )
    all_dy = jnp.concatenate(
        [
            jnp.where(upper, dy_rows1, dy_rows0),
            swapped(jnp.where(upper, dy_rows0, dy_rows1)),
        ],
        axis=0,
    )
    rot_sq = (all_rotated.astype(F32) ** 2).astype(BF16)
    dy_sq = (all_dy.astype(F32) ** 2).astype(BF16)
    over_rows = (((0,), (0,)), ((), ()))
    grad_sum = lax.dot_general(all_rotated, all_dy, over_rows, preferred_element_type=F32)
    scale_sum = lax.dot_general(rot_sq, dy_sq, over_rows, preferred_element_type=F32)
    rotated_grad = (grad_sum * (1.0 / micros)).astype(BF16)
    ekfac_scales = scale_sum * (1.0 / micros)

    keep, away = call(
        finish_kernel,
        (here, slots, back0, grad1),
        [SMEM] * 2 + [VMEM] * 2,
        (shape((tokens, width)), shape((tokens, width))),
        (VMEM,) * 2,
        [pltpu.VMEM((tile_rows, LANES), F32)] * 2,
        1_000_000,
        2_000_000,
    )
    came = swapped(away)
    grads = jnp.stack([jnp.where(upper, came, keep), jnp.where(upper, keep, came)])
    return (grads[None], rotated_grad[None, None], ekfac_scales[None, None])


def solution(mesh):
    in_specs = (
        P("segment", None, "expert", None),
        P(None, "expert", None),
        P("segment", None, "expert", None),
        P("segment", None, "expert", None),
        P("segment", "expert", None, None),
        P("segment", "expert", None, None),
        P("segment", "expert", None, None),
        P("segment", "expert", None, None),
    )
    out_specs = (
        P("segment", None, "expert", None),
        P("segment", "expert", None, None),
        P("segment", "expert", None, None),
    )
    return jax.shard_map(shards, mesh=mesh, in_specs=in_specs, out_specs=out_specs, check_vma=False)
```

profile of v0, /device:TPU:1, one launch (start us, length us, event | category | flops | bytes accessed | tf_op | source)
XLA Modules:
  0.0 250.3 jit_solution(335988483824870569)
XLA Ops:
  1.7 3.3 %collective-permute-start.1 = (f32[128]{0:T(128)S(1)}, f32[128]{0:T(128)S(1)}, u32[]{:S(2)}, u32[]{:S(2)}) collective-permute-start(f32[128]{0:T(128)S(1)} %get-tuple-element.51), channel_id=1, source_target_pairs={{0,128},{128,0},{1,129},{129,1},{2,130},{130,2},{3,131},{131,3},{4... | collective-permute-start | bytes 1544 | tf_op jit(solution)/shard_map/ppermute | solution.py:203
  8.5 4.9 %shard_map.103 = (bf16[128,6,16,128]{3,2,1,0:T(8,128)(2,1)S(1)}, s32[2,128]{1,0:T(2,128)S(1)}, bf16[64,16,128]{2,1,0:T(8,128)(2,1)S(1)}) custom-call(s32[1]{0:T(128)} %bitcast.here, s32[128]{0:T(128)S(1)} %get-tuple-element.54.own_ids, s32[128]{0:T(128)S(1)} %collective-permute-done.other_ids, f32[128]{0:T(128)S(1)} %get-tuple-element.52.own_w, ...), custom_call_target="tpu_custom_call" | custom-call | flops 1000000 | bytes 5000000 | tf_op jit(solution)/shard_map/pallas_call | solution.py:190
  13.5 1.7 copy-done.6
  15.1 13.8 %all-to-all-start = ((bf16[128,6,16,128]{3,2,1,0:T(8,128)(2,1)}), bf16[128,6,16,128]{3,2,1,0:T(8,128)(2,1)S(1)}, u32[]{:S(2)}, u32[]{:S(2)}) async-start(bf16[128,6,16,128]{3,2,1,0:T(8,128)(2,1)} %copy-done.6), calls=%async_computation | async-start | bytes 6291456 | tf_op jit(solution)/shard_map/all_to_all | solution.py:207
  28.9 2.7 %copy.18 = bf16[1,1,2048,384]{2,3,1,0:T(8,128)(2,1)} copy(bf16[1,1,2048,384]{3,2,1,0:T(8,128)(2,1)} %param.12) | data formatting | bytes 3145728 | tf_op args[4]
  32.1 2.6 %copy.19 = bf16[1,1,2048,384]{2,3,1,0:T(8,128)(2,1)} copy(bf16[1,1,2048,384]{3,2,1,0:T(8,128)(2,1)} %param.13) | data formatting | bytes 3145728 | tf_op args[5]
  34.7 2.6 %copy.20 = bf16[1,1,384,2048]{2,3,1,0:T(8,128)(2,1)} copy(bf16[1,1,384,2048]{3,2,1,0:T(8,128)(2,1)} %param.14) | data formatting | bytes 3145728 | tf_op args[6]
  37.8 3.4 %broadcast_select_fusion.1 = (bf16[2048,384]{0,1:T(8,128)(2,1)}, bf16[2048,384]{0,1:T(8,128)(2,1)S(1)}) fusion(bf16[2048,384]{0,1:T(8,128)(2,1)} %collective-permute-done.3, pred[]{:T(512)S(6)} %eq.8, bf16[1,1,2048,384]{2,3,1,0:T(8,128)(2,1)} %copy.18, pred[]{:T(512)S(6)} %eq.7), kind=kLoop, calls=%fused_computation.10 | loop fusion | flops 1572864 | bytes 6291458 | tf_op jit(solution)/shard_map/jit(_where)/select_n | solution.py:255
  41.2 2.8 %broadcast_select_fusion = (bf16[2048,384]{0,1:T(8,128)(2,1)}, bf16[2048,384]{0,1:T(8,128)(2,1)S(1)}) fusion(bf16[2048,384]{0,1:T(8,128)(2,1)} %collective-permute-done.4, pred[]{:T(512)S(6)} %eq.8, bf16[1,1,2048,384]{2,3,1,0:T(8,128)(2,1)S(1)} %copy-done.20, pred[]{:T(512)S(6)} %eq.7), kind=kLoop, calls=%fused_computation.9 | loop fusion | flops 1572864 | bytes 6291458 | tf_op jit(solution)/shard_map/jit(_where)/select_n | solution.py:256
  44.0 3.4 %fusion.14 = (bf16[768,2048]{1,0:T(8,128)(2,1)}, bf16[2048,768]{0,1:T(8,128)(2,1)}) fusion(bf16[2048,384]{0,1:T(8,128)(2,1)S(1)} %get-tuple-element.40, bf16[2048,384]{0,1:T(8,128)(2,1)S(1)} %get-tuple-element.38), kind=kLoop, calls=%fused_computation.44 | loop fusion | flops 6291456 | bytes 9437184 | tf_op jit(solution)/shard_map/transpose | solution.py:260
  47.4 4.7 %copy.21.gate_up = bf16[2048,768]{1,0:T(8,128)(2,1)} copy(bf16[2048,768]{0,1:T(8,128)(2,1)} %get-tuple-element.42) | data formatting | bytes 6291456 | tf_op jit(solution)/shard_map/concatenate | solution.py:259
  52.1 3.8 %select_bitcast_fusion = (bf16[2048,384]{1,0:T(8,128)(2,1)}, bf16[2048,384]{1,0:T(8,128)(2,1)}) fusion(bf16[384,2048]{0,1:T(8,128)(2,1)} %collective-permute-done.5, pred[]{:T(512)S(6)} %eq.8, bf16[1,1,384,2048]{2,3,1,0:T(8,128)(2,1)} %copy.20, pred[]{:T(512)S(6)} %eq.7), kind=kLoop, calls=%fused_computation.7 | loop fusion | flops 1572864 | bytes 6291458 | tf_op jit(solution)/shard_map/transpose | solution.py:260
  55.9 44.6 %all-to-all-done.x.dy = bf16[128,6,16,128]{3,2,1,0:T(8,128)(2,1)S(1)} async-done(((bf16[128,6,16,128]{3,2,1,0:T(8,128)(2,1)}), bf16[128,6,16,128]{3,2,1,0:T(8,128)(2,1)S(1)}, u32[]{:S(2)}, u32[]{:S(2)}) %all-to-all-start) | async-done | bytes 3145760 | tf_op jit(solution)/shard_map/all_to_all | solution.py:207
  100.5 1.7 copy-done.2
  103.6 7.6 %shard_map.104 = (bf16[128,2,16,128]{3,2,1,0:T(8,128)(2,1)S(1)}, bf16[256,2048]{1,0:T(8,128)(2,1)S(1)}, bf16[256,384]{1,0:T(8,128)(2,1)S(1)}) custom-call(bf16[128,6,16,128]{3,2,1,0:T(8,128)(2,1)} %copy-done.2, bf16[128,6,16,128]{3,2,1,0:T(8,128)(2,1)} %copy-done.2, bf16[2048,768]{1,0:T(8,128)(2,1)} %copy.21.gate_up, bf16[2048,384]{1,0:T(8,128)(2,1)S(1)} %copy-done.4, ...), custom_call_target="tpu_custom_call" | custom-call | flops 2013265920 | bytes 9000000 | tf_op jit(solution)/shard_map/pallas_call | solution.py:190
  112.1 37.9 %all_to_all.20.back = bf16[128,2,16,128]{3,2,1,0:T(8,128)(2,1)S(1)} all-to-all(bf16[128,2,16,128]{3,2,1,0:T(8,128)(2,1)S(1)} %get-tuple-element.20), channel_id=1, replica_groups=mesh['segment'=2,'expert'=128] {'expert'}, dimensions={0} | all-to-all | bytes 2097152 | tf_op jit(solution)/shard_map/all_to_all | solution.py:207
  150.1 4.0 %shard_map.105 = (bf16[128,2,16,128]{3,2,1,0:T(8,128)(2,1)}, bf16[64,16,128]{2,1,0:T(8,128)(2,1)S(1)}) custom-call(s32[1]{0:T(128)} %bitcast.here, s32[2,128]{1,0:T(2,128)S(1)} %get-tuple-element.18.slots, f32[128]{0:T(128)S(1)} %get-tuple-element.52.own_w, f32[128]{0:T(128)S(1)} %collective-permute-done.1.other_w, ...), custom_call_target="tpu_custom_call" | custom-call | flops 1000000 | bytes 3000000 | tf_op jit(solution)/shard_map/pallas_call | solution.py:190
  154.7 9.2 %all-to-all-start.2 = ((bf16[128,2,16,128]{3,2,1,0:T(8,128)(2,1)}), bf16[128,2,16,128]{3,2,1,0:T(8,128)(2,1)}, u32[]{:S(2)}, u32[]{:S(2)}) async-start(bf16[128,2,16,128]{3,2,1,0:T(8,128)(2,1)} %get-tuple-element.22), calls=%async_computation.2 | async-start | bytes 2097152 | tf_op jit(solution)/shard_map/all_to_all | solution.py:207
  163.9 3.4 %fusion.13 = (bf16[768,2048]{1,0:T(8,128)(2,1)}, bf16[2048,768]{0,1:T(8,128)(2,1)}) fusion(bf16[2048,384]{0,1:T(8,128)(2,1)S(1)} %copy-done.19, bf16[2048,384]{0,1:T(8,128)(2,1)S(1)} %copy-done.18), kind=kLoop, calls=%fused_computation.43 | loop fusion | flops 6291456 | bytes 9437184 | tf_op jit(solution)/shard_map/transpose | solution.py:260
  167.3 4.8 %copy.22.gate_up = bf16[2048,768]{1,0:T(8,128)(2,1)} copy(bf16[2048,768]{0,1:T(8,128)(2,1)} %get-tuple-element.34) | data formatting | bytes 6291456 | tf_op jit(solution)/shard_map/concatenate | solution.py:259
  172.1 3.7 %shard_map.106 = (f32[256,384]{1,0:T(8,128)S(1)}, f32[256,384]{1,0:T(8,128)S(1)}, bf16[256,384]{1,0:T(8,128)(2,1)S(1)}) custom-call(bf16[128,6,16,128]{3,2,1,0:T(8,128)(2,1)S(1)} %copy-done.3, bf16[2048,768]{1,0:T(8,128)(2,1)} %copy.22.gate_up), custom_call_target="tpu_custom_call" | custom-call | flops 805306368 | bytes 5000000 | tf_op jit(solution)/shard_map/pallas_call | solution.py:190
  177.2 13.1 %all-to-all-done.2.dy = bf16[128,2,16,128]{3,2,1,0:T(8,128)(2,1)} async-done(((bf16[128,2,16,128]{3,2,1,0:T(8,128)(2,1)}), bf16[128,2,16,128]{3,2,1,0:T(8,128)(2,1)}, u32[]{:S(2)}, u32[]{:S(2)}) %all-to-all-start.2) | async-done | bytes 1048608 | tf_op jit(solution)/shard_map/all_to_all | solution.py:207
  192.7 4.7 %shard_map.107 = (bf16[128,2,16,128]{3,2,1,0:T(8,128)(2,1)S(1)}, bf16[256,2048]{1,0:T(8,128)(2,1)S(1)}) custom-call(bf16[128,2,16,128]{3,2,1,0:T(8,128)(2,1)} %all-to-all-done.2.dy, f32[256,384]{1,0:T(8,128)S(1)} %get-tuple-element.23.act, f32[256,384]{1,0:T(8,128)S(1)} %copy-done.11, bf16[2048,384]{1,0:T(8,128)(2,1)S(1)} %copy-done.5, ...), custom_call_target="tpu_custom_call" | custom-call | flops 1207959552 | bytes 8000000 | tf_op jit(solution)/shard_map/pallas_call | solution.py:190
  198.4 8.9 %all-to-all-start.3 = ((bf16[128,2,16,128]{3,2,1,0:T(8,128)(2,1)}), bf16[128,2,16,128]{3,2,1,0:T(8,128)(2,1)S(1)}, u32[]{:S(2)}, u32[]{:S(2)}) async-start(bf16[128,2,16,128]{3,2,1,0:T(8,128)(2,1)} %copy-done.9), calls=%async_computation.3 | async-start | bytes 2097152 | tf_op jit(solution)/shard_map/all_to_all | solution.py:207
  207.4 1.5 broadcast_select_fusion.5
  208.9 2.6 %collective-permute-start.9 = (bf16[256,2048]{1,0:T(8,128)(2,1)}, bf16[256,2048]{1,0:T(8,128)(2,1)}, u32[]{:S(2)}, u32[]{:S(2)}) collective-permute-start(bf16[256,2048]{1,0:T(8,128)(2,1)} %get-tuple-element.44), channel_id=1, source_target_pairs={{0,128},{128,0},{1,129},{129,1},{2,130},{130,2},{3,131},{131,3},{4... | collective-permute-start | bytes 3145736 | tf_op jit(solution)/shard_map/ppermute | solution.py:203
  211.6 2.5 collective-permute-done.7
  215.7 18.5 %all-to-all-done.3.back = bf16[128,2,16,128]{3,2,1,0:T(8,128)(2,1)S(1)} async-done(((bf16[128,2,16,128]{3,2,1,0:T(8,128)(2,1)}), bf16[128,2,16,128]{3,2,1,0:T(8,128)(2,1)S(1)}, u32[]{:S(2)}, u32[]{:S(2)}) %all-to-all-start.3) | async-done | bytes 1048608 | tf_op jit(solution)/shard_map/all_to_all | solution.py:207
  234.2 2.3 shard_map.108
  236.5 5.4 %collective-permute-start.6 = (bf16[64,2048]{1,0:T(8,128)(2,1)S(1)}, bf16[64,2048]{1,0:T(8,128)(2,1)S(1)}, u32[]{:S(2)}, u32[]{:S(2)}) collective-permute-start(bf16[64,2048]{1,0:T(8,128)(2,1)S(1)} %get-tuple-element.27), channel_id=1, source_target_pairs={{0,128},{128,0},{1,129},{129,1},{2,130},{130,2},{3,131},{131,3},{4... | collective-permute-start | bytes 786440 | tf_op jit(solution)/shard_map/ppermute | solution.py:203
  241.9 3.5 %fusion = bf16[1,1,384,2048]{3,2,1,0:T(8,128)(2,1)} fusion(bf16[256,2048]{1,0:T(8,128)(2,1)} %collective-permute-done.9, bf16[256,2048]{1,0:T(8,128)(2,1)S(1)} %copy-done.21, bf16[256,384]{1,0:T(8,128)(2,1)S(1)} %collective-permute-done.8, bf16[256,384]{1,0:T(8,128)(2,1)} %get-tuple-element.49), kind=kOutput, calls=%fused_computation.5 | convolution fusion | flops 811859968 | bytes 4063232 | tf_op jit(solution)/shard_map/dot_general | solution.py:333
  245.5 4.0 %multiply_bitcast_fusion = f32[1,1,384,2048]{3,2,1,0:T(8,128)} fusion(bf16[256,2048]{1,0:T(8,128)(2,1)} %collective-permute-done.9, bf16[256,2048]{1,0:T(8,128)(2,1)S(1)} %copy-done.21, bf16[256,384]{1,0:T(8,128)(2,1)S(1)} %collective-permute-done.8, bf16[256,384]{1,0:T(8,128)(2,1)S(1)} %copy-done.23), kind=kOutput, calls=%fused_computation.3 | convolution fusion | flops 813563904 | bytes 5636096 | tf_op jit(solution)/shard_map/dot_general | solution.py:334
  (74 shorter events, 16.1 us)
Async XLA Ops:
  0.6 7.1 %copy-start = (bf16[2,64,2048]{2,1,0:T(8,128)(2,1)S(1)}, bf16[2,64,2048]{2,1,0:T(8,128)(2,1)}, u32[]{:S(2)}) copy-start(bf16[2,64,2048]{2,1,0:T(8,128)(2,1)} %param.9) | copy-start | bytes 1572868
  1.7 6.1 %collective-permute-start.1 = (f32[128]{0:T(128)S(1)}, f32[128]{0:T(128)S(1)}, u32[]{:S(2)}, u32[]{:S(2)}) collective-permute-start(f32[128]{0:T(128)S(1)} %get-tuple-element.51), channel_id=1, source_target_pairs={{0,128},{128,0},{1,129},{129,1},{2,130},{130,2},{3,131},{131,3},{4... | collective-permute-start | bytes 1544 | tf_op jit(solution)/shard_map/ppermute | solution.py:203
  6.0 2.5 collective-permute-start.2
  7.1 1.4 collective-permute-start
  13.4 1.7 copy-start.6
  15.1 85.4 %all-to-all-start = ((bf16[128,6,16,128]{3,2,1,0:T(8,128)(2,1)}), bf16[128,6,16,128]{3,2,1,0:T(8,128)(2,1)S(1)}, u32[]{:S(2)}, u32[]{:S(2)}) async-start(bf16[128,6,16,128]{3,2,1,0:T(8,128)(2,1)} %copy-done.6), calls=%async_computation | async-start | bytes 6291456 | tf_op jit(solution)/shard_map/all_to_all | solution.py:207
  31.5 6.3 %collective-permute-start.3 = (bf16[2048,384]{0,1:T(8,128)(2,1)}, bf16[2048,384]{0,1:T(8,128)(2,1)}, u32[]{:S(2)}, u32[]{:S(2)}) collective-permute-start(bf16[2048,384]{0,1:T(8,128)(2,1)} %bitcast.61), channel_id=1, source_target_pairs={{0,128},{128,0},{1,129},{129,1},{2,130},{130,2},{3,131},{131,3},{4... | collective-permute-start | bytes 4718600 | tf_op jit(solution)/shard_map/ppermute | solution.py:203
  34.7 6.5 %collective-permute-start.4 = (bf16[2048,384]{0,1:T(8,128)(2,1)}, bf16[2048,384]{0,1:T(8,128)(2,1)}, u32[]{:S(2)}, u32[]{:S(2)}) collective-permute-start(bf16[2048,384]{0,1:T(8,128)(2,1)} %bitcast.60), channel_id=1, source_target_pairs={{0,128},{128,0},{1,129},{129,1},{2,130},{130,2},{3,131},{131,3},{4... | collective-permute-start | bytes 4718600 | tf_op jit(solution)/shard_map/ppermute | solution.py:203
  37.3 14.8 %collective-permute-start.5 = (bf16[384,2048]{0,1:T(8,128)(2,1)}, bf16[384,2048]{0,1:T(8,128)(2,1)}, u32[]{:S(2)}, u32[]{:S(2)}) collective-permute-start(bf16[384,2048]{0,1:T(8,128)(2,1)} %bitcast.59), channel_id=1, source_target_pairs={{0,128},{128,0},{1,129},{129,1},{2,130},{130,2},{3,131},{131,3},{4... | collective-permute-start | bytes 4718600 | tf_op jit(solution)/shard_map/ppermute | solution.py:203
  37.8 3.4 %copy-start.20 = (bf16[1,1,2048,384]{2,3,1,0:T(8,128)(2,1)S(1)}, bf16[1,1,2048,384]{2,3,1,0:T(8,128)(2,1)}, u32[]{:S(2)}) copy-start(bf16[1,1,2048,384]{2,3,1,0:T(8,128)(2,1)} %copy.19) | copy-start | bytes 4718596
  100.5 1.7 copy-start.2
  102.1 1.4 copy-start.4
  111.1 1.0 copy-start.7
  112.1 41.9 %copy-start.16 = (bf16[256,384]{1,0:T(8,128)(2,1)}, bf16[256,384]{1,0:T(8,128)(2,1)S(1)}, u32[]{:S(2)}) copy-start(bf16[256,384]{1,0:T(8,128)(2,1)S(1)} %get-tuple-element.29) | copy-start | bytes 589828
  150.1 13.9 %copy-start.18 = (bf16[2048,384]{0,1:T(8,128)(2,1)S(1)}, bf16[2048,384]{0,1:T(8,128)(2,1)}, u32[]{:S(2)}) copy-start(bf16[2048,384]{0,1:T(8,128)(2,1)} %get-tuple-element.37) | copy-start | bytes 4718596
  150.1 13.9 %copy-start.19 = (bf16[2048,384]{0,1:T(8,128)(2,1)S(1)}, bf16[2048,384]{0,1:T(8,128)(2,1)}, u32[]{:S(2)}) copy-start(bf16[2048,384]{0,1:T(8,128)(2,1)} %get-tuple-element.39) | copy-start | bytes 4718596
  154.7 35.6 %all-to-all-start.2 = ((bf16[128,2,16,128]{3,2,1,0:T(8,128)(2,1)}), bf16[128,2,16,128]{3,2,1,0:T(8,128)(2,1)}, u32[]{:S(2)}, u32[]{:S(2)}) async-start(bf16[128,2,16,128]{3,2,1,0:T(8,128)(2,1)} %get-tuple-element.22), calls=%async_computation.2 | async-start | bytes 2097152 | tf_op jit(solution)/shard_map/all_to_all | solution.py:207
  167.3 4.8 %copy-start.3 = (bf16[128,6,16,128]{3,2,1,0:T(8,128)(2,1)S(1)}, bf16[128,6,16,128]{3,2,1,0:T(8,128)(2,1)}, u32[]{:S(2)}) copy-start(bf16[128,6,16,128]{3,2,1,0:T(8,128)(2,1)} %copy-done.2) | copy-start | bytes 9437188
  190.3 1.4 copy-start.5
  198.4 8.9 %copy-start.8 = (bf16[256,2048]{1,0:T(8,128)(2,1)S(1)}, bf16[256,2048]{1,0:T(8,128)(2,1)}, u32[]{:S(2)}) copy-start(bf16[256,2048]{1,0:T(8,128)(2,1)} %copy-done.7) | copy-start | bytes 3145732
  198.4 35.8 %all-to-all-start.3 = ((bf16[128,2,16,128]{3,2,1,0:T(8,128)(2,1)}), bf16[128,2,16,128]{3,2,1,0:T(8,128)(2,1)S(1)}, u32[]{:S(2)}, u32[]{:S(2)}) async-start(bf16[128,2,16,128]{3,2,1,0:T(8,128)(2,1)} %copy-done.9), calls=%async_computation.3 | async-start | bytes 2097152 | tf_op jit(solution)/shard_map/all_to_all | solution.py:207
  207.3 4.2 %copy-start.22 = (bf16[1,1,384,384]{3,2,1,0:T(8,128)(2,1)S(1)}, bf16[1,1,384,384]{3,2,1,0:T(8,128)(2,1)}, u32[]{:S(2)}) copy-start(bf16[1,1,384,384]{3,2,1,0:T(8,128)(2,1)} %param.15) | copy-start | bytes 884740
  207.3 6.7 %copy-start.15 = (bf16[256,384]{1,0:T(8,128)(2,1)S(1)}, bf16[256,384]{1,0:T(8,128)(2,1)}, u32[]{:S(2)}) copy-start(bf16[256,384]{1,0:T(8,128)(2,1)} %copy-done.14) | copy-start | bytes 589828
  207.3 7.0 %copy-start.17 = (bf16[256,384]{1,0:T(8,128)(2,1)S(1)}, bf16[256,384]{1,0:T(8,128)(2,1)}, u32[]{:S(2)}) copy-start(bf16[256,384]{1,0:T(8,128)(2,1)} %copy-done.16) | copy-start | bytes 589828
  208.8 25.3 %copy-start.13 = (bf16[64,16,128]{2,1,0:T(8,128)(2,1)S(1)}, bf16[64,16,128]{2,1,0:T(8,128)(2,1)}, u32[]{:S(2)}) copy-start(bf16[64,16,128]{2,1,0:T(8,128)(2,1)} %copy-done.12) | copy-start | bytes 786436
  208.8 33.1 %copy-start.21 = (bf16[256,2048]{1,0:T(8,128)(2,1)S(1)}, bf16[256,2048]{1,0:T(8,128)(2,1)}, u32[]{:S(2)}) copy-start(bf16[256,2048]{1,0:T(8,128)(2,1)} %get-tuple-element.43) | copy-start | bytes 3145732
  208.9 33.1 %collective-permute-start.9 = (bf16[256,2048]{1,0:T(8,128)(2,1)}, bf16[256,2048]{1,0:T(8,128)(2,1)}, u32[]{:S(2)}, u32[]{:S(2)}) collective-permute-start(bf16[256,2048]{1,0:T(8,128)(2,1)} %get-tuple-element.44), channel_id=1, source_target_pairs={{0,128},{128,0},{1,129},{129,1},{2,130},{130,2},{3,131},{131,3},{4... | collective-permute-start | bytes 3145736 | tf_op jit(solution)/shard_map/ppermute | solution.py:203
  211.5 2.6 %collective-permute-start.7 = (bf16[384,384]{1,0:T(8,128)(2,1)S(1)}, bf16[384,384]{1,0:T(8,128)(2,1)S(1)}, u32[]{:S(2)}, u32[]{:S(2)}) collective-permute-start(bf16[384,384]{1,0:T(8,128)(2,1)S(1)} %bitcast.62), channel_id=1, source_target_pairs={{0,128},{128,0},{1,129},{129,1},{2,130},{130,2},{3,131},{131,3},{4... | collective-permute-start | bytes 884744 | tf_op jit(solution)/shard_map/ppermute | solution.py:203
  215.3 26.6 %collective-permute-start.8 = (bf16[256,384]{1,0:T(8,128)(2,1)S(1)}, bf16[256,384]{1,0:T(8,128)(2,1)S(1)}, u32[]{:S(2)}, u32[]{:S(2)}) collective-permute-start(bf16[256,384]{1,0:T(8,128)(2,1)S(1)} %get-tuple-element.50), channel_id=1, source_target_pairs={{0,128},{128,0},{1,129},{129,1},{2,130},{130,2},{3,131},{131,3},{4... | collective-permute-start | bytes 589832 | tf_op jit(solution)/shard_map/ppermute | solution.py:203
  236.5 13.0 %collective-permute-start.6 = (bf16[64,2048]{1,0:T(8,128)(2,1)S(1)}, bf16[64,2048]{1,0:T(8,128)(2,1)S(1)}, u32[]{:S(2)}, u32[]{:S(2)}) collective-permute-start(bf16[64,2048]{1,0:T(8,128)(2,1)S(1)} %get-tuple-element.27), channel_id=1, source_target_pairs={{0,128},{128,0},{1,129},{129,1},{2,130},{130,2},{3,131},{131,3},{4... | collective-permute-start | bytes 786440 | tf_op jit(solution)/shard_map/ppermute | solution.py:203
  241.9 3.5 %copy-start.23 = (bf16[256,384]{1,0:T(8,128)(2,1)S(1)}, bf16[256,384]{1,0:T(8,128)(2,1)}, u32[]{:S(2)}) copy-start(bf16[256,384]{1,0:T(8,128)(2,1)} %get-tuple-element.49) | copy-start | bytes 589828
  245.5 4.9 %copy-start.1 = (bf16[2,64,2048]{2,1,0:T(8,128)(2,1)S(1)}, bf16[2,64,2048]{2,1,0:T(8,128)(2,1)}, u32[]{:S(2)}) copy-start(bf16[2,64,2048]{2,1,0:T(8,128)(2,1)} %param.9) | copy-start | bytes 1572868
  (5 other events, 4.1 us)
where the time goes:
time: 251 us; the launch traced here: 250 us
  waiting for transfers between devices  79.4 us (32%)
  starting transfers between devices  45.5 us (18%)
  blocking collectives  37.9 us (15%)
  local copies, waits for them, and re-layouts  31.6 us (13%)
  Pallas kernels  27.2 us (11%)
  other arithmetic  19.1 us (8%)
  matrix products  8.74 us (3%)
    all_to_all x3, waiting for transfers between devices, exchanged(): lax.all_to_all(block, 'expert', split_axis=0, concat_axis=0, tiled=True)  76.1 us
    all_to_all x1, blocking collectives, exchanged(): lax.all_to_all(block, 'expert', split_axis=0, concat_axis=0, tiled=True)  37.9 us
    all_to_all x3, starting transfers between devices, exchanged(): lax.all_to_all(block, 'expert', split_axis=0, concat_axis=0, tiled=True)  31.9 us
    pallas_call x6, Pallas kernels, call(): pl.pallas_call(kernel, grid=(1,), in_specs=in_specs, out_shape=out_shape,...  27.2 us
    unnamed x53, local copies, waits for them, and re-layouts  20.7 us
    ppermute x10, starting transfers between devices, swapped(): return lax.ppermute(block, 'segment', [(0, 1), (1, 0)])  13.7 us
    transpose x3, other arithmetic, of_layer(): return (gate_up, down.T, gate_up.T, basis)  10.6 us
    concatenate x2, local copies, waits for them, and re-layouts, of_layer(): gate_up = jnp.concatenate([gate, up], axis=1)  9.45 us
  transfers between devices with their start and end apart: 13, of which 5 were waited for; matrix products, arithmetic and copies ran while one was open for 18% of the time, Pallas kernels for 2%

commit v1 on v0

v1 whole, which is shorter than its diff:
```python
import functools
import jax
import jax.numpy as jnp
from jax import lax
from jax.experimental import pallas as pl
from jax.experimental.pallas import tpu as pltpu
from jax.sharding import PartitionSpec as P

LANES = 128
CAP = 2
F32 = jnp.float32
BF16 = jnp.bfloat16
SMEM = pl.BlockSpec(memory_space=pltpu.SMEM)
VMEM = pl.BlockSpec(memory_space=pltpu.VMEM)
HBM = pl.BlockSpec(memory_space=pltpu.HBM)


def rows_to_tiles(rows, tiles, count, depth):
    for j in range(depth):
        tiles[pl.ds(j, count, stride=depth), :] = rows[:, j * LANES : (j + 1) * LANES]


def tiles_to_rows(tiles, rows, count, depth):
    for j in range(depth):
        rows[:, j * LANES : (j + 1) * LANES] = tiles[pl.ds(j, count, stride=depth), :].astype(
            rows.dtype
        )


def clear(send, experts):
    zero = jnp.zeros(send.shape[1:], send.dtype)

    def one(e, carry):
        send[e] = zero
        return carry

    lax.fori_loop(0, experts, one, 0, unroll=8)


def on_core(which):
    return lax.axis_index("segment") == which


def fetch(source, target, sem):
    copy = pltpu.make_async_copy(source, target, sem)
    copy.start()
    return copy


def fetch_one_of(first, own, other, target, sem):
    @pl.when(first)
    def _():
        pltpu.make_async_copy(own, target, sem).start()

    @pl.when(jnp.logical_not(first))
    def _():
        pltpu.make_async_copy(other, target, sem).start()

    return pltpu.make_async_copy(own, target, sem)


def dispatch_kernel(
    own_ids, other_ids, own_w, other_w, own_x, other_x, grad, after, sent, slots, grad_tiles,
    send, x_upper, x_lower, g_tiles, counts, sems,
):
    tokens, width = grad.shape
    depth = width // LANES
    experts = send.shape[0]
    upper = on_core(1)
    own = own_x[...].astype(F32)
    other = other_x[...].astype(F32)
    rows_to_tiles(jnp.where(upper, own, other), x_upper, tokens, depth)
    rows_to_tiles(jnp.where(upper, other, own), x_lower, tokens, depth)
    rows_to_tiles(grad[...].astype(F32), g_tiles, tokens, depth)
    clear(send, experts)

    def reset(e, carry):
        counts[0, e] = 0
        counts[1, e] = 0
        return carry

    lax.fori_loop(0, experts, reset, 0, unroll=8)

    def first(t, carry):
        at = pl.ds(pl.multiple_of(t * depth, depth), depth)
        row = x_upper[at, :].astype(BF16)
        g = g_tiles[at, :]
        grad_tiles[t] = g.astype(BF16)
        for k in range(2):
            p = 2 * t + k
            e = jnp.where(upper, own_ids[p], other_ids[p])
            c = jnp.minimum(counts[0, e], CAP - 1)
            counts[0, e] = c + 1
            slots[1, p] = e * CAP + c
            weight = jnp.where(upper, own_w[p], other_w[p])
            send[e, c] = row
            send[e, CAP + c] = (weight * g).astype(BF16)
        return carry

    lax.fori_loop(0, tokens, first, 0, unroll=2)
    urgent = fetch(send.at[:, : 2 * CAP], sent.at[:, : 2 * CAP], sems.at[0])

    def second(t, carry):
        at = pl.ds(pl.multiple_of(t * depth, depth), depth)
        row = x_lower[at, :].astype(BF16)
        for k in range(2):
            p = 2 * t + k
            e = jnp.where(upper, other_ids[p], own_ids[p])
            c = jnp.minimum(counts[1, e], CAP - 1)
            counts[1, e] = c + 1
            slots[0, p] = e * CAP + c
            send[e, 2 * CAP + c] = row
        return carry

    lax.fori_loop(0, tokens, second, 0, unroll=2)
    rest = fetch(send.at[:, 2 * CAP :], sent.at[:, 2 * CAP :], sems.at[1])
    urgent.wait()
    rest.wait()


def relay_kernel(slots, own_w, other_w, back, upstream, sent, grad_out, send, sems):
    tokens = upstream.shape[0]
    upper = on_core(1)
    clear(send, send.shape[0])

    def token(t, carry):
        total = upstream[t].astype(F32)
        for k in range(2):
            total = total + back[slots[1, 2 * t + k]].astype(F32)
        rounded = total.astype(BF16)
        grad_out[t] = rounded
        g = rounded.astype(F32)
        for k in range(2):
            p = 2 * t + k
            weight = jnp.where(upper, other_w[p], own_w[p])
            send[slots[0, p]] = (weight * g).astype(BF16)
        return carry

    lax.fori_loop(0, tokens, token, 0, unroll=4)
    fetch(send, sent, sems.at[0]).wait()


def finish_kernel(slots, back, upstream, keep, away, low, up):
    tokens, depth = upstream.shape[0], upstream.shape[1]
    upper = on_core(1)

    def token(t, carry):
        at = pl.ds(pl.multiple_of(t * depth, depth), depth)
        g = upstream[t].astype(F32)
        up[at, :] = g
        total = g
        for k in range(2):
            total = total + back[slots[0, 2 * t + k]].astype(F32)
        low[at, :] = total
        return carry

    lax.fori_loop(0, tokens, token, 0, unroll=4)
    for j in range(depth):
        columns = slice(j * LANES, (j + 1) * LANES)
        high = up[pl.ds(j, tokens, stride=depth), :]
        down = low[pl.ds(j, tokens, stride=depth), :]
        keep[:, columns] = jnp.where(upper, high, down).astype(BF16)
        away[:, columns] = jnp.where(upper, down, high).astype(BF16)


def turn_kernel(turn, gate, up, down, *refs):
    gate_up_t, down_t, a, b, c, turned, turned_down, sems = refs[-8:]
    hidden, width = down.shape
    step = 256

    def work():
        copies = [
            fetch(gate, a, sems.at[0]), fetch(up, b, sems.at[1]), fetch(down, c, sems.at[2])
        ]
        for n, block in enumerate((a, b)):
            copies[n].wait()
            for i in range(0, width, step):
                turned[n * hidden : (n + 1) * hidden, i : i + step] = block[i : i + step, :].T
        first = fetch(turned, gate_up_t, sems.at[3])
        copies[2].wait()
        for i in range(0, width, step):
            turned_down[i : i + step, :] = c[:, i : i + step].T
        fetch(turned_down, down_t, sems.at[4]).wait()
        first.wait()

    if turn is None:
        work()
    else:
        pl.when(on_core(turn))(work)


def untile(block, tiles, rows, depth):
    count, lanes = rows.shape[0], LANES
    tiles[...] = block[...].astype(F32).reshape(count * depth, lanes)
    tiles_to_rows(tiles, rows, count, depth)


def forward_parts(rows, gate, up):
    hidden_gate = jnp.dot(rows[...], gate[...], preferred_element_type=F32)
    hidden_up = jnp.dot(rows[...], up[...], preferred_element_type=F32)
    sigma = 1.0 / (1.0 + jnp.exp(-hidden_gate))
    act = hidden_gate * sigma
    dact = sigma * (1.0 + hidden_gate * (1.0 - sigma))
    return act, hidden_up * dact, (act * hidden_up).astype(BF16)


def backward_parts(act, slope, dy_rows, down_t, matrices, gate_up_t, tiles, send, sent, sem):
    count, depth, lanes = send.shape
    grad_act = jnp.dot(dy_rows[...], down_t[...], preferred_element_type=F32)
    both = jnp.concatenate(
        [(grad_act * slope).astype(BF16), (grad_act * act).astype(BF16)], axis=1
    )
    matrices.wait()
    dx = jnp.dot(both, gate_up_t[...], preferred_element_type=F32)
    rows_to_tiles(dx, tiles, count, depth)
    pieces, copies = 4, []
    part = count // pieces
    for n in range(pieces):
        rows = tiles[n * part * depth : (n + 1) * part * depth, :]
        send[n * part : (n + 1) * part] = rows.reshape(part, depth, lanes).astype(BF16)
        here = pl.ds(n * part, part)
        copies.append(fetch(send.at[here], sent.at[here], sem.at[n]))
    return copies


def upper_kernel(
    arrived, own_gate, other_gate, own_up, other_up, own_dt, other_dt, own_gut, other_gut,
    sent, dy_out, act_out,
    x, dy, gate, up, down_t, gate_up_t, tiles, x_rows, dy_rows, activ, send, sems,
):
    mine = on_core(1)
    depth = send.shape[1]
    x_copy = fetch(arrived.at[:, :CAP], x, sems.at[0])
    gate_copy = fetch_one_of(mine, own_gate, other_gate, gate, sems.at[1])
    up_copy = fetch_one_of(mine, own_up, other_up, up, sems.at[2])
    dy_copy = fetch(arrived.at[:, CAP : 2 * CAP], dy, sems.at[3])
    down_copy = fetch_one_of(mine, own_dt, other_dt, down_t, sems.at[4])
    back_copy = fetch_one_of(mine, own_gut, other_gut, gate_up_t, sems.at[5])
    x_copy.wait()
    untile(x, tiles, x_rows, depth)
    gate_copy.wait()
    up_copy.wait()
    act, slope, rounded = forward_parts(x_rows, gate, up)
    activ[...] = rounded
    dy_copy.wait()
    untile(dy, tiles, dy_rows, depth)
    saves = [fetch(activ, act_out, sems.at[6]), fetch(dy_rows, dy_out, sems.at[7])]
    down_copy.wait()
    saves += backward_parts(
        act, slope, dy_rows, down_t, back_copy, gate_up_t, tiles, send, sent, sems.at[pl.ds(8, 4)]
    )
    for copy in saves:
        copy.wait()


def forward_kernel(
    arrived, own_gate, other_gate, own_up, other_up, act_out, slope_out, activ_out,
    x, gate, up, tiles, x_rows, sems,
):
    mine = on_core(0)
    depth = arrived.shape[2]
    x_copy = fetch(arrived.at[:, 2 * CAP :], x, sems.at[0])
    gate_copy = fetch_one_of(mine, own_gate, other_gate, gate, sems.at[1])
    up_copy = fetch_one_of(mine, own_up, other_up, up, sems.at[2])
    x_copy.wait()
    untile(x, tiles, x_rows, depth)
    gate_copy.wait()
    up_copy.wait()
    act, slope, rounded = forward_parts(x_rows, gate, up)
    act_out[...] = act
    slope_out[...] = slope
    activ_out[...] = rounded


def lower_kernel(
    dy, act, slope, own_dt, other_dt, own_gut, other_gut, sent, dy_out,
    down_t, gate_up_t, tiles, dy_rows, send, sems,
):
    mine = on_core(0)
    down_copy = fetch_one_of(mine, own_dt, other_dt, down_t, sems.at[0])
    back_copy = fetch_one_of(mine, own_gut, other_gut, gate_up_t, sems.at[1])
    untile(dy, tiles, dy_rows, send.shape[1])
    save = fetch(dy_rows, dy_out, sems.at[2])
    down_copy.wait()
    saves = backward_parts(
        act[...], slope[...], dy_rows, down_t, back_copy, gate_up_t, tiles, send, sent,
        sems.at[pl.ds(3, 4)],
    )
    for copy in saves:
        copy.wait()
    save.wait()


def call(kernel, args, in_specs, out_shape, out_specs, scratch, flops, moved, aliases={}):
    return pl.pallas_call(
        kernel,
        in_specs=in_specs,
        out_shape=out_shape,
        out_specs=out_specs,
        scratch_shapes=scratch,
        input_output_aliases=aliases,
        compiler_params=pltpu.CompilerParams(vmem_limit_bytes=63 * 1024 * 1024),
        cost_estimate=pl.CostEstimate(flops=flops, bytes_accessed=moved, transcendentals=0),
    )(*args)


def swapped(block):
    return lax.ppermute(block, "segment", [(0, 1), (1, 0)])


def exchanged(block):
    return lax.all_to_all(block, "expert", split_axis=0, concat_axis=0, tiled=True)


def shape(dims, kind=BF16):
    return jax.ShapeDtypeStruct(dims, kind)


def shards(saved_input, out_grad, expert_ids, router_weights, w_gate, w_up, w_down, eigenbasis):
    experts = lax.axis_size("expert")
    segment = lax.axis_index("segment")
    upper = segment == 1
    micros, tokens, width = saved_input.shape[1:]
    hidden = w_gate.shape[-1]
    depth = width // LANES
    count = experts * CAP
    gate, up, down, basis = w_gate[0, 0], w_up[0, 0], w_down[0, 0], eigenbasis[0, 0]

    ids = expert_ids[0].reshape(micros, tokens * 2)
    weights = router_weights[0].reshape(micros, tokens * 2)
    mine = functools.partial(lax.dynamic_index_in_dim, index=segment, axis=0, keepdims=False)
    theirs = functools.partial(lax.dynamic_index_in_dim, index=1 - segment, axis=0, keepdims=False)
    own_x, other_x = mine(saved_input[0]), swapped(theirs(saved_input[0]))
    own_ids, other_ids = mine(ids), swapped(theirs(ids))
    own_w, other_w = mine(weights), swapped(theirs(weights))
    grad = mine(out_grad)

    matrix = pltpu.VMEM((width, hidden), BF16)
    turned_shapes = (shape((2 * hidden, width)), shape((width, hidden)))
    turn_scratch = [
        matrix, matrix, pltpu.VMEM((hidden, width), BF16), pltpu.VMEM((2 * hidden, width), BF16),
        matrix, pltpu.SemaphoreType.DMA((5,)),
    ]

    def turned(turn, matrices, made=()):
        return call(
            functools.partial(turn_kernel, turn),
            (*matrices, *made),
            [HBM] * (3 + len(made)),
            turned_shapes,
            (HBM,) * 2,
            turn_scratch,
            1_000_000,
            9_000_000,
            {3: 0, 4: 1} if made else {},
        )

    early_gut, early_dt = turned(0, (gate, up, down))

    tile_rows = tokens * depth
    send, slots, grad_tiles = call(
        dispatch_kernel,
        (own_ids, other_ids, own_w, other_w, own_x, other_x, grad, early_dt),
        [SMEM] * 4 + [VMEM] * 3 + [HBM],
        (
            shape((experts, 3 * CAP, depth, LANES)),
            shape((2, tokens * 2), jnp.int32),
            shape((tokens, depth, LANES)),
        ),
        (HBM, SMEM, VMEM),
        [pltpu.VMEM((experts, 3 * CAP, depth, LANES), BF16)]
        + [pltpu.VMEM((tile_rows, LANES), F32)] * 3
        + [pltpu.SMEM((2, experts), jnp.int32), pltpu.SemaphoreType.DMA((2,))],
        1_000_000,
        5_000_000,
    )
    arrived = exchanged(send)

    own_gut, own_dt = turned(1, (gate, up, down), (early_gut, early_dt))
    other_gate, other_up, other_down = swapped(gate), swapped(up), swapped(down)
    other_basis = swapped(basis)
    other_gut, other_dt = turned(None, (other_gate, other_up, other_down))

    tiles = pltpu.VMEM((count * depth, LANES), F32)
    rows = pltpu.VMEM((count, width), BF16)
    part = pltpu.VMEM((experts, CAP, depth, LANES), BF16)
    flat = (count, depth, LANES)
    flat_scratch = pltpu.VMEM(flat, BF16)
    mat = 2 * count * width * hidden
    back_send, dy_rows1, activ1 = call(
        upper_kernel,
        (arrived, gate, other_gate, up, other_up, own_dt, other_dt, own_gut, other_gut),
        [HBM] * 9,
        (shape(flat), shape((count, width)), shape((count, hidden))),
        (HBM,) * 3,
        [
            part, part, matrix, matrix, matrix, pltpu.VMEM((2 * hidden, width), BF16), tiles,
            rows, rows, pltpu.VMEM((count, hidden), BF16), flat_scratch,
            pltpu.SemaphoreType.DMA((12,)),
        ],
        5 * mat,
        9_000_000,
    )

    def returned(block):
        return exchanged(block.reshape(experts, CAP, depth, LANES)).reshape(flat)

    back = returned(back_send)
    act0, slope0, activ0 = call(
        forward_kernel,
        (arrived, gate, other_gate, up, other_up),
        [HBM] * 5,
        (shape((count, hidden), F32), shape((count, hidden), F32), shape((count, hidden))),
        (VMEM,) * 3,
        [part, matrix, matrix, tiles, rows, pltpu.SemaphoreType.DMA((3,))],
        2 * mat,
        5_000_000,
    )
    basis1 = jnp.where(upper, basis, other_basis)
    basis0 = jnp.where(upper, other_basis, basis)
    rotated1 = jnp.dot(activ1, basis1, preferred_element_type=F32).astype(BF16)
    rotated0 = jnp.dot(activ0, basis0, preferred_element_type=F32).astype(BF16)

    dy_send, grad1 = call(
        relay_kernel,
        (slots, own_w, other_w, back, grad_tiles),
        [SMEM] * 3 + [VMEM] * 2,
        (shape(flat), shape((tokens, depth, LANES))),
        (HBM, VMEM),
        [flat_scratch, pltpu.SemaphoreType.DMA((1,))],
        1_000_000,
        3_000_000,
    )
    dy = returned(dy_send)
    back_send0, dy_rows0 = call(
        lower_kernel,
        (dy, act0, slope0, own_dt, other_dt, own_gut, other_gut),
        [VMEM] * 3 + [HBM] * 4,
        (shape(flat), shape((count, width))),
        (HBM,) * 2,
        [
            matrix, pltpu.VMEM((2 * hidden, width), BF16), tiles, rows, flat_scratch,
            pltpu.SemaphoreType.DMA((7,)),
        ],
        3 * mat,
        8_000_000,
    )
    back0 = returned(back_send0)

    all_rotated = jnp.concatenate(
        [
            jnp.where(upper, rotated1, rotated0),
            swapped(jnp.where(upper, rotated0, rotated1)),
        ],
        axis=0,
    )
    all_dy = jnp.concatenate(
        [
            jnp.where(upper, dy_rows1, dy_rows0),
            swapped(jnp.where(upper, dy_rows0, dy_rows1)),
        ],
        axis=0,
    )
    rot_sq = (all_rotated.astype(F32) ** 2).astype(BF16)
    dy_sq = (all_dy.astype(F32) ** 2).astype(BF16)
    over_rows = (((0,), (0,)), ((), ()))
    grad_sum = lax.dot_general(all_rotated, all_dy, over_rows, preferred_element_type=F32)
    scale_sum = lax.dot_general(rot_sq, dy_sq, over_rows, preferred_element_type=F32)
    rotated_grad = (grad_sum * (1.0 / micros)).astype(BF16)
    ekfac_scales = scale_sum * (1.0 / micros)
    back0, rotated_grad, ekfac_scales = lax.optimization_barrier(
        (back0, rotated_grad, ekfac_scales)
    )

    keep, away = call(
        finish_kernel,
        (slots, back0, grad1),
        [SMEM] + [VMEM] * 2,
        (shape((tokens, width)), shape((tokens, width))),
        (VMEM,) * 2,
        [pltpu.VMEM((tile_rows, LANES), F32)] * 2,
        1_000_000,
        2_000_000,
    )
    came = swapped(away)
    grads = jnp.stack([jnp.where(upper, came, keep), jnp.where(upper, keep, came)])
    return (grads[None], rotated_grad[None, None], ekfac_scales[None, None])


def solution(mesh):
    in_specs = (
        P("segment", None, "expert", None),
        P(None, "expert", None),
        P("segment", None, "expert", None),
        P("segment", None, "expert", None),
        P("segment", "expert", None, None),
        P("segment", "expert", None, None),
        P("segment", "expert", None, None),
        P("segment", "expert", None, None),
    )
    out_specs = (
        P("segment", None, "expert", None),
        P("segment", "expert", None, None),
        P("segment", "expert", None, None),
    )
    return jax.shard_map(shards, mesh=mesh, in_specs=in_specs, out_specs=out_specs, check_vma=False)
```

time: 251 us -> 235 us (0.936)
  local copies, waits for them, and re-layouts: 31.6 us -> 6.16 us
  other arithmetic: 19.1 us -> 3.51 us
  Pallas kernels: 27.2 us -> 41.2 us
  starting transfers between devices: 45.5 us -> 56.8 us
  waiting for transfers between devices: 79.4 us -> 83.5 us
  matrix products: 8.74 us -> 5.42 us
    unnamed x53 -> x14, local copies, waits for them, and re-layouts: 20.7 us -> 2.2 us
    pallas_call x6 -> x9, Pallas kernels: 27.2 us -> 41.2 us  [call(): pl.pallas_call(kernel, in_specs=in_specs, out_shape=out_shape, out_specs=...]
    transpose x3 -> x0, other arithmetic: 10.6 us -> none  [of_layer(): return (gate_up, down.T, gate_up.T, basis)]
    ppermute x10, starting transfers between devices: 13.7 us -> 23.3 us  [swapped(): return lax.ppermute(block, 'segment', [(0, 1), (1, 0)])]
    concatenate x2 -> x0, local copies, waits for them, and re-layouts: 9.45 us -> none  [of_layer(): gate_up = jnp.concatenate([gate, up], axis=1)]
    select_n x2 -> x0, other arithmetic: 6.12 us -> none  [the longest x1 3.36 us: of_layer(): gate = jnp.where(here_now, w_gate[0, 0], other_gate)]
    ppermute x10, waiting for transfers between devices: 3.29 us -> 7.83 us  [swapped(): return lax.ppermute(block, 'segment', [(0, 1), (1, 0)])]
  transfers between devices with their start and end apart: 13 -> 13, of which waited for: 5 -> 8; matrix products, arithmetic and copies ran while one was open for 18% -> 5% of each run, Pallas kernels for 2% -> 6%
where the time goes in v1:
time: 235 us; the launch traced here: 234 us
  waiting for transfers between devices  83.5 us (36%)
  starting transfers between devices  56.8 us (24%)
  Pallas kernels  41.2 us (18%)
  blocking collectives  36.8 us (16%)
  local copies, waits for them, and re-layouts  6.16 us (3%)
  matrix products  5.42 us (2%)
  other arithmetic  3.51 us (1%)
    all_to_all x3, waiting for transfers between devices, exchanged(): lax.all_to_all(block, 'expert', split_axis=0, concat_axis=0, tiled=True)  75.7 us
    pallas_call x9, Pallas kernels, call(): pl.pallas_call(kernel, in_specs=in_specs, out_shape=out_shape, out_specs=...  41.2 us
    all_to_all x1, blocking collectives, exchanged(): lax.all_to_all(block, 'expert', split_axis=0, concat_axis=0, tiled=True)  36.8 us
    all_to_all x3, starting transfers between devices, exchanged(): lax.all_to_all(block, 'expert', split_axis=0, concat_axis=0, tiled=True)  33.6 us
    ppermute x10, starting transfers between devices, swapped(): return lax.ppermute(block, 'segment', [(0, 1), (1, 0)])  23.3 us
    ppermute x10, waiting for transfers between devices, swapped(): return lax.ppermute(block, 'segment', [(0, 1), (1, 0)])  7.83 us
  transfers between devices with their start and end apart: 13, of which 8 were waited for; matrix products, arithmetic and copies ran while one was open for 5% of the time, Pallas kernels for 6%

profile of v1, /device:TPU:1, one launch (start us, length us, event | category | flops | bytes accessed | tf_op | source)
XLA Modules:
  0.0 234.2 jit_solution(4970440005026209081)
XLA Ops:
  0.7 0.8 copy.14
  2.2 3.2 %collective-permute-start.1 = (f32[128]{0:T(128)S(1)}, f32[128]{0:T(128)S(1)}, u32[]{:S(2)}, u32[]{:S(2)}) collective-permute-start(f32[128]{0:T(128)S(1)} %get-tuple-element.59), channel_id=1, source_target_pairs={{0,128},{128,0},{1,129},{129,1},{2,130},{130,2},{3,131},{131,3},{4... | collective-permute-start | bytes 1544 | tf_op jit(solution)/shard_map/ppermute | solution.py:308
  5.5 1.8 dynamic-slice_bitcast_fusion.1
  7.2 0.8 copy.13
  9.3 0.7 dynamic-slice_bitcast_fusion.grad
  10.7 6.7 %shard_map.104 = (bf16[128,6,16,128]{3,2,1,0:T(8,128)(2,1)}, s32[2,128]{1,0:T(2,128)}, bf16[64,16,128]{2,1,0:T(8,128)(2,1)}) custom-call(s32[128]{0:T(128)} %get-tuple-element.62.own_ids, s32[128]{0:T(128)} %copy-done.4, f32[128]{0:T(128)} %get-tuple-element.60.own_w, f32[128]{0:T(128)} %copy-done.3, bf16[64,2048]{1,0:T(8,128)(2,1)} %get-tuple-element.56.own_x, ...), custom_call_target="tpu_custom_call" | custom-call | flops 1000000 | bytes 5000000 | tf_op jit(solution)/shard_map/pallas_call | solution.py:295
  17.4 14.3 %all-to-all-start = ((bf16[128,6,16,128]{3,2,1,0:T(8,128)(2,1)}), bf16[128,6,16,128]{3,2,1,0:T(8,128)(2,1)}, u32[]{:S(2)}, u32[]{:S(2)}) async-start(bf16[128,6,16,128]{3,2,1,0:T(8,128)(2,1)} %get-tuple-element.29), calls=%async_computation | async-start | bytes 6291456 | tf_op jit(solution)/shard_map/all_to_all | solution.py:312
  31.6 4.9 %collective-permute-start.3 = (bf16[2048,384]{1,0:T(8,128)(2,1)}, bf16[2048,384]{1,0:T(8,128)(2,1)}, u32[]{:S(2)}, u32[]{:S(2)}) collective-permute-start(bf16[2048,384]{1,0:T(8,128)(2,1)} %bitcast.7.gate.own_gate), channel_id=1, source_target_pairs={{0,128},{128,0},{1,129},{129,1},{2,130},{130,2},{3,131},{131,3},{4... | collective-permute-start | bytes 4718600 | tf_op jit(solution)/shard_map/ppermute | solution.py:308
  37.0 4.6 %shard_map.105 = (bf16[768,2048]{1,0:T(8,128)(2,1)}, bf16[2048,384]{1,0:T(8,128)(2,1)}) custom-call(bf16[2048,384]{1,0:T(8,128)(2,1)} %bitcast.7.gate.own_gate, bf16[2048,384]{1,0:T(8,128)(2,1)} %bitcast.8.up.own_up, bf16[384,2048]{1,0:T(8,128)(2,1)} %bitcast.9.down, ...), custom_call_target="tpu_custom_call", output_to_operand_aliasing={{0}: (3, {}), {1}: (4, {})} | custom-call | flops 1000000 | bytes 9000000 | tf_op jit(solution)/shard_map/pallas_call | solution.py:295
  42.2 2.2 collective-permute-done.5.down
  44.4 4.5 %shard_map.106 = (bf16[768,2048]{1,0:T(8,128)(2,1)}, bf16[2048,384]{1,0:T(8,128)(2,1)}) custom-call(bf16[2048,384]{1,0:T(8,128)(2,1)} %collective-permute-done.3.gate.other_gate, bf16[2048,384]{1,0:T(8,128)(2,1)} %collective-permute-done.4.up.other_up, bf16[384,2048]{1,0:T(8,128)(2,1)} %collective-permute-done.5.down), custom_call_target="tpu_custom_call" | custom-call | flops 1000000 | bytes 9000000 | tf_op jit(solution)/shard_map/pallas_call | solution.py:295
  49.0 49.2 %all-to-all-done.arrived = bf16[128,6,16,128]{3,2,1,0:T(8,128)(2,1)} async-done(((bf16[128,6,16,128]{3,2,1,0:T(8,128)(2,1)}), bf16[128,6,16,128]{3,2,1,0:T(8,128)(2,1)}, u32[]{:S(2)}, u32[]{:S(2)}) %all-to-all-start) | async-done | bytes 3145760 | tf_op jit(solution)/shard_map/all_to_all | solution.py:312
  98.2 7.8 %shard_map.107 = (bf16[256,16,128]{2,1,0:T(8,128)(2,1)}, bf16[256,2048]{1,0:T(8,128)(2,1)}, bf16[256,384]{1,0:T(8,128)(2,1)}) custom-call(bf16[128,6,16,128]{3,2,1,0:T(8,128)(2,1)} %all-to-all-done.arrived, bf16[2048,384]{1,0:T(8,128)(2,1)} %bitcast.7.gate.own_gate, bf16[2048,384]{1,0:T(8,128)(2,1)} %collective-permute-done.3.gate.other_gate, ...), custom_call_target="tpu_custom_call" | custom-call | flops 2013265920 | bytes 9000000 | tf_op jit(solution)/shard_map/pallas_call | solution.py:295
  106.0 36.8 %all_to_all.20 = bf16[128,2,16,128]{3,2,1,0:T(8,128)(2,1)} all-to-all(bf16[128,2,16,128]{3,2,1,0:T(8,128)(2,1)} %bitcast.51), channel_id=1, replica_groups=mesh['segment'=2,'expert'=128] {'expert'}, dimensions={0} | all-to-all | bytes 2097152 | tf_op jit(solution)/shard_map/all_to_all | solution.py:312
  142.7 3.9 %shard_map.108 = (bf16[256,16,128]{2,1,0:T(8,128)(2,1)}, bf16[64,16,128]{2,1,0:T(8,128)(2,1)}) custom-call(s32[2,128]{1,0:T(2,128)} %get-tuple-element.28.slots, f32[128]{0:T(128)} %get-tuple-element.60.own_w, f32[128]{0:T(128)} %copy-done.3, bf16[256,16,128]{2,1,0:T(8,128)(2,1)} %bitcast.48, bf16[64,16,128]{2,1,0:T(8,128)(2,1)} %get-tuple-element.36.upstream), custom_call_target="tpu_custom_call" | custom-call | flops 1000000 | bytes 3000000 | tf_op jit(solution)/shard_map/pallas_call | solution.py:295
  146.6 9.7 %all-to-all-start.2 = ((bf16[128,2,16,128]{3,2,1,0:T(8,128)(2,1)}), bf16[128,2,16,128]{3,2,1,0:T(8,128)(2,1)}, u32[]{:S(2)}, u32[]{:S(2)}) async-start(bf16[128,2,16,128]{3,2,1,0:T(8,128)(2,1)} %bitcast.50), calls=%async_computation.2 | async-start | bytes 2097152 | tf_op jit(solution)/shard_map/all_to_all | solution.py:312
  156.3 4.4 %shard_map.109 = (f32[256,384]{1,0:T(8,128)}, f32[256,384]{1,0:T(8,128)}, bf16[256,384]{1,0:T(8,128)(2,1)}) custom-call(bf16[128,6,16,128]{3,2,1,0:T(8,128)(2,1)} %all-to-all-done.arrived, bf16[2048,384]{1,0:T(8,128)(2,1)} %bitcast.7.gate.own_gate, bf16[2048,384]{1,0:T(8,128)(2,1)} %collective-permute-done.3.gate.other_gate, ...), custom_call_target="tpu_custom_call" | custom-call | flops 805306368 | bytes 5000000 | tf_op jit(solution)/shard_map/pallas_call | solution.py:295
  160.7 19.5 %all-to-all-done.2 = bf16[128,2,16,128]{3,2,1,0:T(8,128)(2,1)} async-done(((bf16[128,2,16,128]{3,2,1,0:T(8,128)(2,1)}), bf16[128,2,16,128]{3,2,1,0:T(8,128)(2,1)}, u32[]{:S(2)}, u32[]{:S(2)}) %all-to-all-start.2) | async-done | bytes 1048608 | tf_op jit(solution)/shard_map/all_to_all | solution.py:312
  180.2 6.6 %shard_map.110 = (bf16[256,16,128]{2,1,0:T(8,128)(2,1)}, bf16[256,2048]{1,0:T(8,128)(2,1)}) custom-call(bf16[256,16,128]{2,1,0:T(8,128)(2,1)} %bitcast.13.dy, f32[256,384]{1,0:T(8,128)} %get-tuple-element.38.act, f32[256,384]{1,0:T(8,128)} %get-tuple-element.39.slope, bf16[2048,384]{1,0:T(8,128)(2,1)} %get-tuple-element.31.own_dt, ...), custom_call_target="tpu_custom_call" | custom-call | flops 1207959552 | bytes 8000000 | tf_op jit(solution)/shard_map/pallas_call | solution.py:295
  186.8 9.7 %all-to-all-start.3 = ((bf16[128,2,16,128]{3,2,1,0:T(8,128)(2,1)}), bf16[128,2,16,128]{3,2,1,0:T(8,128)(2,1)}, u32[]{:S(2)}, u32[]{:S(2)}) async-start(bf16[128,2,16,128]{3,2,1,0:T(8,128)(2,1)} %bitcast.49), calls=%async_computation.3 | async-start | bytes 2097152 | tf_op jit(solution)/shard_map/all_to_all | solution.py:312
  196.5 1.7 broadcast_select_fusion.1
  198.2 5.6 %collective-permute-start.8 = (bf16[256,2048]{1,0:T(8,128)(2,1)S(1)}, bf16[256,2048]{1,0:T(8,128)(2,1)S(1)}, u32[]{:S(2)}, u32[]{:S(2)}) collective-permute-start(bf16[256,2048]{1,0:T(8,128)(2,1)S(1)} %get-tuple-element.52), channel_id=1, source_target_pairs={{0,128},{128,0},{1,129},{129,1},{2,130},{130,2},{3,131},{131,3},{4... | collective-permute-start | bytes 3145736 | tf_op jit(solution)/shard_map/ppermute | solution.py:308
  203.8 2.6 %collective-permute-done.6 = bf16[384,384]{1,0:T(8,128)(2,1)S(1)} collective-permute-done((bf16[384,384]{1,0:T(8,128)(2,1)S(1)}, bf16[384,384]{1,0:T(8,128)(2,1)S(1)}, u32[]{:S(2)}, u32[]{:S(2)}) %collective-permute-start.6) | collective-permute-done | bytes 294944 | tf_op jit(solution)/shard_map/ppermute | solution.py:308
  207.5 1.1 collective-permute-done.7
  208.6 2.2 multiply_convert_fusion.1
  210.7 2.7 %convolution_multiply_fusion = f32[384,2048]{1,0:T(8,128)} fusion(bf16[256,2048]{1,0:T(8,128)(2,1)S(1)} %collective-permute-done.8, bf16[256,2048]{1,0:T(8,128)(2,1)S(1)} %get-tuple-element.51, bf16[256,384]{1,0:T(8,128)(2,1)S(1)} %collective-permute-done.7, bf16[256,384]{1,0:T(8,128)(2,1)S(1)} %get-tuple-element.57), kind=kOutput, calls=%fused_computation.2 | convolution fusion | flops 813563904 | bytes 5636096 | tf_op jit(solution)/shard_map/dot_general | solution.py:468
  213.4 6.9 %all-to-all-done.3 = bf16[128,2,16,128]{3,2,1,0:T(8,128)(2,1)} async-done(((bf16[128,2,16,128]{3,2,1,0:T(8,128)(2,1)}), bf16[128,2,16,128]{3,2,1,0:T(8,128)(2,1)}, u32[]{:S(2)}, u32[]{:S(2)}) %all-to-all-start.3) | async-done | bytes 1048608 | tf_op jit(solution)/shard_map/all_to_all | solution.py:312
  220.3 2.7 %shard_map.111 = (bf16[64,2048]{1,0:T(8,128)(2,1)}, bf16[64,2048]{1,0:T(8,128)(2,1)}) custom-call(s32[2,128]{1,0:T(2,128)} %get-tuple-element.28.slots, bf16[256,16,128]{2,1,0:T(8,128)(2,1)} %bitcast.15.back, bf16[64,16,128]{2,1,0:T(8,128)(2,1)} %get-tuple-element.46.upstream), custom_call_target="tpu_custom_call" | custom-call | flops 1000000 | bytes 2000000 | tf_op jit(solution)/shard_map/pallas_call | solution.py:295
  223.0 8.0 %collective-permute-start.9 = (bf16[64,2048]{1,0:T(8,128)(2,1)}, bf16[64,2048]{1,0:T(8,128)(2,1)S(1)}, u32[]{:S(2)}, u32[]{:S(2)}) collective-permute-start(bf16[64,2048]{1,0:T(8,128)(2,1)} %get-tuple-element.47), channel_id=1, source_target_pairs={{0,128},{128,0},{1,129},{129,1},{2,130},{130,2},{3,131},{131,3},{4... | collective-permute-start | bytes 786440 | tf_op jit(solution)/shard_map/ppermute | solution.py:308
  231.0 1.4 collective-permute-done.9
  232.4 1.0 select_bitcast_fusion.1
  233.3 0.8 maximum_bitcast_fusion
  (31 shorter events, 4.8 us)
Async XLA Ops:
  0.6 8.6 %copy-start = (bf16[2,64,2048]{2,1,0:T(8,128)(2,1)S(1)}, bf16[2,64,2048]{2,1,0:T(8,128)(2,1)}, u32[]{:S(2)}) copy-start(bf16[2,64,2048]{2,1,0:T(8,128)(2,1)} %param.9) | copy-start | bytes 1572868
  2.2 7.8 %collective-permute-start.1 = (f32[128]{0:T(128)S(1)}, f32[128]{0:T(128)S(1)}, u32[]{:S(2)}, u32[]{:S(2)}) collective-permute-start(f32[128]{0:T(128)S(1)} %get-tuple-element.59), channel_id=1, source_target_pairs={{0,128},{128,0},{1,129},{129,1},{2,130},{130,2},{3,131},{131,3},{4... | collective-permute-start | bytes 1544 | tf_op jit(solution)/shard_map/ppermute | solution.py:308
  7.2 2.9 %collective-permute-start.2 = (bf16[64,2048]{1,0:T(8,128)(2,1)S(1)}, bf16[64,2048]{1,0:T(8,128)(2,1)}, u32[]{:S(2)}, u32[]{:S(2)}) collective-permute-start(bf16[64,2048]{1,0:T(8,128)(2,1)S(1)} %get-tuple-element.55), channel_id=1, source_target_pairs={{0,128},{128,0},{1,129},{129,1},{2,130},{130,2},{3,131},{131,3},{4... | collective-permute-start | bytes 786440 | tf_op jit(solution)/shard_map/ppermute | solution.py:308
  8.8 1.3 collective-permute-start
  10.1 0.5 copy-start.3
  10.1 0.6 copy-start.4
  17.4 80.9 %all-to-all-start = ((bf16[128,6,16,128]{3,2,1,0:T(8,128)(2,1)}), bf16[128,6,16,128]{3,2,1,0:T(8,128)(2,1)}, u32[]{:S(2)}, u32[]{:S(2)}) async-start(bf16[128,6,16,128]{3,2,1,0:T(8,128)(2,1)} %get-tuple-element.29), calls=%async_computation | async-start | bytes 6291456 | tf_op jit(solution)/shard_map/all_to_all | solution.py:312
  31.6 10.0 %collective-permute-start.3 = (bf16[2048,384]{1,0:T(8,128)(2,1)}, bf16[2048,384]{1,0:T(8,128)(2,1)}, u32[]{:S(2)}, u32[]{:S(2)}) collective-permute-start(bf16[2048,384]{1,0:T(8,128)(2,1)} %bitcast.7.gate.own_gate), channel_id=1, source_target_pairs={{0,128},{128,0},{1,129},{129,1},{2,130},{130,2},{3,131},{131,3},{4... | collective-permute-start | bytes 4718600 | tf_op jit(solution)/shard_map/ppermute | solution.py:308
  36.5 5.6 %collective-permute-start.4 = (bf16[2048,384]{1,0:T(8,128)(2,1)}, bf16[2048,384]{1,0:T(8,128)(2,1)}, u32[]{:S(2)}, u32[]{:S(2)}) collective-permute-start(bf16[2048,384]{1,0:T(8,128)(2,1)} %bitcast.8.up.own_up), channel_id=1, source_target_pairs={{0,128},{128,0},{1,129},{129,1},{2,130},{130,2},{3,131},{131,3},{4... | collective-permute-start | bytes 4718600 | tf_op jit(solution)/shard_map/ppermute | solution.py:308
  36.6 7.8 %collective-permute-start.5 = (bf16[384,2048]{1,0:T(8,128)(2,1)}, bf16[384,2048]{1,0:T(8,128)(2,1)}, u32[]{:S(2)}, u32[]{:S(2)}) collective-permute-start(bf16[384,2048]{1,0:T(8,128)(2,1)} %bitcast.9.down), channel_id=1, source_target_pairs={{0,128},{128,0},{1,129},{129,1},{2,130},{130,2},{3,131},{131,3},{4... | collective-permute-start | bytes 4718600 | tf_op jit(solution)/shard_map/ppermute | solution.py:308
  146.6 33.6 %all-to-all-start.2 = ((bf16[128,2,16,128]{3,2,1,0:T(8,128)(2,1)}), bf16[128,2,16,128]{3,2,1,0:T(8,128)(2,1)}, u32[]{:S(2)}, u32[]{:S(2)}) async-start(bf16[128,2,16,128]{3,2,1,0:T(8,128)(2,1)} %bitcast.50), calls=%async_computation.2 | async-start | bytes 2097152 | tf_op jit(solution)/shard_map/all_to_all | solution.py:312
  186.8 17.0 %copy-start.1 = (bf16[1,1,384,384]{3,2,1,0:T(8,128)(2,1)S(1)}, bf16[1,1,384,384]{3,2,1,0:T(8,128)(2,1)}, u32[]{:S(2)}) copy-start(bf16[1,1,384,384]{3,2,1,0:T(8,128)(2,1)} %param.15) | copy-start | bytes 884740
  186.8 19.7 %copy-start.2 = (bf16[256,384]{1,0:T(8,128)(2,1)S(1)}, bf16[256,384]{1,0:T(8,128)(2,1)}, u32[]{:S(2)}) copy-start(bf16[256,384]{1,0:T(8,128)(2,1)} %get-tuple-element.42) | copy-start | bytes 589828
  186.8 19.9 %copy-start.5 = (bf16[256,384]{1,0:T(8,128)(2,1)S(1)}, bf16[256,384]{1,0:T(8,128)(2,1)}, u32[]{:S(2)}) copy-start(bf16[256,384]{1,0:T(8,128)(2,1)} %get-tuple-element.41) | copy-start | bytes 589828
  186.8 33.5 %all-to-all-start.3 = ((bf16[128,2,16,128]{3,2,1,0:T(8,128)(2,1)}), bf16[128,2,16,128]{3,2,1,0:T(8,128)(2,1)}, u32[]{:S(2)}, u32[]{:S(2)}) async-start(bf16[128,2,16,128]{3,2,1,0:T(8,128)(2,1)} %bitcast.49), calls=%async_computation.3 | async-start | bytes 2097152 | tf_op jit(solution)/shard_map/all_to_all | solution.py:312
  198.2 10.4 %collective-permute-start.8 = (bf16[256,2048]{1,0:T(8,128)(2,1)S(1)}, bf16[256,2048]{1,0:T(8,128)(2,1)S(1)}, u32[]{:S(2)}, u32[]{:S(2)}) collective-permute-start(bf16[256,2048]{1,0:T(8,128)(2,1)S(1)} %get-tuple-element.52), channel_id=1, source_target_pairs={{0,128},{128,0},{1,129},{129,1},{2,130},{130,2},{3,131},{131,3},{4... | collective-permute-start | bytes 3145736 | tf_op jit(solution)/shard_map/ppermute | solution.py:308
  203.7 2.7 %collective-permute-start.6 = (bf16[384,384]{1,0:T(8,128)(2,1)S(1)}, bf16[384,384]{1,0:T(8,128)(2,1)S(1)}, u32[]{:S(2)}, u32[]{:S(2)}) collective-permute-start(bf16[384,384]{1,0:T(8,128)(2,1)S(1)} %bitcast.52), channel_id=1, source_target_pairs={{0,128},{128,0},{1,129},{129,1},{2,130},{130,2},{3,131},{131,3},{4... | collective-permute-start | bytes 884744 | tf_op jit(solution)/shard_map/ppermute | solution.py:308
  207.0 1.5 collective-permute-start.7
  223.0 9.3 %collective-permute-start.9 = (bf16[64,2048]{1,0:T(8,128)(2,1)}, bf16[64,2048]{1,0:T(8,128)(2,1)S(1)}, u32[]{:S(2)}, u32[]{:S(2)}) collective-permute-start(bf16[64,2048]{1,0:T(8,128)(2,1)} %get-tuple-element.47), channel_id=1, source_target_pairs={{0,128},{128,0},{1,129},{129,1},{2,130},{130,2},{3,131},{131,3},{4... | collective-permute-start | bytes 786440 | tf_op jit(solution)/shard_map/ppermute | solution.py:308

commit v2 on v1

--- a/solution.py
+++ b/solution.py
@@ -59,63 +59,77 @@
     return pltpu.make_async_copy(own, target, sem)
 
 
-def dispatch_kernel(
-    own_ids, other_ids, own_w, other_w, own_x, other_x, grad, after, sent, slots, grad_tiles,
-    send, x_upper, x_lower, g_tiles, counts, sems,
-):
+def dispatch_kernel(core, own_ids, other_ids, own_w, other_w, own_x, other_x, grads, *refs):
+    sent, slots_out, tiles_out = refs[-14:-11]
+    send, slots, grad_tiles, own, other, grad, x_upper, x_lower, g_tiles, counts, sems = refs[-11:]
     tokens, width = grad.shape
     depth = width // LANES
     experts = send.shape[0]
-    upper = on_core(1)
-    own = own_x[...].astype(F32)
-    other = other_x[...].astype(F32)
-    rows_to_tiles(jnp.where(upper, own, other), x_upper, tokens, depth)
-    rows_to_tiles(jnp.where(upper, other, own), x_lower, tokens, depth)
-    rows_to_tiles(grad[...].astype(F32), g_tiles, tokens, depth)
-    clear(send, experts)
-
-    def reset(e, carry):
-        counts[0, e] = 0
-        counts[1, e] = 0
-        return carry
-
-    lax.fori_loop(0, experts, reset, 0, unroll=8)
-
-    def first(t, carry):
-        at = pl.ds(pl.multiple_of(t * depth, depth), depth)
-        row = x_upper[at, :].astype(BF16)
-        g = g_tiles[at, :]
-        grad_tiles[t] = g.astype(BF16)
-        for k in range(2):
-            p = 2 * t + k
-            e = jnp.where(upper, own_ids[p], other_ids[p])
-            c = jnp.minimum(counts[0, e], CAP - 1)
-            counts[0, e] = c + 1
-            slots[1, p] = e * CAP + c
-            weight = jnp.where(upper, own_w[p], other_w[p])
-            send[e, c] = row
-            send[e, CAP + c] = (weight * g).astype(BF16)
-        return carry
-
-    lax.fori_loop(0, tokens, first, 0, unroll=2)
-    urgent = fetch(send.at[:, : 2 * CAP], sent.at[:, : 2 * CAP], sems.at[0])
-
-    def second(t, carry):
-        at = pl.ds(pl.multiple_of(t * depth, depth), depth)
-        row = x_lower[at, :].astype(BF16)
-        for k in range(2):
-            p = 2 * t + k
-            e = jnp.where(upper, other_ids[p], own_ids[p])
-            c = jnp.minimum(counts[1, e], CAP - 1)
-            counts[1, e] = c + 1
-            slots[0, p] = e * CAP + c
-            send[e, 2 * CAP + c] = row
-        return carry
-
-    lax.fori_loop(0, tokens, second, 0, unroll=2)
-    rest = fetch(send.at[:, 2 * CAP :], sent.at[:, 2 * CAP :], sems.at[1])
-    urgent.wait()
-    rest.wait()
+    upper = core == 1
+
+    def work():
+        copies = [
+            fetch(own_x.at[core], own, sems.at[0]),
+            fetch(other_x, other, sems.at[1]),
+            fetch(grads.at[core], grad, sems.at[2]),
+        ]
+        first_ids, second_ids = (own_ids, other_ids) if upper else (other_ids, own_ids)
+        weights = own_w if upper else other_w
+        clear(send, experts)
+
+        def reset(e, carry):
+            counts[0, e] = 0
+            counts[1, e] = 0
+            return carry
+
+        lax.fori_loop(0, experts, reset, 0, unroll=8)
+        for copy in copies:
+            copy.wait()
+        first_x, second_x = (own, other) if upper else (other, own)
+        rows_to_tiles(first_x[...].astype(F32), x_upper, tokens, depth)
+        rows_to_tiles(second_x[...].astype(F32), x_lower, tokens, depth)
+        rows_to_tiles(grad[...].astype(F32), g_tiles, tokens, depth)
+
+        def first(t, carry):
+            at = pl.ds(pl.multiple_of(t * depth, depth), depth)
+            row = x_upper[at, :].astype(BF16)
+            g = g_tiles[at, :]
+            grad_tiles[t] = g.astype(BF16)
+            for k in range(2):
+                p = 2 * t + k
+                e = first_ids[core, p]
+                c = jnp.minimum(counts[0, e], CAP - 1)
+                counts[0, e] = c + 1
+                slots[1, p] = e * CAP + c
+                send[e, c] = row
+                send[e, CAP + c] = (weights[core, p] * g).astype(BF16)
+            return carry
+
+        lax.fori_loop(0, tokens, first, 0, unroll=2)
+        saves = [
+            fetch(send.at[:, : 2 * CAP], sent.at[:, : 2 * CAP], sems.at[3]),
+            fetch(grad_tiles, tiles_out, sems.at[4]),
+        ]
+
+        def second(t, carry):
+            at = pl.ds(pl.multiple_of(t * depth, depth), depth)
+            row = x_lower[at, :].astype(BF16)
+            for k in range(2):
+                p = 2 * t + k
+                e = second_ids[core, p]
+                c = jnp.minimum(counts[1, e], CAP - 1)
+                counts[1, e] = c + 1
+                slots[0, p] = e * CAP + c
+                send[e, 2 * CAP + c] = row
+            return carry
+
+        lax.fori_loop(0, tokens, second, 0, unroll=2)
+        saves.append(fetch(send.at[:, 2 * CAP :], sent.at[:, 2 * CAP :], sems.at[5]))
+        saves.append(fetch(slots, slots_out, sems.at[6]))
+        for copy in saves:
+            copy.wait()
+
+    pl.when(on_core(core))(work)
 
 
 def relay_kernel(slots, own_w, other_w, back, upstream, sent, grad_out, send, sems):
@@ -132,7 +146,7 @@
         g = rounded.astype(F32)
         for k in range(2):
             p = 2 * t + k
-            weight = jnp.where(upper, other_w[p], own_w[p])
+            weight = jnp.where(upper, other_w[1, p], own_w[0, p])
             send[slots[0, p]] = (weight * g).astype(BF16)
         return carry
 
@@ -163,30 +177,39 @@
         away[:, columns] = jnp.where(upper, down, high).astype(BF16)
 
 
-def turn_kernel(turn, gate, up, down, *refs):
-    gate_up_t, down_t, a, b, c, turned, turned_down, sems = refs[-8:]
-    hidden, width = down.shape
+def turn_kernel(core, *refs):
+    outs, (a, b, c, turned, turned_down, sems) = refs[-10:-6], refs[-6:]
+    hidden, width = refs[2].shape
     step = 256
 
     def work():
-        copies = [
-            fetch(gate, a, sems.at[0]), fetch(up, b, sems.at[1]), fetch(down, c, sems.at[2])
-        ]
-        for n, block in enumerate((a, b)):
-            copies[n].wait()
+        saves = []
+        for layer in range(2):
+            copies = [
+                fetch(source, target, sems.at[layer, n])
+                for n, (source, target) in enumerate(
+                    zip(refs[3 * layer : 3 * layer + 3], (a.at[layer], b.at[layer], c.at[layer]))
+                )
+            ]
+            saves.append(copies)
+        for layer, copies in enumerate(saves):
+            gate_up_t, down_t = outs[2 * layer], outs[2 * layer + 1]
+            for n, block in enumerate((a, b)):
+                copies[n].wait()
+                for i in range(0, width, step):
+                    turned[layer, n * hidden : (n + 1) * hidden, i : i + step] = block[
+                        layer, i : i + step, :
+                    ].T
+            copies.append(fetch(turned.at[layer], gate_up_t, sems.at[layer, 3]))
+            copies[2].wait()
             for i in range(0, width, step):
-                turned[n * hidden : (n + 1) * hidden, i : i + step] = block[i : i + step, :].T
-        first = fetch(turned, gate_up_t, sems.at[3])
-        copies[2].wait()
-        for i in range(0, width, step):
-            turned_down[i : i + step, :] = c[:, i : i + step].T
-        fetch(turned_down, down_t, sems.at[4]).wait()
-        first.wait()
-
-    if turn is None:
-        work()
-    else:
-        pl.when(on_core(turn))(work)
+                turned_down[layer, i : i + step, :] = c[layer, :, i : i + step].T
+            copies.append(fetch(turned_down.at[layer], down_t, sems.at[layer, 4]))
+        for copies in saves:
+            copies[3].wait()
+            copies[4].wait()
+
+    pl.when(on_core(core))(work)
 
 
 def untile(block, tiles, rows, depth):
@@ -224,7 +247,7 @@
 
 
 def upper_kernel(
-    arrived, own_gate, other_gate, own_up, other_up, own_dt, other_dt, own_gut, other_gut,
+    arrived, own_gate, other_gate, own_up, other_up, turned_down, turned,
     sent, dy_out, act_out,
     x, dy, gate, up, down_t, gate_up_t, tiles, x_rows, dy_rows, activ, send, sems,
 ):
@@ -234,8 +257,8 @@
     gate_copy = fetch_one_of(mine, own_gate, other_gate, gate, sems.at[1])
     up_copy = fetch_one_of(mine, own_up, other_up, up, sems.at[2])
     dy_copy = fetch(arrived.at[:, CAP : 2 * CAP], dy, sems.at[3])
-    down_copy = fetch_one_of(mine, own_dt, other_dt, down_t, sems.at[4])
-    back_copy = fetch_one_of(mine, own_gut, other_gut, gate_up_t, sems.at[5])
+    down_copy = fetch(turned_down, down_t, sems.at[4])
+    back_copy = fetch(turned, gate_up_t, sems.at[5])
     x_copy.wait()
     untile(x, tiles, x_rows, depth)
     gate_copy.wait()
@@ -273,12 +296,11 @@
 
 
 def lower_kernel(
-    dy, act, slope, own_dt, other_dt, own_gut, other_gut, sent, dy_out,
+    dy, act, slope, turned_down, turned, sent, dy_out,
     down_t, gate_up_t, tiles, dy_rows, send, sems,
 ):
-    mine = on_core(0)
-    down_copy = fetch_one_of(mine, own_dt, other_dt, down_t, sems.at[0])
-    back_copy = fetch_one_of(mine, own_gut, other_gut, gate_up_t, sems.at[1])
+    down_copy = fetch(turned_down, down_t, sems.at[0])
+    back_copy = fetch(turned, gate_up_t, sems.at[1])
     untile(dy, tiles, dy_rows, send.shape[1])
     save = fetch(dy_rows, dy_out, sems.at[2])
     down_copy.wait()
@@ -326,60 +348,71 @@
     count = experts * CAP
     gate, up, down, basis = w_gate[0, 0], w_up[0, 0], w_down[0, 0], eigenbasis[0, 0]
 
-    ids = expert_ids[0].reshape(micros, tokens * 2)
-    weights = router_weights[0].reshape(micros, tokens * 2)
-    mine = functools.partial(lax.dynamic_index_in_dim, index=segment, axis=0, keepdims=False)
-    theirs = functools.partial(lax.dynamic_index_in_dim, index=1 - segment, axis=0, keepdims=False)
-    own_x, other_x = mine(saved_input[0]), swapped(theirs(saved_input[0]))
-    own_ids, other_ids = mine(ids), swapped(theirs(ids))
-    own_w, other_w = mine(weights), swapped(theirs(weights))
-    grad = mine(out_grad)
-
+    theirs = lax.dynamic_index_in_dim(saved_input[0], 1 - segment, 0, keepdims=False)
+    other_x = swapped(theirs)
+    own_ids = expert_ids[0].reshape(micros, tokens * 2)
+    own_w = router_weights[0].reshape(micros, tokens * 2)
+    other_ids, other_w = swapped(own_ids), swapped(own_w)
+
+    tile_rows = tokens * depth
     matrix = pltpu.VMEM((width, hidden), BF16)
-    turned_shapes = (shape((2 * hidden, width)), shape((width, hidden)))
-    turn_scratch = [
-        matrix, matrix, pltpu.VMEM((hidden, width), BF16), pltpu.VMEM((2 * hidden, width), BF16),
-        matrix, pltpu.SemaphoreType.DMA((5,)),
-    ]
-
-    def turned(turn, matrices, made=()):
+    pair = pltpu.VMEM((2, width, hidden), BF16)
+    pair_t = pltpu.VMEM((2, 2 * hidden, width), BF16)
+    row_block = pltpu.VMEM((tokens, width), BF16)
+
+    def dispatched(core, after, made=()):
+        inputs = (own_ids, other_ids, own_w, other_w, saved_input[0], other_x, out_grad)
         return call(
-            functools.partial(turn_kernel, turn),
-            (*matrices, *made),
-            [HBM] * (3 + len(made)),
-            turned_shapes,
-            (HBM,) * 2,
-            turn_scratch,
+            functools.partial(dispatch_kernel, core),
+            (*inputs, *after, *made),
+            [SMEM] * 4 + [HBM] * (3 + len(after) + len(made)),
+            (
+                shape((experts, 3 * CAP, depth, LANES)),
+                shape((2, tokens * 2), jnp.int32),
+                shape((tokens, depth, LANES)),
+            ),
+            (HBM,) * 3,
+            [
+                pltpu.VMEM((experts, 3 * CAP, depth, LANES), BF16),
+                pltpu.SMEM((2, tokens * 2), jnp.int32),
+                pltpu.VMEM((tokens, depth, LANES), BF16),
+            ]
+            + [row_block] * 3
+            + [pltpu.VMEM((tile_rows, LANES), F32)] * 3
+            + [pltpu.SMEM((2, experts), jnp.int32), pltpu.SemaphoreType.DMA((7,))],
             1_000_000,
-            9_000_000,
-            {3: 0, 4: 1} if made else {},
+            5_000_000,
+            {len(inputs) + len(after) + n: n for n in range(len(made))},
         )
 
-    early_gut, early_dt = turned(0, (gate, up, down))
-
-    tile_rows = tokens * depth
-    send, slots, grad_tiles = call(
-        dispatch_kernel,
-        (own_ids, other_ids, own_w, other_w, own_x, other_x, grad, early_dt),
-        [SMEM] * 4 + [VMEM] * 3 + [HBM],
-        (
-            shape((experts, 3 * CAP, depth, LANES)),
-            shape((2, tokens * 2), jnp.int32),
-            shape((tokens, depth, LANES)),
-        ),
-        (HBM, SMEM, VMEM),
-        [pltpu.VMEM((experts, 3 * CAP, depth, LANES), BF16)]
-        + [pltpu.VMEM((tile_rows, LANES), F32)] * 3
-        + [pltpu.SMEM((2, experts), jnp.int32), pltpu.SemaphoreType.DMA((2,))],
-        1_000_000,
-        5_000_000,
-    )
+    def turned(core, matrices, after, made=()):
+        return call(
+            functools.partial(turn_kernel, core),
+            (*matrices, *after, *made),
+            [HBM] * (6 + len(after) + len(made)),
+            (shape((2 * hidden, width)), shape((width, hidden))) * 2,
+            (HBM,) * 4,
+            [
+                pair, pair, pltpu.VMEM((2, hidden, width), BF16), pair_t, pair,
+                pltpu.SemaphoreType.DMA((2, 5)),
+            ],
+            1_000_000,
+            18_000_000,
+            {6 + len(after) + n: n for n in range(len(made))},
+        )
+
+    def moved(block, source):
+        return lax.ppermute(block, "segment", [(source, 1 - source)])
+
+    first_sent = dispatched(1, ())
+    layer1 = tuple(moved(block, 1) for block in (gate, up, down))
+    early = turned(0, (*layer1, gate, up, down), first_sent[2:])
+    send, slots, grad_tiles = dispatched(0, early[:1], first_sent)
     arrived = exchanged(send)
 
-    own_gut, own_dt = turned(1, (gate, up, down), (early_gut, early_dt))
-    other_gate, other_up, other_down = swapped(gate), swapped(up), swapped(down)
+    layer0 = tuple(moved(block, 0) for block in (gate, up, down))
     other_basis = swapped(basis)
-    other_gut, other_dt = turned(None, (other_gate, other_up, other_down))
+    gut1, dt1, gut0, dt0 = turned(1, (gate, up, down, *layer0), (), early)
 
     tiles = pltpu.VMEM((count * depth, LANES), F32)
     rows = pltpu.VMEM((count, width), BF16)
@@ -389,8 +422,8 @@
     mat = 2 * count * width * hidden
     back_send, dy_rows1, activ1 = call(
         upper_kernel,
-        (arrived, gate, other_gate, up, other_up, own_dt, other_dt, own_gut, other_gut),
-        [HBM] * 9,
+        (arrived, gate, layer1[0], up, layer1[1], dt1, gut1),
+        [HBM] * 7,
         (shape(flat), shape((count, width)), shape((count, hidden))),
         (HBM,) * 3,
         [
@@ -408,7 +441,7 @@
     back = returned(back_send)
     act0, slope0, activ0 = call(
         forward_kernel,
-        (arrived, gate, other_gate, up, other_up),
+        (arrived, gate, layer0[0], up, layer0[1]),
         [HBM] * 5,
         (shape((count, hidden), F32), shape((count, hidden), F32), shape((count, hidden))),
         (VMEM,) * 3,
@@ -434,8 +467,8 @@
     dy = returned(dy_send)
     back_send0, dy_rows0 = call(
         lower_kernel,
-        (dy, act0, slope0, own_dt, other_dt, own_gut, other_gut),
-        [VMEM] * 3 + [HBM] * 4,
+        (dy, act0, slope0, dt0, gut0),
+        [VMEM] * 3 + [HBM] * 2,
         (shape(flat), shape((count, width))),
         (HBM,) * 2,
         [

time: 235 us -> 238 us (1.013)
  starting transfers between devices: 56.8 us -> 66.7 us
  Pallas kernels: 41.2 us -> 38.1 us
  blocking collectives: 36.8 us -> 34.4 us
    ppermute x0 -> x6, starting transfers between devices: none -> 15.2 us  [moved(): return lax.ppermute(block, 'segment', [(source, 1 - source)])]
    ppermute x0 -> x6, waiting for transfers between devices: none -> 11.5 us  [moved(): return lax.ppermute(block, 'segment', [(source, 1 - source)])]
    all_to_all x3, waiting for transfers between devices: 75.7 us -> 67.7 us  [exchanged(): lax.all_to_all(block, 'expert', split_axis=0, concat_axis=0, tiled=True)]
    ppermute x10 -> x7, starting transfers between devices: 23.3 us -> 17.9 us  [swapped(): return lax.ppermute(block, 'segment', [(0, 1), (1, 0)])]
    pallas_call x9, Pallas kernels: 41.2 us -> 38.1 us  [call(): pl.pallas_call(kernel, in_specs=in_specs, out_shape=out_shape, out_specs=...]
    squeeze x4 -> x1, local copies, waits for them, and re-layouts: 3.68 us -> 0.97 us  [shards(): lax.dynamic_index_in_dim(saved_input[0], 1 - segment, 0, keepdims=False)]
    all_to_all x1, blocking collectives: 36.8 us -> 34.4 us  [exchanged(): lax.all_to_all(block, 'expert', split_axis=0, concat_axis=0, tiled=True)]
    ppermute x10 -> x7, waiting for transfers between devices: 7.83 us -> 5.5 us  [swapped(): return lax.ppermute(block, 'segment', [(0, 1), (1, 0)])]
  transfers between devices with their start and end apart: 13 -> 16, of which waited for: 8 -> 10; matrix products, arithmetic and copies ran while one was open for 5% -> 4% of each run, Pallas kernels for 6% -> 7%
where the time goes in v2:
time: 238 us; the launch traced here: 237 us
  waiting for transfers between devices  84.7 us (36%)
  starting transfers between devices  66.7 us (28%)
  Pallas kernels  38.1 us (16%)
  blocking collectives  34.4 us (14%)
  matrix products  5.43 us (2%)
  local copies, waits for them, and re-layouts  4.71 us (2%)
    all_to_all x3, waiting for transfers between devices, exchanged(): lax.all_to_all(block, 'expert', split_axis=0, concat_axis=0, tiled=True)  67.7 us
    pallas_call x9, Pallas kernels, call(): pl.pallas_call(kernel, in_specs=in_specs, out_shape=out_shape, out_specs=...  38.1 us
    all_to_all x1, blocking collectives, exchanged(): lax.all_to_all(block, 'expert', split_axis=0, concat_axis=0, tiled=True)  34.4 us
    all_to_all x3, starting transfers between devices, exchanged(): lax.all_to_all(block, 'expert', split_axis=0, concat_axis=0, tiled=True)  33.7 us
    ppermute x7, starting transfers between devices, swapped(): return lax.ppermute(block, 'segment', [(0, 1), (1, 0)])  17.9 us
    ppermute x6, starting transfers between devices, moved(): return lax.ppermute(block, 'segment', [(source, 1 - source)])  15.2 us
    ppermute x6, waiting for transfers between devices, moved(): return lax.ppermute(block, 'segment', [(source, 1 - source)])  11.5 us
    ppermute x7, waiting for transfers between devices, swapped(): return lax.ppermute(block, 'segment', [(0, 1), (1, 0)])  5.5 us
  transfers between devices with their start and end apart: 16, of which 10 were waited for; matrix products, arithmetic and copies ran while one was open for 4% of the time, Pallas kernels for 7%

profile of v2, /device:TPU:1, one launch (start us, length us, event | category | flops | bytes accessed | tf_op | source)
XLA Modules:
  0.0 237.0 jit_solution(576607378118401313)
XLA Ops:
  0.6 6.3 %collective-permute-start.3 = (bf16[2048,384]{1,0:T(8,128)(2,1)}, bf16[2048,384]{1,0:T(8,128)(2,1)}, u32[]{:S(2)}, u32[]{:S(2)}) collective-permute-start(bf16[2048,384]{1,0:T(8,128)(2,1)} %bitcast.37), channel_id=1, source_target_pairs={{128,0},{129,1},{130,2},{131,3},{132,4},{133,5},{134,6},{135,7},{1... | collective-permute-start | bytes 4718600 | tf_op jit(solution)/shard_map/ppermute | solution.py:405
  6.9 2.5 %collective-permute-start.4 = (bf16[2048,384]{1,0:T(8,128)(2,1)}, bf16[2048,384]{1,0:T(8,128)(2,1)}, u32[]{:S(2)}, u32[]{:S(2)}) collective-permute-start(bf16[2048,384]{1,0:T(8,128)(2,1)} %bitcast.43), channel_id=1, source_target_pairs={{128,0},{129,1},{130,2},{131,3},{132,4},{133,5},{134,6},{135,7},{1... | collective-permute-start | bytes 4718600 | tf_op jit(solution)/shard_map/ppermute | solution.py:405
  9.4 2.5 %collective-permute-start.5 = (bf16[384,2048]{1,0:T(8,128)(2,1)}, bf16[384,2048]{1,0:T(8,128)(2,1)}, u32[]{:S(2)}, u32[]{:S(2)}) collective-permute-start(bf16[384,2048]{1,0:T(8,128)(2,1)} %bitcast.49), channel_id=1, source_target_pairs={{128,0},{129,1},{130,2},{131,3},{132,4},{133,5},{134,6},{135,7},{1... | collective-permute-start | bytes 4718600 | tf_op jit(solution)/shard_map/ppermute | solution.py:405
  15.6 1.0 collective-permute-done.other_ids
  17.4 5.9 %shard_map.103 = (bf16[128,6,16,128]{3,2,1,0:T(8,128)(2,1)}, s32[2,128]{1,0:T(2,128)}, bf16[64,16,128]{2,1,0:T(8,128)(2,1)}) custom-call(s32[2,128]{1,0:T(2,128)} %copy-done.11, s32[2,128]{1,0:T(2,128)} %copy-done.13, f32[2,128]{1,0:T(2,128)} %copy-done.10, f32[2,128]{1,0:T(2,128)} %copy-done.12, bf16[2,64,2048]{2,1,0:T(8,128)(2,1)} %bitcast.54, ...), custom_call_target="tpu_custom_call" | custom-call | flops 1000000 | bytes 5000000 | tf_op jit(solution)/shard_map/pallas_call | solution.py:317
  24.3 14.5 %all-to-all-start = ((bf16[128,6,16,128]{3,2,1,0:T(8,128)(2,1)}), bf16[128,6,16,128]{3,2,1,0:T(8,128)(2,1)}, u32[]{:S(2)}, u32[]{:S(2)}) async-start(bf16[128,6,16,128]{3,2,1,0:T(8,128)(2,1)} %get-tuple-element.37), calls=%async_computation | async-start | bytes 6291456 | tf_op jit(solution)/shard_map/all_to_all | solution.py:334
  38.8 1.3 collective-permute-start.6
  40.1 1.3 collective-permute-start.7
  41.4 1.3 collective-permute-start.8
  42.7 6.8 %collective-permute-done.6.refs_3_.other_gate = bf16[2048,384]{1,0:T(8,128)(2,1)S(1)} collective-permute-done((bf16[2048,384]{1,0:T(8,128)(2,1)S(1)}, bf16[2048,384]{1,0:T(8,128)(2,1)S(1)}, u32[]{:S(2)}, u32[]{:S(2)}) %collective-permute-start.6) | collective-permute-done | bytes 1572896 | tf_op jit(solution)/shard_map/ppermute | solution.py:405
  49.5 2.2 collective-permute-done.7.refs_4_.other_up
  51.8 2.5 %collective-permute-done.8.refs_5_ = bf16[384,2048]{1,0:T(8,128)(2,1)S(1)} collective-permute-done((bf16[384,2048]{1,0:T(8,128)(2,1)}, bf16[384,2048]{1,0:T(8,128)(2,1)S(1)}, u32[]{:S(2)}, u32[]{:S(2)}) %collective-permute-start.8) | collective-permute-done | bytes 1572896 | tf_op jit(solution)/shard_map/ppermute | solution.py:405
  54.2 1.2 copy-done.4
  55.4 6.4 %shard_map.106 = (bf16[768,2048]{1,0:T(8,128)(2,1)}, bf16[2048,384]{1,0:T(8,128)(2,1)}, bf16[768,2048]{1,0:T(8,128)(2,1)}, bf16[2048,384]{1,0:T(8,128)(2,1)}) custom-call(bf16[2048,384]{1,0:T(8,128)(2,1)} %bitcast.39, bf16[2048,384]{1,0:T(8,128)(2,1)} %bitcast.45, ...), custom_call_target="tpu_custom_call", output_to_operand_aliasing={{0}: (6, {}), {1}: (7, {}), {2}: (8, {}), {3}: (9, {})} | custom-call | flops 1000000 | bytes 18000000 | tf_op jit(solution)/shard_map/pallas_call | solution.py:317
  61.8 43.1 %all-to-all-done.arrived = bf16[128,6,16,128]{3,2,1,0:T(8,128)(2,1)} async-done(((bf16[128,6,16,128]{3,2,1,0:T(8,128)(2,1)}), bf16[128,6,16,128]{3,2,1,0:T(8,128)(2,1)}, u32[]{:S(2)}, u32[]{:S(2)}) %all-to-all-start) | async-done | bytes 3145760 | tf_op jit(solution)/shard_map/all_to_all | solution.py:334
  104.8 7.6 %shard_map.107 = (bf16[256,16,128]{2,1,0:T(8,128)(2,1)}, bf16[256,2048]{1,0:T(8,128)(2,1)}, bf16[256,384]{1,0:T(8,128)(2,1)}) custom-call(bf16[128,6,16,128]{3,2,1,0:T(8,128)(2,1)} %all-to-all-done.arrived, bf16[2048,384]{1,0:T(8,128)(2,1)} %bitcast.40, bf16[2048,384]{1,0:T(8,128)(2,1)} %collective-permute-done.3.refs_0_.other_gate, ...), custom_call_target="tpu_custom_call" | custom-call | flops 2013265920 | bytes 9000000 | tf_op jit(solution)/shard_map/pallas_call | solution.py:317
  112.5 34.4 %all_to_all.20 = bf16[128,2,16,128]{3,2,1,0:T(8,128)(2,1)} all-to-all(bf16[128,2,16,128]{3,2,1,0:T(8,128)(2,1)} %bitcast.58), channel_id=1, replica_groups=mesh['segment'=2,'expert'=128] {'expert'}, dimensions={0} | all-to-all | bytes 2097152 | tf_op jit(solution)/shard_map/all_to_all | solution.py:334
  146.8 3.8 %shard_map.108 = (bf16[256,16,128]{2,1,0:T(8,128)(2,1)}, bf16[64,16,128]{2,1,0:T(8,128)(2,1)}) custom-call(s32[2,128]{1,0:T(2,128)} %get-tuple-element.36.slots, f32[2,128]{1,0:T(2,128)} %copy-done.10, f32[2,128]{1,0:T(2,128)} %copy-done.12, bf16[256,16,128]{2,1,0:T(8,128)(2,1)} %bitcast.53, bf16[64,16,128]{2,1,0:T(8,128)(2,1)} %get-tuple-element.44.upstream), custom_call_target="tpu_custom_call" | custom-call | flops 1000000 | bytes 3000000 | tf_op jit(solution)/shard_map/pallas_call | solution.py:317
  150.6 9.8 %all-to-all-start.2 = ((bf16[128,2,16,128]{3,2,1,0:T(8,128)(2,1)}), bf16[128,2,16,128]{3,2,1,0:T(8,128)(2,1)}, u32[]{:S(2)}, u32[]{:S(2)}) async-start(bf16[128,2,16,128]{3,2,1,0:T(8,128)(2,1)} %bitcast.57), calls=%async_computation.2 | async-start | bytes 2097152 | tf_op jit(solution)/shard_map/all_to_all | solution.py:334
  160.4 4.4 %shard_map.109 = (f32[256,384]{1,0:T(8,128)}, f32[256,384]{1,0:T(8,128)}, bf16[256,384]{1,0:T(8,128)(2,1)}) custom-call(bf16[128,6,16,128]{3,2,1,0:T(8,128)(2,1)} %all-to-all-done.arrived, bf16[2048,384]{1,0:T(8,128)(2,1)} %bitcast.41, bf16[2048,384]{1,0:T(8,128)(2,1)} %copy-done.2, bf16[2048,384]{1,0:T(8,128)(2,1)} %bitcast.47, bf16[2048,384]{1,0:T(8,128)(2,1)} %copy-done.3), custom_call_target="tpu_custom_call" | custom-call | flops 805306368 | bytes 5000000 | tf_op jit(solution)/shard_map/pallas_call | solution.py:317
  164.8 18.6 %all-to-all-done.2 = bf16[128,2,16,128]{3,2,1,0:T(8,128)(2,1)} async-done(((bf16[128,2,16,128]{3,2,1,0:T(8,128)(2,1)}), bf16[128,2,16,128]{3,2,1,0:T(8,128)(2,1)}, u32[]{:S(2)}, u32[]{:S(2)}) %all-to-all-start.2) | async-done | bytes 1048608 | tf_op jit(solution)/shard_map/all_to_all | solution.py:334
  183.4 6.4 %shard_map.110 = (bf16[256,16,128]{2,1,0:T(8,128)(2,1)}, bf16[256,2048]{1,0:T(8,128)(2,1)}) custom-call(bf16[256,16,128]{2,1,0:T(8,128)(2,1)} %bitcast.8.dy, f32[256,384]{1,0:T(8,128)} %get-tuple-element.46.act, f32[256,384]{1,0:T(8,128)} %get-tuple-element.47.slope, bf16[2048,384]{1,0:T(8,128)(2,1)} %get-tuple-element.48.turned_down, ...), custom_call_target="tpu_custom_call" | custom-call | flops 1207959552 | bytes 8000000 | tf_op jit(solution)/shard_map/pallas_call | solution.py:317
  189.8 9.4 %all-to-all-start.3 = ((bf16[128,2,16,128]{3,2,1,0:T(8,128)(2,1)}), bf16[128,2,16,128]{3,2,1,0:T(8,128)(2,1)}, u32[]{:S(2)}, u32[]{:S(2)}) async-start(bf16[128,2,16,128]{3,2,1,0:T(8,128)(2,1)} %bitcast.56), calls=%async_computation.3 | async-start | bytes 2097152 | tf_op jit(solution)/shard_map/all_to_all | solution.py:334
  199.4 6.8 %collective-permute-start.11 = (bf16[256,2048]{1,0:T(8,128)(2,1)S(1)}, bf16[256,2048]{1,0:T(8,128)(2,1)S(1)}, u32[]{:S(2)}, u32[]{:S(2)}) collective-permute-start(bf16[256,2048]{1,0:T(8,128)(2,1)S(1)} %get-tuple-element.62), channel_id=1, source_target_pairs={{0,128},{128,0},{1,129},{129,1},{2,130},{130,2},{3,131},{131,3},{4... | collective-permute-start | bytes 3145736 | tf_op jit(solution)/shard_map/ppermute | solution.py:330
  206.9 2.0 collective-permute-done.9
  210.0 1.1 collective-permute-done.10
  211.0 2.2 multiply_convert_fusion.1
  213.2 2.7 %convolution_multiply_fusion = f32[384,2048]{1,0:T(8,128)} fusion(bf16[256,2048]{1,0:T(8,128)(2,1)S(1)} %collective-permute-done.11, bf16[256,2048]{1,0:T(8,128)(2,1)S(1)} %get-tuple-element.61, bf16[256,384]{1,0:T(8,128)(2,1)S(1)} %collective-permute-done.10, bf16[256,384]{1,0:T(8,128)(2,1)S(1)} %get-tuple-element.65), kind=kOutput, calls=%fused_computation.2 | convolution fusion | flops 813563904 | bytes 5636096 | tf_op jit(solution)/shard_map/dot_general | solution.py:501
  215.9 6.0 %all-to-all-done.3 = bf16[128,2,16,128]{3,2,1,0:T(8,128)(2,1)} async-done(((bf16[128,2,16,128]{3,2,1,0:T(8,128)(2,1)}), bf16[128,2,16,128]{3,2,1,0:T(8,128)(2,1)}, u32[]{:S(2)}, u32[]{:S(2)}) %all-to-all-start.3) | async-done | bytes 1048608 | tf_op jit(solution)/shard_map/all_to_all | solution.py:334
  221.9 2.7 %shard_map.111 = (bf16[64,2048]{1,0:T(8,128)(2,1)}, bf16[64,2048]{1,0:T(8,128)(2,1)}) custom-call(s32[2,128]{1,0:T(2,128)} %get-tuple-element.36.slots, bf16[256,16,128]{2,1,0:T(8,128)(2,1)} %bitcast.10.back, bf16[64,16,128]{2,1,0:T(8,128)(2,1)} %get-tuple-element.56.upstream), custom_call_target="tpu_custom_call" | custom-call | flops 1000000 | bytes 2000000 | tf_op jit(solution)/shard_map/pallas_call | solution.py:317
  224.7 9.1 %collective-permute-start.12 = (bf16[64,2048]{1,0:T(8,128)(2,1)}, bf16[64,2048]{1,0:T(8,128)(2,1)S(1)}, u32[]{:S(2)}, u32[]{:S(2)}) collective-permute-start(bf16[64,2048]{1,0:T(8,128)(2,1)} %get-tuple-element.57), channel_id=1, source_target_pairs={{0,128},{128,0},{1,129},{129,1},{2,130},{130,2},{3,131},{131,3},{4... | collective-permute-start | bytes 786440 | tf_op jit(solution)/shard_map/ppermute | solution.py:330
  233.7 1.4 collective-permute-done.12
  (52 shorter events, 9.0 us)
Async XLA Ops:
  0.6 22.6 %collective-permute-start.3 = (bf16[2048,384]{1,0:T(8,128)(2,1)}, bf16[2048,384]{1,0:T(8,128)(2,1)}, u32[]{:S(2)}, u32[]{:S(2)}) collective-permute-start(bf16[2048,384]{1,0:T(8,128)(2,1)} %bitcast.37), channel_id=1, source_target_pairs={{128,0},{129,1},{130,2},{131,3},{132,4},{133,5},{134,6},{135,7},{1... | collective-permute-start | bytes 4718600 | tf_op jit(solution)/shard_map/ppermute | solution.py:405
  6.9 16.4 %collective-permute-start.4 = (bf16[2048,384]{1,0:T(8,128)(2,1)}, bf16[2048,384]{1,0:T(8,128)(2,1)}, u32[]{:S(2)}, u32[]{:S(2)}) collective-permute-start(bf16[2048,384]{1,0:T(8,128)(2,1)} %bitcast.43), channel_id=1, source_target_pairs={{128,0},{129,1},{130,2},{131,3},{132,4},{133,5},{134,6},{135,7},{1... | collective-permute-start | bytes 4718600 | tf_op jit(solution)/shard_map/ppermute | solution.py:405
  9.4 13.8 %collective-permute-start.5 = (bf16[384,2048]{1,0:T(8,128)(2,1)}, bf16[384,2048]{1,0:T(8,128)(2,1)}, u32[]{:S(2)}, u32[]{:S(2)}) collective-permute-start(bf16[384,2048]{1,0:T(8,128)(2,1)} %bitcast.49), channel_id=1, source_target_pairs={{128,0},{129,1},{130,2},{131,3},{132,4},{133,5},{134,6},{135,7},{1... | collective-permute-start | bytes 4718600 | tf_op jit(solution)/shard_map/ppermute | solution.py:405
  12.9 3.8 %collective-permute-start.2 = (bf16[64,2048]{1,0:T(8,128)(2,1)S(1)}, bf16[64,2048]{1,0:T(8,128)(2,1)S(1)}, u32[]{:S(2)}, u32[]{:S(2)}) collective-permute-start(bf16[64,2048]{1,0:T(8,128)(2,1)S(1)} %dynamic-slice_bitcast_fusion), channel_id=1, source_target_pairs={{0,128},{128,0},{1,129},{129,1},{2,130},{130,2},{3,131},{131,3},{4... | collective-permute-start | bytes 786440 | tf_op jit(solution)/shard_map/ppermute | solution.py:330
  13.9 2.8 %copy-start.10 = (f32[2,128]{1,0:T(2,128)}, f32[2,128]{1,0:T(2,128)S(1)}, u32[]{:S(2)}) copy-start(f32[2,128]{1,0:T(2,128)S(1)} %reshape_squeeze.7.own_w) | copy-start | bytes 3076
  13.9 1.5 collective-permute-start.1
  15.4 1.3 copy-start.11
  15.4 1.3 copy-start.12
  15.5 1.2 collective-permute-start
  16.7 0.5 copy-start.13
  16.7 0.7 copy-start.7
  24.2 14.5 %copy-start = (bf16[1,1,2048,384]{3,2,1,0:T(8,128)(2,1)S(1)}, bf16[1,1,2048,384]{3,2,1,0:T(8,128)(2,1)}, u32[]{:S(2)}) copy-start(bf16[1,1,2048,384]{3,2,1,0:T(8,128)(2,1)} %param.12) | copy-start | bytes 4718596
  24.3 15.8 %copy-start.1 = (bf16[1,1,2048,384]{3,2,1,0:T(8,128)(2,1)S(1)}, bf16[1,1,2048,384]{3,2,1,0:T(8,128)(2,1)}, u32[]{:S(2)}) copy-start(bf16[1,1,2048,384]{3,2,1,0:T(8,128)(2,1)} %param.13) | copy-start | bytes 4718596
  24.3 80.6 %all-to-all-start = ((bf16[128,6,16,128]{3,2,1,0:T(8,128)(2,1)}), bf16[128,6,16,128]{3,2,1,0:T(8,128)(2,1)}, u32[]{:S(2)}, u32[]{:S(2)}) async-start(bf16[128,6,16,128]{3,2,1,0:T(8,128)(2,1)} %get-tuple-element.37), calls=%async_computation | async-start | bytes 6291456 | tf_op jit(solution)/shard_map/all_to_all | solution.py:334
  38.8 10.7 %collective-permute-start.6 = (bf16[2048,384]{1,0:T(8,128)(2,1)S(1)}, bf16[2048,384]{1,0:T(8,128)(2,1)S(1)}, u32[]{:S(2)}, u32[]{:S(2)}) collective-permute-start(bf16[2048,384]{1,0:T(8,128)(2,1)S(1)} %bitcast.42), channel_id=1, source_target_pairs={{0,128},{1,129},{2,130},{3,131},{4,132},{5,133},{6,134},{7,135},{8... | collective-permute-start | bytes 4718600 | tf_op jit(solution)/shard_map/ppermute | solution.py:405
  40.1 11.7 %collective-permute-start.7 = (bf16[2048,384]{1,0:T(8,128)(2,1)S(1)}, bf16[2048,384]{1,0:T(8,128)(2,1)S(1)}, u32[]{:S(2)}, u32[]{:S(2)}) collective-permute-start(bf16[2048,384]{1,0:T(8,128)(2,1)S(1)} %bitcast.48), channel_id=1, source_target_pairs={{0,128},{1,129},{2,130},{3,131},{4,132},{5,133},{6,134},{7,135},{8... | collective-permute-start | bytes 4718600 | tf_op jit(solution)/shard_map/ppermute | solution.py:405
  41.4 12.8 %collective-permute-start.8 = (bf16[384,2048]{1,0:T(8,128)(2,1)}, bf16[384,2048]{1,0:T(8,128)(2,1)S(1)}, u32[]{:S(2)}, u32[]{:S(2)}) collective-permute-start(bf16[384,2048]{1,0:T(8,128)(2,1)} %bitcast.51), channel_id=1, source_target_pairs={{0,128},{1,129},{2,130},{3,131},{4,132},{5,133},{6,134},{7,135},{8... | collective-permute-start | bytes 4718600 | tf_op jit(solution)/shard_map/ppermute | solution.py:405
  49.5 2.3 copy-start.2
  51.8 2.5 %copy-start.3 = (bf16[2048,384]{1,0:T(8,128)(2,1)}, bf16[2048,384]{1,0:T(8,128)(2,1)S(1)}, u32[]{:S(2)}) copy-start(bf16[2048,384]{1,0:T(8,128)(2,1)S(1)} %collective-permute-done.7.refs_4_.other_up) | copy-start | bytes 4718596
  54.2 1.2 copy-start.4
  150.6 32.8 %all-to-all-start.2 = ((bf16[128,2,16,128]{3,2,1,0:T(8,128)(2,1)}), bf16[128,2,16,128]{3,2,1,0:T(8,128)(2,1)}, u32[]{:S(2)}, u32[]{:S(2)}) async-start(bf16[128,2,16,128]{3,2,1,0:T(8,128)(2,1)} %bitcast.57), calls=%async_computation.2 | async-start | bytes 2097152 | tf_op jit(solution)/shard_map/all_to_all | solution.py:334
  189.8 9.4 %copy-start.5 = (bf16[256,2048]{1,0:T(8,128)(2,1)S(1)}, bf16[256,2048]{1,0:T(8,128)(2,1)}, u32[]{:S(2)}) copy-start(bf16[256,2048]{1,0:T(8,128)(2,1)} %get-tuple-element.53) | copy-start | bytes 3145732
  189.8 9.4 %copy-start.6 = (bf16[256,2048]{1,0:T(8,128)(2,1)S(1)}, bf16[256,2048]{1,0:T(8,128)(2,1)}, u32[]{:S(2)}) copy-start(bf16[256,2048]{1,0:T(8,128)(2,1)} %get-tuple-element.54) | copy-start | bytes 3145732
  189.8 32.1 %all-to-all-start.3 = ((bf16[128,2,16,128]{3,2,1,0:T(8,128)(2,1)}), bf16[128,2,16,128]{3,2,1,0:T(8,128)(2,1)}, u32[]{:S(2)}, u32[]{:S(2)}) async-start(bf16[128,2,16,128]{3,2,1,0:T(8,128)(2,1)} %bitcast.56), calls=%async_computation.3 | async-start | bytes 2097152 | tf_op jit(solution)/shard_map/all_to_all | solution.py:334
  199.2 7.0 %copy-start.8 = (bf16[1,1,384,384]{3,2,1,0:T(8,128)(2,1)S(1)}, bf16[1,1,384,384]{3,2,1,0:T(8,128)(2,1)}, u32[]{:S(2)}) copy-start(bf16[1,1,384,384]{3,2,1,0:T(8,128)(2,1)} %param.15) | copy-start | bytes 884740
  199.3 9.7 %copy-start.9 = (bf16[256,384]{1,0:T(8,128)(2,1)S(1)}, bf16[256,384]{1,0:T(8,128)(2,1)}, u32[]{:S(2)}) copy-start(bf16[256,384]{1,0:T(8,128)(2,1)} %get-tuple-element.52) | copy-start | bytes 589828
  199.3 9.9 %copy-start.14 = (bf16[256,384]{1,0:T(8,128)(2,1)S(1)}, bf16[256,384]{1,0:T(8,128)(2,1)}, u32[]{:S(2)}) copy-start(bf16[256,384]{1,0:T(8,128)(2,1)} %get-tuple-element.51) | copy-start | bytes 589828
  199.4 11.6 %collective-permute-start.11 = (bf16[256,2048]{1,0:T(8,128)(2,1)S(1)}, bf16[256,2048]{1,0:T(8,128)(2,1)S(1)}, u32[]{:S(2)}, u32[]{:S(2)}) collective-permute-start(bf16[256,2048]{1,0:T(8,128)(2,1)S(1)} %get-tuple-element.62), channel_id=1, source_target_pairs={{0,128},{128,0},{1,129},{129,1},{2,130},{130,2},{3,131},{131,3},{4... | collective-permute-start | bytes 3145736 | tf_op jit(solution)/shard_map/ppermute | solution.py:330
  206.2 2.7 %collective-permute-start.9 = (bf16[384,384]{1,0:T(8,128)(2,1)S(1)}, bf16[384,384]{1,0:T(8,128)(2,1)S(1)}, u32[]{:S(2)}, u32[]{:S(2)}) collective-permute-start(bf16[384,384]{1,0:T(8,128)(2,1)S(1)} %bitcast.59), channel_id=1, source_target_pairs={{0,128},{128,0},{1,129},{129,1},{2,130},{130,2},{3,131},{131,3},{4... | collective-permute-start | bytes 884744 | tf_op jit(solution)/shard_map/ppermute | solution.py:330
  209.5 1.5 collective-permute-start.10
  224.7 10.5 %collective-permute-start.12 = (bf16[64,2048]{1,0:T(8,128)(2,1)}, bf16[64,2048]{1,0:T(8,128)(2,1)S(1)}, u32[]{:S(2)}, u32[]{:S(2)}) collective-permute-start(bf16[64,2048]{1,0:T(8,128)(2,1)} %get-tuple-element.57), channel_id=1, source_target_pairs={{0,128},{128,0},{1,129},{129,1},{2,130},{130,2},{3,131},{131,3},{4... | collective-permute-start | bytes 786440 | tf_op jit(solution)/shard_map/ppermute | solution.py:330

commit v3 on v1

v3 whole, which is shorter than its diff:
```python
import functools
import jax
import jax.numpy as jnp
import numpy as np
from jax import lax
from jax.experimental import pallas as pl
from jax.experimental.pallas import tpu as pltpu
from jax.sharding import PartitionSpec as P

LANES = 128
CAP = 2
F32 = jnp.float32
BF16 = jnp.bfloat16
SMEM = pl.BlockSpec(memory_space=pltpu.SMEM)
VMEM = pl.BlockSpec(memory_space=pltpu.VMEM)
HBM = pl.BlockSpec(memory_space=pltpu.HBM)


def rows_to_tiles(rows, tiles, count, depth):
    for j in range(depth):
        tiles[pl.ds(j, count, stride=depth), :] = rows[:, j * LANES : (j + 1) * LANES]


def tile_columns(tiles, first, number, count, depth):
    return jnp.concatenate(
        [tiles[pl.ds(j, count, stride=depth), :] for j in range(first, first + number)], axis=1
    ).astype(BF16)


def clear(send, experts):
    zero = jnp.zeros(send.shape[1:], send.dtype)

    def one(e, carry):
        send[e] = zero
        return carry

    lax.fori_loop(0, experts, one, 0, unroll=8)


def on_core(which):
    return lax.axis_index("segment") == which


def fetch(source, target, sem):
    copy = pltpu.make_async_copy(source, target, sem)
    copy.start()
    return copy


def fetch_one_of(first, own, other, target, sem):
    @pl.when(first)
    def _():
        pltpu.make_async_copy(own, target, sem).start()

    @pl.when(jnp.logical_not(first))
    def _():
        pltpu.make_async_copy(other, target, sem).start()

    return pltpu.make_async_copy(own, target, sem)


def slot_reader(own_slots, other_slots):
    segment = lax.axis_index("segment")

    def slot(layer, k, t):
        mine, theirs = own_slots[segment, k, t], other_slots[segment, k, t]
        return jnp.where(segment == layer, mine, theirs)

    return slot


def dispatch_kernel(
    own_slots, other_slots, own_w, other_w, own_x, other_x, grads, after, sent, tiles_out,
    send, grad_tiles, own, other, grad, x_upper, x_lower, g_tiles, sems,
):
    tokens, width = grad.shape
    depth = width // LANES
    segment = lax.axis_index("segment")
    upper = segment == 1
    slot = slot_reader(own_slots, other_slots)
    copies = [
        fetch(own_x.at[segment], own, sems.at[0]),
        fetch(other_x, other, sems.at[1]),
        fetch(grads.at[segment], grad, sems.at[2]),
    ]
    clear(send, send.shape[0])
    for copy in copies:
        copy.wait()
    mine, theirs = own[...].astype(F32), other[...].astype(F32)
    rows_to_tiles(jnp.where(upper, mine, theirs), x_upper, tokens, depth)
    saves = []

    def part(n):
        here = slice(n * CAP, (n + 1) * CAP)
        saves.append(fetch(send.at[:, here], sent.at[:, here], sems.at[3 + n]))

    def first(t, carry):
        row = x_upper[pl.ds(pl.multiple_of(t * depth, depth), depth), :].astype(BF16)
        for k in range(2):
            s = slot(1, k, t)
            send[s >> 1, s & 1] = row
        return carry

    lax.fori_loop(0, tokens, first, 0, unroll=4)
    part(0)
    rows_to_tiles(grad[...].astype(F32), g_tiles, tokens, depth)

    def second(t, carry):
        g = g_tiles[pl.ds(pl.multiple_of(t * depth, depth), depth), :]
        grad_tiles[t] = g.astype(BF16)
        for k in range(2):
            s = slot(1, k, t)
            weight = jnp.where(upper, own_w[segment, k, t], other_w[segment, k, t])
            send[s >> 1, CAP + (s & 1)] = (weight * g).astype(BF16)
        return carry

    lax.fori_loop(0, tokens, second, 0, unroll=4)
    part(1)
    saves.append(fetch(grad_tiles, tiles_out, sems.at[6]))
    rows_to_tiles(jnp.where(upper, theirs, mine), x_lower, tokens, depth)

    def third(t, carry):
        row = x_lower[pl.ds(pl.multiple_of(t * depth, depth), depth), :].astype(BF16)
        for k in range(2):
            s = slot(0, k, t)
            send[s >> 1, 2 * CAP + (s & 1)] = row
        return carry

    lax.fori_loop(0, tokens, third, 0, unroll=4)
    part(2)
    for copy in saves:
        copy.wait()


def relay_kernel(
    own_slots, other_slots, own_w, other_w, back, upstream, sent, grad_out, send, sems
):
    tokens = upstream.shape[0]
    segment = lax.axis_index("segment")
    upper = segment == 1
    slot = slot_reader(own_slots, other_slots)
    clear(send, send.shape[0])

    def token(t, carry):
        total = upstream[t].astype(F32)
        for k in range(2):
            total = total + back[slot(1, k, t)].astype(F32)
        rounded = total.astype(BF16)
        grad_out[t] = rounded
        g = rounded.astype(F32)
        for k in range(2):
            weight = jnp.where(upper, other_w[segment, k, t], own_w[segment, k, t])
            send[slot(0, k, t)] = (weight * g).astype(BF16)
        return carry

    lax.fori_loop(0, tokens, token, 0, unroll=4)
    fetch(send, sent, sems.at[0]).wait()


def finish_kernel(own_slots, other_slots, back, upstream, keep, away, low, up):
    tokens, depth = upstream.shape[0], upstream.shape[1]
    upper = on_core(1)
    slot = slot_reader(own_slots, other_slots)

    def token(t, carry):
        at = pl.ds(pl.multiple_of(t * depth, depth), depth)
        g = upstream[t].astype(F32)
        up[at, :] = g
        total = g
        for k in range(2):
            total = total + back[slot(0, k, t)].astype(F32)
        low[at, :] = total
        return carry

    lax.fori_loop(0, tokens, token, 0, unroll=4)
    for j in range(depth):
        columns = slice(j * LANES, (j + 1) * LANES)
        high = up[pl.ds(j, tokens, stride=depth), :]
        down = low[pl.ds(j, tokens, stride=depth), :]
        keep[:, columns] = jnp.where(upper, high, down).astype(BF16)
        away[:, columns] = jnp.where(upper, down, high).astype(BF16)


def join_kernel(keep, came, out, sems):
    segment = lax.axis_index("segment")
    copies = [
        fetch(keep, out.at[segment], sems.at[0]),
        fetch(came, out.at[1 - segment], sems.at[1]),
    ]
    for copy in copies:
        copy.wait()


def turn_kernel(turn, gate, up, down, *refs):
    gate_up_t, down_t, a, b, c, turned, turned_down, sems = refs[-8:]
    hidden, width = down.shape
    step = 256

    def work():
        copies = [
            fetch(gate, a, sems.at[0]), fetch(up, b, sems.at[1]), fetch(down, c, sems.at[2])
        ]
        for n, block in enumerate((a, b)):
            copies[n].wait()
            for i in range(0, width, step):
                turned[n * hidden : (n + 1) * hidden, i : i + step] = block[i : i + step, :].T
        first = fetch(turned, gate_up_t, sems.at[3])
        copies[2].wait()
        for i in range(0, width, step):
            turned_down[i : i + step, :] = c[:, i : i + step].T
        fetch(turned_down, down_t, sems.at[4]).wait()
        first.wait()

    if turn is None:
        work()
    else:
        pl.when(on_core(turn))(work)


def forward_parts(tiles, gate, up, count, depth):
    number = depth // 2
    hidden_gate = hidden_up = 0.0
    for first in range(0, depth, number):
        rows = tile_columns(tiles, first, number, count, depth)
        here = slice(first * LANES, (first + number) * LANES)
        hidden_gate += jnp.dot(rows, gate[here, :], preferred_element_type=F32)
        hidden_up += jnp.dot(rows, up[here, :], preferred_element_type=F32)
    sigma = 1.0 / (1.0 + jnp.exp(-hidden_gate))
    act = hidden_gate * sigma
    dact = sigma * (1.0 + hidden_gate * (1.0 - sigma))
    return act, hidden_up * dact, (act * hidden_up).astype(BF16)


def down_part(tiles, dy_rows, down_t, depth):
    count = dy_rows.shape[0]
    number = depth // 2
    grad_act = 0.0
    for first in range(0, depth, number):
        rows = tile_columns(tiles, first, number, count, depth)
        here = slice(first * LANES, (first + number) * LANES)
        dy_rows[:, here] = rows
        grad_act += jnp.dot(rows, down_t[here, :], preferred_element_type=F32)
    return grad_act


def back_part(grad_act, act, slope, gate_up_t, tiles, send, sent, sems):
    count, depth, lanes = send.shape
    both = jnp.concatenate(
        [(grad_act * slope).astype(BF16), (grad_act * act).astype(BF16)], axis=1
    )
    number = depth // 4
    for first in range(0, depth, number):
        here = slice(first * LANES, (first + number) * LANES)
        dx = jnp.dot(both, gate_up_t[:, here], preferred_element_type=F32)
        for j in range(number):
            tiles[pl.ds(first + j, count, stride=depth), :] = dx[:, j * LANES : (j + 1) * LANES]
    pieces, copies = 4, []
    part = count // pieces
    for n in range(pieces):
        rows = tiles[n * part * depth : (n + 1) * part * depth, :]
        send[n * part : (n + 1) * part] = rows.reshape(part, depth, lanes).astype(BF16)
        here = pl.ds(n * part, part)
        copies.append(fetch(send.at[here], sent.at[here], sems.at[n]))
    return copies


def widened(block, tiles):
    tiles[...] = block[...].astype(F32).reshape(tiles.shape)


def upper_kernel(
    arrived, own_gate, other_gate, own_up, other_up, own_dt, other_dt, own_gut, other_gut,
    sent, dy_out, act_out,
    x, dy, gate, up, down_t, gate_up_t, x_tiles, dy_tiles, dx_tiles, dy_rows, activ, send, sems,
):
    mine = on_core(1)
    count, depth = send.shape[:2]
    x_copy = fetch(arrived.at[:, :CAP], x, sems.at[0])
    gate_copy = fetch_one_of(mine, own_gate, other_gate, gate, sems.at[1])
    up_copy = fetch_one_of(mine, own_up, other_up, up, sems.at[2])
    dy_copy = fetch(arrived.at[:, CAP : 2 * CAP], dy, sems.at[3])
    down_copy = fetch_one_of(mine, own_dt, other_dt, down_t, sems.at[4])
    back_copy = fetch_one_of(mine, own_gut, other_gut, gate_up_t, sems.at[5])
    x_copy.wait()
    widened(x, x_tiles)
    for copy in (gate_copy, up_copy, dy_copy, down_copy, back_copy):
        copy.wait()
    widened(dy, dy_tiles)
    act, slope, rounded = forward_parts(x_tiles, gate, up, count, depth)
    activ[...] = rounded
    grad_act = down_part(dy_tiles, dy_rows, down_t, depth)
    saves = [fetch(activ, act_out, sems.at[6]), fetch(dy_rows, dy_out, sems.at[7])]
    saves += back_part(
        grad_act, act, slope, gate_up_t, dx_tiles, send, sent, sems.at[pl.ds(8, 4)]
    )
    for copy in saves:
        copy.wait()


def forward_kernel(
    arrived, own_gate, other_gate, own_up, other_up, act_out, slope_out, activ_out,
    x, gate, up, tiles, sems,
):
    mine = on_core(0)
    experts, cap, depth = x.shape[:3]
    x_copy = fetch(arrived.at[:, 2 * CAP :], x, sems.at[0])
    gate_copy = fetch_one_of(mine, own_gate, other_gate, gate, sems.at[1])
    up_copy = fetch_one_of(mine, own_up, other_up, up, sems.at[2])
    x_copy.wait()
    widened(x, tiles)
    gate_copy.wait()
    up_copy.wait()
    act, slope, rounded = forward_parts(tiles, gate, up, experts * cap, depth)
    act_out[...] = act
    slope_out[...] = slope
    activ_out[...] = rounded


def lower_kernel(
    dy_in, act_in, slope_in, own_dt, other_dt, own_gut, other_gut, sent, dy_out,
    dy, act, slope, down_t, gate_up_t, dy_tiles, dx_tiles, dy_rows, send, sems,
):
    mine = on_core(0)
    count, depth = send.shape[:2]
    pieces = 4
    part = count // pieces
    arriving = [
        fetch(dy_in.at[pl.ds(n * part, part)], dy.at[pl.ds(n * part, part)], sems.at[9 + n])
        for n in range(pieces)
    ]
    down_copy = fetch_one_of(mine, own_dt, other_dt, down_t, sems.at[0])
    act_copy = fetch(act_in, act, sems.at[1])
    slope_copy = fetch(slope_in, slope, sems.at[2])
    back_copy = fetch_one_of(mine, own_gut, other_gut, gate_up_t, sems.at[3])
    for n, copy in enumerate(arriving):
        copy.wait()
        dy_tiles[n * part * depth : (n + 1) * part * depth, :] = (
            dy[n * part : (n + 1) * part].astype(F32).reshape(part * depth, LANES)
        )
    for copy in (down_copy, act_copy, slope_copy, back_copy):
        copy.wait()
    grad_act = down_part(dy_tiles, dy_rows, down_t, depth)
    saves = [fetch(dy_rows, dy_out, sems.at[4])]
    saves += back_part(
        grad_act, act[...], slope[...], gate_up_t, dx_tiles, send, sent, sems.at[pl.ds(5, 4)]
    )
    for copy in saves:
        copy.wait()


def call(kernel, args, in_specs, out_shape, out_specs, scratch, flops, moved, aliases={}):
    return pl.pallas_call(
        kernel,
        in_specs=in_specs,
        out_shape=out_shape,
        out_specs=out_specs,
        scratch_shapes=scratch,
        input_output_aliases=aliases,
        compiler_params=pltpu.CompilerParams(vmem_limit_bytes=63 * 1024 * 1024),
        cost_estimate=pl.CostEstimate(flops=flops, bytes_accessed=moved, transcendentals=0),
    )(*args)


def swapped(block):
    return lax.ppermute(block, "segment", [(0, 1), (1, 0)])


def exchanged(block):
    return lax.all_to_all(block, "expert", split_axis=0, concat_axis=0, tiled=True)


def shape(dims, kind=BF16):
    return jax.ShapeDtypeStruct(dims, kind)


def shards(saved_input, out_grad, expert_ids, router_weights, w_gate, w_up, w_down, eigenbasis):
    experts = lax.axis_size("expert")
    segment = lax.axis_index("segment")
    upper = segment == 1
    micros, tokens, width = saved_input.shape[1:]
    hidden = w_gate.shape[-1]
    depth = width // LANES
    count = experts * CAP
    gate, up, down, basis = w_gate[0, 0], w_up[0, 0], w_down[0, 0], eigenbasis[0, 0]

    other_x = swapped(
        lax.dynamic_index_in_dim(saved_input[0], 1 - segment, 0, keepdims=False)
    )
    ids = jnp.swapaxes(expert_ids[0], 1, 2)
    own_w = jnp.swapaxes(router_weights[0], 1, 2)
    order = 2 * np.arange(tokens)[None, :] + np.arange(2)[:, None]
    earlier = order[None, None] < order[..., None, None]
    same = ids[:, None, None] == ids[..., None, None]
    rank = jnp.sum((same & earlier[None]).astype(jnp.int32), axis=(3, 4))
    own_slots = ids * CAP + jnp.minimum(rank, CAP - 1)
    other_slots, other_w = swapped(own_slots), swapped(own_w)

    matrix = pltpu.VMEM((width, hidden), BF16)
    turned_shapes = (shape((2 * hidden, width)), shape((width, hidden)))
    turn_scratch = [
        matrix, matrix, pltpu.VMEM((hidden, width), BF16), pltpu.VMEM((2 * hidden, width), BF16),
        matrix, pltpu.SemaphoreType.DMA((5,)),
    ]

    def turned(turn, matrices, made=()):
        return call(
            functools.partial(turn_kernel, turn),
            (*matrices, *made),
            [HBM] * (3 + len(made)),
            turned_shapes,
            (HBM,) * 2,
            turn_scratch,
            1_000_000,
            9_000_000,
            {3: 0, 4: 1} if made else {},
        )

    early_gut, early_dt = turned(0, (gate, up, down))

    tile_rows = tokens * depth
    row_block = pltpu.VMEM((tokens, width), BF16)
    send, grad_tiles = call(
        dispatch_kernel,
        (own_slots, other_slots, own_w, other_w, saved_input[0], other_x, out_grad, early_dt),
        [SMEM] * 4 + [HBM] * 4,
        (shape((experts, 3 * CAP, depth, LANES)), shape((tokens, depth, LANES))),
        (HBM,) * 2,
        [
            pltpu.VMEM((experts, 3 * CAP, depth, LANES), BF16),
            pltpu.VMEM((tokens, depth, LANES), BF16),
        ]
        + [row_block] * 3
        + [pltpu.VMEM((tile_rows, LANES), F32)] * 3
        + [pltpu.SemaphoreType.DMA((7,))],
        1_000_000,
        5_000_000,
    )
    arrived = exchanged(send)

    own_gut, own_dt = turned(1, (gate, up, down), (early_gut, early_dt))
    other_gate, other_up, other_down = swapped(gate), swapped(up), swapped(down)
    other_basis = swapped(basis)
    other_gut, other_dt = turned(None, (other_gate, other_up, other_down))

    tiles = pltpu.VMEM((count * depth, LANES), F32)
    rows = pltpu.VMEM((count, width), BF16)
    part = pltpu.VMEM((experts, CAP, depth, LANES), BF16)
    flat = (count, depth, LANES)
    flat_scratch = pltpu.VMEM(flat, BF16)
    mat = 2 * count * width * hidden
    back_send, dy_rows1, activ1 = call(
        upper_kernel,
        (arrived, gate, other_gate, up, other_up, own_dt, other_dt, own_gut, other_gut),
        [HBM] * 9,
        (shape(flat), shape((count, width)), shape((count, hidden))),
        (HBM,) * 3,
        [
            part, part, matrix, matrix, matrix, pltpu.VMEM((2 * hidden, width), BF16), tiles,
            tiles, tiles, rows, pltpu.VMEM((count, hidden), BF16), flat_scratch,
            pltpu.SemaphoreType.DMA((12,)),
        ],
        5 * mat,
        9_000_000,
    )

    def returned(block):
        return exchanged(block.reshape(experts, CAP, depth, LANES)).reshape(flat)

    back = returned(back_send)
    act0, slope0, activ0 = call(
        forward_kernel,
        (arrived, gate, other_gate, up, other_up),
        [HBM] * 5,
        (shape((count, hidden), F32), shape((count, hidden), F32), shape((count, hidden))),
        (VMEM,) * 3,
        [part, matrix, matrix, tiles, pltpu.SemaphoreType.DMA((3,))],
        2 * mat,
        5_000_000,
    )
    basis1 = jnp.where(upper, basis, other_basis)
    basis0 = jnp.where(upper, other_basis, basis)
    rotated1 = jnp.dot(activ1, basis1, preferred_element_type=F32).astype(BF16)
    rotated0 = jnp.dot(activ0, basis0, preferred_element_type=F32).astype(BF16)

    dy_send, grad1 = call(
        relay_kernel,
        (own_slots, other_slots, own_w, other_w, back, grad_tiles),
        [SMEM] * 4 + [VMEM] * 2,
        (shape(flat), shape((tokens, depth, LANES))),
        (HBM, VMEM),
        [flat_scratch, pltpu.SemaphoreType.DMA((1,))],
        1_000_000,
        3_000_000,
    )
    dy = returned(dy_send)
    back_send0, dy_rows0 = call(
        lower_kernel,
        (dy, act0, slope0, own_dt, other_dt, own_gut, other_gut),
        [HBM] * 7,
        (shape(flat), shape((count, width))),
        (HBM,) * 2,
        [
            flat_scratch, pltpu.VMEM((count, hidden), F32), pltpu.VMEM((count, hidden), F32),
            matrix, pltpu.VMEM((2 * hidden, width), BF16), tiles, tiles, rows, flat_scratch,
            pltpu.SemaphoreType.DMA((13,)),
        ],
        3 * mat,
        8_000_000,
    )
    back0 = returned(back_send0)

    all_rotated = jnp.concatenate(
        [
            jnp.where(upper, rotated1, rotated0),
            swapped(jnp.where(upper, rotated0, rotated1)),
        ],
        axis=0,
    )
    all_dy = jnp.concatenate(
        [
            jnp.where(upper, dy_rows1, dy_rows0),
            swapped(jnp.where(upper, dy_rows0, dy_rows1)),
        ],
        axis=0,
    )
    rot_sq = (all_rotated.astype(F32) ** 2).astype(BF16)
    dy_sq = (all_dy.astype(F32) ** 2).astype(BF16)
    over_rows = (((0,), (0,)), ((), ()))
    grad_sum = lax.dot_general(all_rotated, all_dy, over_rows, preferred_element_type=F32)
    scale_sum = lax.dot_general(rot_sq, dy_sq, over_rows, preferred_element_type=F32)
    rotated_grad = (grad_sum * (1.0 / micros)).astype(BF16)
    ekfac_scales = scale_sum * (1.0 / micros)
    back0, rotated_grad, ekfac_scales = lax.optimization_barrier(
        (back0, rotated_grad, ekfac_scales)
    )

    keep, away = call(
        finish_kernel,
        (own_slots, other_slots, back0, grad1),
        [SMEM] * 2 + [VMEM] * 2,
        (shape((tokens, width)), shape((tokens, width))),
        (VMEM,) * 2,
        [pltpu.VMEM((tile_rows, LANES), F32)] * 2,
        1_000_000,
        2_000_000,
    )
    came = swapped(away)
    grads = call(
        join_kernel,
        (keep, came),
        [HBM] * 2,
        shape((micros, tokens, width)),
        HBM,
        [pltpu.SemaphoreType.DMA((2,))],
        0,
        1_000_000,
    )
    return (grads[None], rotated_grad[None, None], ekfac_scales[None, None])


def solution(mesh):
    in_specs = (
        P("segment", None, "expert", None),
        P(None, "expert", None),
        P("segment", None, "expert", None),
        P("segment", None, "expert", None),
        P("segment", "expert", None, None),
        P("segment", "expert", None, None),
        P("segment", "expert", None, None),
        P("segment", "expert", None, None),
    )
    out_specs = (
        P("segment", None, "expert", None),
        P("segment", "expert", None, None),
        P("segment", "expert", None, None),
    )
    return jax.shard_map(shards, mesh=mesh, in_specs=in_specs, out_specs=out_specs, check_vma=False)
```

time: 235 us -> 249 us (1.060)
  Pallas kernels: 41.2 us -> 58 us
  waiting for transfers between devices: 83.5 us -> 87.5 us
  local copies, waits for them, and re-layouts: 6.16 us -> 2.38 us
    pallas_call x9 -> x10, Pallas kernels: 41.2 us -> 58 us  [call(): pl.pallas_call(kernel, in_specs=in_specs, out_shape=out_shape, out_specs=...]
    all_to_all x3, waiting for transfers between devices: 75.7 us -> 78.7 us  [exchanged(): lax.all_to_all(block, 'expert', split_axis=0, concat_axis=0, tiled=True)]
    squeeze x4 -> x1, local copies, waits for them, and re-layouts: 3.68 us -> 0.97 us  [shards(): lax.dynamic_index_in_dim(saved_input[0], 1 - segment, 0, keepdims=False)]
  transfers between devices with their start and end apart: 13 -> 13, of which waited for: 8 -> 10; matrix products, arithmetic and copies ran while one was open for 5% -> 4% of each run, Pallas kernels for 6% -> 6%
where the time goes in v3:
time: 249 us
  waiting for transfers between devices  87.5 us (35%)
  Pallas kernels  58 us (23%)
  starting transfers between devices  55.5 us (22%)
  blocking collectives  35.6 us (14%)
  matrix products  5.42 us (2%)
  other arithmetic  3.39 us (1%)
    all_to_all x3, waiting for transfers between devices, exchanged(): lax.all_to_all(block, 'expert', split_axis=0, concat_axis=0, tiled=True)  78.7 us
    pallas_call x10, Pallas kernels, call(): pl.pallas_call(kernel, in_specs=in_specs, out_shape=out_shape, out_specs=...  58 us
    all_to_all x1, blocking collectives, exchanged(): lax.all_to_all(block, 'expert', split_axis=0, concat_axis=0, tiled=True)  35.6 us
    all_to_all x3, starting transfers between devices, exchanged(): lax.all_to_all(block, 'expert', split_axis=0, concat_axis=0, tiled=True)  33.1 us
    ppermute x10, starting transfers between devices, swapped(): return lax.ppermute(block, 'segment', [(0, 1), (1, 0)])  22.4 us
    ppermute x10, waiting for transfers between devices, swapped(): return lax.ppermute(block, 'segment', [(0, 1), (1, 0)])  8.78 us
  transfers between devices with their start and end apart: 13, of which 10 were waited for; matrix products, arithmetic and copies ran while one was open for 4% of the time, Pallas kernels for 6%

profile of v3, /device:TPU:1, one launch (start us, length us, event | category | flops | bytes accessed | tf_op | source)
XLA Modules:
  0.0 248.7 jit_solution(2431962701295549200)
XLA Ops:
  0.6 1.0 dynamic-slice_bitcast_fusion
  1.6 3.3 %collective-permute-start.2 = (bf16[64,2048]{1,0:T(8,128)(2,1)S(1)}, bf16[64,2048]{1,0:T(8,128)(2,1)S(1)}, u32[]{:S(2)}, u32[]{:S(2)}) collective-permute-start(bf16[64,2048]{1,0:T(8,128)(2,1)S(1)} %dynamic-slice_bitcast_fusion), channel_id=1, source_target_pairs={{0,128},{128,0},{1,129},{129,1},{2,130},{130,2},{3,131},{131,3},{4... | collective-permute-start | bytes 786440 | tf_op jit(solution)/shard_map/ppermute | solution.py:365
  4.9 1.0 convert_reduce_fusion
  6.0 0.7 minimum_add_fusion.own_slots
  7.2 0.6 collective-permute-done.other_slots
  8.9 5.6 %shard_map.113 = (bf16[128,6,16,128]{3,2,1,0:T(8,128)(2,1)}, bf16[64,16,128]{2,1,0:T(8,128)(2,1)}) custom-call(s32[2,2,64]{2,1,0:T(2,128)} %copy-done.4, s32[2,2,64]{2,1,0:T(2,128)} %copy-done.5, f32[2,2,64]{2,1,0:T(2,128)} %bitcast.46, f32[2,2,64]{2,1,0:T(2,128)} %copy-done.6, bf16[2,64,2048]{2,1,0:T(8,128)(2,1)} %bitcast.37, bf16[64,2048]{1,0:T(8,128)(2,1)} %copy-done.2, ...), custom_call_target="tpu_custom_call" | custom-call | flops 1000000 | bytes 5000000 | tf_op jit(solution)/shard_map/pallas_call | solution.py:352
  14.6 14.3 %all-to-all-start = ((bf16[128,6,16,128]{3,2,1,0:T(8,128)(2,1)}), bf16[128,6,16,128]{3,2,1,0:T(8,128)(2,1)}, u32[]{:S(2)}, u32[]{:S(2)}) async-start(bf16[128,6,16,128]{3,2,1,0:T(8,128)(2,1)} %get-tuple-element.27), calls=%async_computation | async-start | bytes 6291456 | tf_op jit(solution)/shard_map/all_to_all | solution.py:369
  28.8 4.1 %collective-permute-start.3 = (bf16[2048,384]{1,0:T(8,128)(2,1)}, bf16[2048,384]{1,0:T(8,128)(2,1)}, u32[]{:S(2)}, u32[]{:S(2)}) collective-permute-start(bf16[2048,384]{1,0:T(8,128)(2,1)} %bitcast.8.gate.own_gate), channel_id=1, source_target_pairs={{0,128},{128,0},{1,129},{129,1},{2,130},{130,2},{3,131},{131,3},{4... | collective-permute-start | bytes 4718600 | tf_op jit(solution)/shard_map/ppermute | solution.py:365
  33.4 4.6 %shard_map.114 = (bf16[768,2048]{1,0:T(8,128)(2,1)}, bf16[2048,384]{1,0:T(8,128)(2,1)}) custom-call(bf16[2048,384]{1,0:T(8,128)(2,1)} %bitcast.8.gate.own_gate, bf16[2048,384]{1,0:T(8,128)(2,1)} %bitcast.9.up.own_up, bf16[384,2048]{1,0:T(8,128)(2,1)} %bitcast.10.down, ...), custom_call_target="tpu_custom_call", output_to_operand_aliasing={{0}: (3, {}), {1}: (4, {})} | custom-call | flops 1000000 | bytes 9000000 | tf_op jit(solution)/shard_map/pallas_call | solution.py:352
  38.5 2.2 collective-permute-done.5.down
  40.8 4.6 %shard_map.115 = (bf16[768,2048]{1,0:T(8,128)(2,1)}, bf16[2048,384]{1,0:T(8,128)(2,1)}) custom-call(bf16[2048,384]{1,0:T(8,128)(2,1)} %collective-permute-done.3.gate.other_gate, bf16[2048,384]{1,0:T(8,128)(2,1)} %collective-permute-done.4.up.other_up, bf16[384,2048]{1,0:T(8,128)(2,1)} %collective-permute-done.5.down), custom_call_target="tpu_custom_call" | custom-call | flops 1000000 | bytes 9000000 | tf_op jit(solution)/shard_map/pallas_call | solution.py:352
  45.4 52.0 %all-to-all-done.arrived = bf16[128,6,16,128]{3,2,1,0:T(8,128)(2,1)} async-done(((bf16[128,6,16,128]{3,2,1,0:T(8,128)(2,1)}), bf16[128,6,16,128]{3,2,1,0:T(8,128)(2,1)}, u32[]{:S(2)}, u32[]{:S(2)}) %all-to-all-start) | async-done | bytes 3145760 | tf_op jit(solution)/shard_map/all_to_all | solution.py:369
  97.4 8.7 %shard_map.116 = (bf16[256,16,128]{2,1,0:T(8,128)(2,1)}, bf16[256,2048]{1,0:T(8,128)(2,1)}, bf16[256,384]{1,0:T(8,128)(2,1)}) custom-call(bf16[128,6,16,128]{3,2,1,0:T(8,128)(2,1)} %all-to-all-done.arrived, bf16[2048,384]{1,0:T(8,128)(2,1)} %bitcast.8.gate.own_gate, bf16[2048,384]{1,0:T(8,128)(2,1)} %collective-permute-done.3.gate.other_gate, ...), custom_call_target="tpu_custom_call" | custom-call | flops 2013265920 | bytes 9000000 | tf_op jit(solution)/shard_map/pallas_call | solution.py:352
  106.0 35.6 %all_to_all.20 = bf16[128,2,16,128]{3,2,1,0:T(8,128)(2,1)} all-to-all(bf16[128,2,16,128]{3,2,1,0:T(8,128)(2,1)} %bitcast.40), channel_id=1, replica_groups=mesh['segment'=2,'expert'=128] {'expert'}, dimensions={0} | all-to-all | bytes 2097152 | tf_op jit(solution)/shard_map/all_to_all | solution.py:369
  141.6 3.9 %shard_map.117 = (bf16[256,16,128]{2,1,0:T(8,128)(2,1)}, bf16[64,16,128]{2,1,0:T(8,128)(2,1)}) custom-call(s32[2,2,64]{2,1,0:T(2,128)} %copy-done.4, s32[2,2,64]{2,1,0:T(2,128)} %copy-done.5, f32[2,2,64]{2,1,0:T(2,128)} %bitcast.47, f32[2,2,64]{2,1,0:T(2,128)} %copy-done.6, bf16[256,16,128]{2,1,0:T(8,128)(2,1)} %bitcast.36, ...), custom_call_target="tpu_custom_call" | custom-call | flops 1000000 | bytes 3000000 | tf_op jit(solution)/shard_map/pallas_call | solution.py:352
  145.5 9.5 %all-to-all-start.2 = ((bf16[128,2,16,128]{3,2,1,0:T(8,128)(2,1)}), bf16[128,2,16,128]{3,2,1,0:T(8,128)(2,1)}, u32[]{:S(2)}, u32[]{:S(2)}) async-start(bf16[128,2,16,128]{3,2,1,0:T(8,128)(2,1)} %bitcast.39), calls=%async_computation.2 | async-start | bytes 2097152 | tf_op jit(solution)/shard_map/all_to_all | solution.py:369
  155.0 4.5 %shard_map.118 = (f32[256,384]{1,0:T(8,128)}, f32[256,384]{1,0:T(8,128)}, bf16[256,384]{1,0:T(8,128)(2,1)}) custom-call(bf16[128,6,16,128]{3,2,1,0:T(8,128)(2,1)} %all-to-all-done.arrived, bf16[2048,384]{1,0:T(8,128)(2,1)} %bitcast.8.gate.own_gate, bf16[2048,384]{1,0:T(8,128)(2,1)} %collective-permute-done.3.gate.other_gate, ...), custom_call_target="tpu_custom_call" | custom-call | flops 805306368 | bytes 5000000 | tf_op jit(solution)/shard_map/pallas_call | solution.py:352
  159.5 19.7 %all-to-all-done.2 = bf16[128,2,16,128]{3,2,1,0:T(8,128)(2,1)} async-done(((bf16[128,2,16,128]{3,2,1,0:T(8,128)(2,1)}), bf16[128,2,16,128]{3,2,1,0:T(8,128)(2,1)}, u32[]{:S(2)}, u32[]{:S(2)}) %all-to-all-start.2) | async-done | bytes 1048608 | tf_op jit(solution)/shard_map/all_to_all | solution.py:369
  179.2 6.1 %shard_map.119 = (bf16[256,16,128]{2,1,0:T(8,128)(2,1)}, bf16[256,2048]{1,0:T(8,128)(2,1)}) custom-call(bf16[256,16,128]{2,1,0:T(8,128)(2,1)} %bitcast.14.dy_in, f32[256,384]{1,0:T(8,128)} %get-tuple-element.36.act_in, f32[256,384]{1,0:T(8,128)} %get-tuple-element.37.slope_in, bf16[2048,384]{1,0:T(8,128)(2,1)} %get-tuple-element.29.own_dt, ...), custom_call_target="tpu_custom_call" | custom-call | flops 1207959552 | bytes 8000000 | tf_op jit(solution)/shard_map/pallas_call | solution.py:352
  185.4 9.3 %all-to-all-start.3 = ((bf16[128,2,16,128]{3,2,1,0:T(8,128)(2,1)}), bf16[128,2,16,128]{3,2,1,0:T(8,128)(2,1)}, u32[]{:S(2)}, u32[]{:S(2)}) async-start(bf16[128,2,16,128]{3,2,1,0:T(8,128)(2,1)} %bitcast.38), calls=%async_computation.3 | async-start | bytes 2097152 | tf_op jit(solution)/shard_map/all_to_all | solution.py:369
  194.8 1.7 broadcast_select_fusion.1
  196.4 5.5 %collective-permute-start.8 = (bf16[256,2048]{1,0:T(8,128)(2,1)S(1)}, bf16[256,2048]{1,0:T(8,128)(2,1)S(1)}, u32[]{:S(2)}, u32[]{:S(2)}) collective-permute-start(bf16[256,2048]{1,0:T(8,128)(2,1)S(1)} %get-tuple-element.50), channel_id=1, source_target_pairs={{0,128},{128,0},{1,129},{129,1},{2,130},{130,2},{3,131},{131,3},{4... | collective-permute-start | bytes 3145736 | tf_op jit(solution)/shard_map/ppermute | solution.py:365
  202.1 2.6 %collective-permute-done.6 = bf16[384,384]{1,0:T(8,128)(2,1)S(1)} collective-permute-done((bf16[384,384]{1,0:T(8,128)(2,1)S(1)}, bf16[384,384]{1,0:T(8,128)(2,1)S(1)}, u32[]{:S(2)}, u32[]{:S(2)}) %collective-permute-start.6) | collective-permute-done | bytes 294944 | tf_op jit(solution)/shard_map/ppermute | solution.py:365
  205.7 1.1 collective-permute-done.7
  206.8 2.2 multiply_convert_fusion.1
  209.0 2.7 %convolution_multiply_fusion = f32[384,2048]{1,0:T(8,128)} fusion(bf16[256,2048]{1,0:T(8,128)(2,1)S(1)} %collective-permute-done.8, bf16[256,2048]{1,0:T(8,128)(2,1)S(1)} %get-tuple-element.49, bf16[256,384]{1,0:T(8,128)(2,1)S(1)} %collective-permute-done.7, bf16[256,384]{1,0:T(8,128)(2,1)S(1)} %get-tuple-element.51), kind=kOutput, calls=%fused_computation.2 | convolution fusion | flops 813563904 | bytes 5636096 | tf_op jit(solution)/shard_map/dot_general | solution.py:530
  211.7 7.0 %all-to-all-done.3 = bf16[128,2,16,128]{3,2,1,0:T(8,128)(2,1)} async-done(((bf16[128,2,16,128]{3,2,1,0:T(8,128)(2,1)}), bf16[128,2,16,128]{3,2,1,0:T(8,128)(2,1)}, u32[]{:S(2)}, u32[]{:S(2)}) %all-to-all-start.3) | async-done | bytes 1048608 | tf_op jit(solution)/shard_map/all_to_all | solution.py:369
  218.7 2.9 %shard_map.120 = (bf16[64,2048]{1,0:T(8,128)(2,1)}, bf16[64,2048]{1,0:T(8,128)(2,1)}) custom-call(s32[2,2,64]{2,1,0:T(2,128)} %copy-done.4, s32[2,2,64]{2,1,0:T(2,128)} %copy-done.5, bf16[256,16,128]{2,1,0:T(8,128)(2,1)} %bitcast.16.back, bf16[64,16,128]{2,1,0:T(8,128)(2,1)} %get-tuple-element.44.upstream), custom_call_target="tpu_custom_call" | custom-call | flops 1000000 | bytes 2000000 | tf_op jit(solution)/shard_map/pallas_call | solution.py:352
  221.6 7.9 %collective-permute-start.9 = (bf16[64,2048]{1,0:T(8,128)(2,1)}, bf16[64,2048]{1,0:T(8,128)(2,1)S(1)}, u32[]{:S(2)}, u32[]{:S(2)}) collective-permute-start(bf16[64,2048]{1,0:T(8,128)(2,1)} %get-tuple-element.46), channel_id=1, source_target_pairs={{0,128},{128,0},{1,129},{129,1},{2,130},{130,2},{3,131},{131,3},{4... | collective-permute-start | bytes 786440 | tf_op jit(solution)/shard_map/ppermute | solution.py:365
  229.5 1.4 collective-permute-done.9.came
  230.9 0.7 copy-done.1
  231.6 17.0 %shard_map.121 = bf16[2,64,2048]{2,1,0:T(8,128)(2,1)} custom-call(bf16[64,2048]{1,0:T(8,128)(2,1)} %get-tuple-element.45.keep, bf16[64,2048]{1,0:T(8,128)(2,1)} %copy-done.1), custom_call_target="tpu_custom_call" | custom-call | bytes 1000000 | tf_op jit(solution)/shard_map/pallas_call | solution.py:352
  (29 shorter events, 3.8 us)
Async XLA Ops:
  1.6 6.6 %collective-permute-start.2 = (bf16[64,2048]{1,0:T(8,128)(2,1)S(1)}, bf16[64,2048]{1,0:T(8,128)(2,1)S(1)}, u32[]{:S(2)}, u32[]{:S(2)}) collective-permute-start(bf16[64,2048]{1,0:T(8,128)(2,1)S(1)} %dynamic-slice_bitcast_fusion), channel_id=1, source_target_pairs={{0,128},{128,0},{1,129},{129,1},{2,130},{130,2},{3,131},{131,3},{4... | collective-permute-start | bytes 786440 | tf_op jit(solution)/shard_map/ppermute | solution.py:365
  6.6 1.6 copy-start.4
  6.7 1.2 collective-permute-start
  6.7 1.5 collective-permute-start.1
  7.8 0.6 copy-start.5
  8.2 0.6 copy-start.6
  8.2 0.7 copy-start.2
  14.6 82.8 %all-to-all-start = ((bf16[128,6,16,128]{3,2,1,0:T(8,128)(2,1)}), bf16[128,6,16,128]{3,2,1,0:T(8,128)(2,1)}, u32[]{:S(2)}, u32[]{:S(2)}) async-start(bf16[128,6,16,128]{3,2,1,0:T(8,128)(2,1)} %get-tuple-element.27), calls=%async_computation | async-start | bytes 6291456 | tf_op jit(solution)/shard_map/all_to_all | solution.py:369
  28.8 9.2 %collective-permute-start.3 = (bf16[2048,384]{1,0:T(8,128)(2,1)}, bf16[2048,384]{1,0:T(8,128)(2,1)}, u32[]{:S(2)}, u32[]{:S(2)}) collective-permute-start(bf16[2048,384]{1,0:T(8,128)(2,1)} %bitcast.8.gate.own_gate), channel_id=1, source_target_pairs={{0,128},{128,0},{1,129},{129,1},{2,130},{130,2},{3,131},{131,3},{4... | collective-permute-start | bytes 4718600 | tf_op jit(solution)/shard_map/ppermute | solution.py:365
  32.9 5.6 %collective-permute-start.4 = (bf16[2048,384]{1,0:T(8,128)(2,1)}, bf16[2048,384]{1,0:T(8,128)(2,1)}, u32[]{:S(2)}, u32[]{:S(2)}) collective-permute-start(bf16[2048,384]{1,0:T(8,128)(2,1)} %bitcast.9.up.own_up), channel_id=1, source_target_pairs={{0,128},{128,0},{1,129},{129,1},{2,130},{130,2},{3,131},{131,3},{4... | collective-permute-start | bytes 4718600 | tf_op jit(solution)/shard_map/ppermute | solution.py:365
  33.0 7.8 %collective-permute-start.5 = (bf16[384,2048]{1,0:T(8,128)(2,1)}, bf16[384,2048]{1,0:T(8,128)(2,1)}, u32[]{:S(2)}, u32[]{:S(2)}) collective-permute-start(bf16[384,2048]{1,0:T(8,128)(2,1)} %bitcast.10.down), channel_id=1, source_target_pairs={{0,128},{128,0},{1,129},{129,1},{2,130},{130,2},{3,131},{131,3},{4... | collective-permute-start | bytes 4718600 | tf_op jit(solution)/shard_map/ppermute | solution.py:365
  145.5 33.7 %all-to-all-start.2 = ((bf16[128,2,16,128]{3,2,1,0:T(8,128)(2,1)}), bf16[128,2,16,128]{3,2,1,0:T(8,128)(2,1)}, u32[]{:S(2)}, u32[]{:S(2)}) async-start(bf16[128,2,16,128]{3,2,1,0:T(8,128)(2,1)} %bitcast.39), calls=%async_computation.2 | async-start | bytes 2097152 | tf_op jit(solution)/shard_map/all_to_all | solution.py:369
  185.4 16.6 %copy-start = (bf16[1,1,384,384]{3,2,1,0:T(8,128)(2,1)S(1)}, bf16[1,1,384,384]{3,2,1,0:T(8,128)(2,1)}, u32[]{:S(2)}) copy-start(bf16[1,1,384,384]{3,2,1,0:T(8,128)(2,1)} %param.16) | copy-start | bytes 884740
  185.4 19.3 %copy-start.3 = (bf16[256,384]{1,0:T(8,128)(2,1)S(1)}, bf16[256,384]{1,0:T(8,128)(2,1)}, u32[]{:S(2)}) copy-start(bf16[256,384]{1,0:T(8,128)(2,1)} %get-tuple-element.40) | copy-start | bytes 589828
  185.4 19.6 %copy-start.7 = (bf16[256,384]{1,0:T(8,128)(2,1)S(1)}, bf16[256,384]{1,0:T(8,128)(2,1)}, u32[]{:S(2)}) copy-start(bf16[256,384]{1,0:T(8,128)(2,1)} %get-tuple-element.39) | copy-start | bytes 589828
  185.4 33.3 %all-to-all-start.3 = ((bf16[128,2,16,128]{3,2,1,0:T(8,128)(2,1)}), bf16[128,2,16,128]{3,2,1,0:T(8,128)(2,1)}, u32[]{:S(2)}, u32[]{:S(2)}) async-start(bf16[128,2,16,128]{3,2,1,0:T(8,128)(2,1)} %bitcast.38), calls=%async_computation.3 | async-start | bytes 2097152 | tf_op jit(solution)/shard_map/all_to_all | solution.py:369
  196.4 10.4 %collective-permute-start.8 = (bf16[256,2048]{1,0:T(8,128)(2,1)S(1)}, bf16[256,2048]{1,0:T(8,128)(2,1)S(1)}, u32[]{:S(2)}, u32[]{:S(2)}) collective-permute-start(bf16[256,2048]{1,0:T(8,128)(2,1)S(1)} %get-tuple-element.50), channel_id=1, source_target_pairs={{0,128},{128,0},{1,129},{129,1},{2,130},{130,2},{3,131},{131,3},{4... | collective-permute-start | bytes 3145736 | tf_op jit(solution)/shard_map/ppermute | solution.py:365
  202.0 2.7 %collective-permute-start.6 = (bf16[384,384]{1,0:T(8,128)(2,1)S(1)}, bf16[384,384]{1,0:T(8,128)(2,1)S(1)}, u32[]{:S(2)}, u32[]{:S(2)}) collective-permute-start(bf16[384,384]{1,0:T(8,128)(2,1)S(1)} %bitcast.42), channel_id=1, source_target_pairs={{0,128},{128,0},{1,129},{129,1},{2,130},{130,2},{3,131},{131,3},{4... | collective-permute-start | bytes 884744 | tf_op jit(solution)/shard_map/ppermute | solution.py:365
  205.3 1.5 collective-permute-start.7
  221.6 9.3 %collective-permute-start.9 = (bf16[64,2048]{1,0:T(8,128)(2,1)}, bf16[64,2048]{1,0:T(8,128)(2,1)S(1)}, u32[]{:S(2)}, u32[]{:S(2)}) collective-permute-start(bf16[64,2048]{1,0:T(8,128)(2,1)} %get-tuple-element.46), channel_id=1, source_target_pairs={{0,128},{128,0},{1,129},{129,1},{2,130},{130,2},{3,131},{131,3},{4... | collective-permute-start | bytes 786440 | tf_op jit(solution)/shard_map/ppermute | solution.py:365
  230.9 0.7 copy-start.1

commit v4 on v3

--- a/solution.py
+++ b/solution.py
@@ -14,6 +14,7 @@
 SMEM = pl.BlockSpec(memory_space=pltpu.SMEM)
 VMEM = pl.BlockSpec(memory_space=pltpu.VMEM)
 HBM = pl.BlockSpec(memory_space=pltpu.HBM)
+VMEM_MIB = 28
 
 
 def rows_to_tiles(rows, tiles, count, depth):
@@ -21,10 +22,11 @@
         tiles[pl.ds(j, count, stride=depth), :] = rows[:, j * LANES : (j + 1) * LANES]
 
 
-def tile_columns(tiles, first, number, count, depth):
-    return jnp.concatenate(
-        [tiles[pl.ds(j, count, stride=depth), :] for j in range(first, first + number)], axis=1
-    ).astype(BF16)
+def tiles_to_rows(tiles, rows, count, depth):
+    for j in range(depth):
+        rows[:, j * LANES : (j + 1) * LANES] = tiles[pl.ds(j, count, stride=depth), :].astype(
+            rows.dtype
+        )
 
 
 def clear(send, experts):
@@ -157,7 +159,7 @@
     fetch(send, sent, sems.at[0]).wait()
 
 
-def finish_kernel(own_slots, other_slots, back, upstream, keep, away, low, up):
+def finish_kernel(own_slots, other_slots, back, upstream, out, away, keep, low, up, sems):
     tokens, depth = upstream.shape[0], upstream.shape[1]
     upper = on_core(1)
     slot = slot_reader(own_slots, other_slots)
@@ -179,16 +181,11 @@
         down = low[pl.ds(j, tokens, stride=depth), :]
         keep[:, columns] = jnp.where(upper, high, down).astype(BF16)
         away[:, columns] = jnp.where(upper, down, high).astype(BF16)
-
-
-def join_kernel(keep, came, out, sems):
-    segment = lax.axis_index("segment")
-    copies = [
-        fetch(keep, out.at[segment], sems.at[0]),
-        fetch(came, out.at[1 - segment], sems.at[1]),
-    ]
-    for copy in copies:
-        copy.wait()
+    fetch(keep, out.at[lax.axis_index("segment")], sems.at[0]).wait()
+
+
+def join_kernel(came, partial, out, sems):
+    fetch(came, out.at[1 - lax.axis_index("segment")], sems.at[0]).wait()
 
 
 def turn_kernel(turn, gate, up, down, *refs):
@@ -217,43 +214,22 @@
         pl.when(on_core(turn))(work)
 
 
-def forward_parts(tiles, gate, up, count, depth):
-    number = depth // 2
-    hidden_gate = hidden_up = 0.0
-    for first in range(0, depth, number):
-        rows = tile_columns(tiles, first, number, count, depth)
-        here = slice(first * LANES, (first + number) * LANES)
-        hidden_gate += jnp.dot(rows, gate[here, :], preferred_element_type=F32)
-        hidden_up += jnp.dot(rows, up[here, :], preferred_element_type=F32)
+def forward_parts(rows, gate, up):
+    hidden_gate = jnp.dot(rows[...], gate[...], preferred_element_type=F32)
+    hidden_up = jnp.dot(rows[...], up[...], preferred_element_type=F32)
     sigma = 1.0 / (1.0 + jnp.exp(-hidden_gate))
     act = hidden_gate * sigma
     dact = sigma * (1.0 + hidden_gate * (1.0 - sigma))
     return act, hidden_up * dact, (act * hidden_up).astype(BF16)
 
 
-def down_part(tiles, dy_rows, down_t, depth):
-    count = dy_rows.shape[0]
-    number = depth // 2
-    grad_act = 0.0
-    for first in range(0, depth, number):
-        rows = tile_columns(tiles, first, number, count, depth)
-        here = slice(first * LANES, (first + number) * LANES)
-        dy_rows[:, here] = rows
-        grad_act += jnp.dot(rows, down_t[here, :], preferred_element_type=F32)
-    return grad_act
-
-
 def back_part(grad_act, act, slope, gate_up_t, tiles, send, sent, sems):
     count, depth, lanes = send.shape
     both = jnp.concatenate(
         [(grad_act * slope).astype(BF16), (grad_act * act).astype(BF16)], axis=1
     )
-    number = depth // 4
-    for first in range(0, depth, number):
-        here = slice(first * LANES, (first + number) * LANES)
-        dx = jnp.dot(both, gate_up_t[:, here], preferred_element_type=F32)
-        for j in range(number):
-            tiles[pl.ds(first + j, count, stride=depth), :] = dx[:, j * LANES : (j + 1) * LANES]
+    dx = jnp.dot(both, gate_up_t[...], preferred_element_type=F32)
+    rows_to_tiles(dx, tiles, count, depth)
     pieces, copies = 4, []
     part = count // pieces
     for n in range(pieces):
@@ -264,101 +240,106 @@
     return copies
 
 
-def widened(block, tiles):
-    tiles[...] = block[...].astype(F32).reshape(tiles.shape)
+def untile(block, tiles, rows, depth):
+    count = rows.shape[0]
+    tiles[...] = block.astype(F32).reshape(count * depth, LANES)
+    tiles_to_rows(tiles, rows, count, depth)
 
 
 def upper_kernel(
     arrived, own_gate, other_gate, own_up, other_up, own_dt, other_dt, own_gut, other_gut,
     sent, dy_out, act_out,
-    x, dy, gate, up, down_t, gate_up_t, x_tiles, dy_tiles, dx_tiles, dy_rows, activ, send, sems,
+    gate, up, down_t, gate_up_t, tiles, x_rows, dy_rows, activ, send, sems,
 ):
     mine = on_core(1)
-    count, depth = send.shape[:2]
-    x_copy = fetch(arrived.at[:, :CAP], x, sems.at[0])
-    gate_copy = fetch_one_of(mine, own_gate, other_gate, gate, sems.at[1])
-    up_copy = fetch_one_of(mine, own_up, other_up, up, sems.at[2])
-    dy_copy = fetch(arrived.at[:, CAP : 2 * CAP], dy, sems.at[3])
-    down_copy = fetch_one_of(mine, own_dt, other_dt, down_t, sems.at[4])
-    back_copy = fetch_one_of(mine, own_gut, other_gut, gate_up_t, sems.at[5])
-    x_copy.wait()
-    widened(x, x_tiles)
-    for copy in (gate_copy, up_copy, dy_copy, down_copy, back_copy):
-        copy.wait()
-    widened(dy, dy_tiles)
-    act, slope, rounded = forward_parts(x_tiles, gate, up, count, depth)
+    depth = send.shape[1]
+    gate_copy = fetch_one_of(mine, own_gate, other_gate, gate, sems.at[0])
+    up_copy = fetch_one_of(mine, own_up, other_up, up, sems.at[1])
+    down_copy = fetch_one_of(mine, own_dt, other_dt, down_t, sems.at[2])
+    back_copy = fetch_one_of(mine, own_gut, other_gut, gate_up_t, sems.at[3])
+    untile(arrived[:, :CAP], tiles, x_rows, depth)
+    gate_copy.wait()
+    up_copy.wait()
+    act, slope, rounded = forward_parts(x_rows, gate, up)
     activ[...] = rounded
-    grad_act = down_part(dy_tiles, dy_rows, down_t, depth)
-    saves = [fetch(activ, act_out, sems.at[6]), fetch(dy_rows, dy_out, sems.at[7])]
-    saves += back_part(
-        grad_act, act, slope, gate_up_t, dx_tiles, send, sent, sems.at[pl.ds(8, 4)]
-    )
+    untile(arrived[:, CAP : 2 * CAP], tiles, dy_rows, depth)
+    saves = [fetch(activ, act_out, sems.at[4]), fetch(dy_rows, dy_out, sems.at[5])]
+    down_copy.wait()
+    grad_act = jnp.dot(dy_rows[...], down_t[...], preferred_element_type=F32)
+    back_copy.wait()
+    saves += back_part(grad_act, act, slope, gate_up_t, tiles, send, sent, sems.at[pl.ds(6, 4)])
     for copy in saves:
         copy.wait()
 
 
 def forward_kernel(
     arrived, own_gate, other_gate, own_up, other_up, act_out, slope_out, activ_out,
-    x, gate, up, tiles, sems,
+    act, slope, activ, gate, up, tiles, x_rows, sems,
 ):
     mine = on_core(0)
-    experts, cap, depth = x.shape[:3]
-    x_copy = fetch(arrived.at[:, 2 * CAP :], x, sems.at[0])
-    gate_copy = fetch_one_of(mine, own_gate, other_gate, gate, sems.at[1])
-    up_copy = fetch_one_of(mine, own_up, other_up, up, sems.at[2])
-    x_copy.wait()
-    widened(x, tiles)
+    depth = arrived.shape[2]
+    gate_copy = fetch_one_of(mine, own_gate, other_gate, gate, sems.at[0])
+    up_copy = fetch_one_of(mine, own_up, other_up, up, sems.at[1])
+    untile(arrived[:, 2 * CAP :], tiles, x_rows, depth)
     gate_copy.wait()
     up_copy.wait()
-    act, slope, rounded = forward_parts(tiles, gate, up, experts * cap, depth)
-    act_out[...] = act
-    slope_out[...] = slope
-    activ_out[...] = rounded
+    act[...], slope[...], activ[...] = forward_parts(x_rows, gate, up)
+    saves = [
+        fetch(act, act_out, sems.at[2]),
+        fetch(slope, slope_out, sems.at[3]),
+        fetch(activ, activ_out, sems.at[4]),
+    ]
+    for copy in saves:
+        copy.wait()
 
 
 def lower_kernel(
-    dy_in, act_in, slope_in, own_dt, other_dt, own_gut, other_gut, sent, dy_out,
-    dy, act, slope, down_t, gate_up_t, dy_tiles, dx_tiles, dy_rows, send, sems,
+    dy, act_in, slope_in, own_dt, other_dt, own_gut, other_gut, sent, dy_out,
+    act, slope, down_t, gate_up_t, tiles, dy_rows, send, sems,
 ):
     mine = on_core(0)
-    count, depth = send.shape[:2]
-    pieces = 4
-    part = count // pieces
-    arriving = [
-        fetch(dy_in.at[pl.ds(n * part, part)], dy.at[pl.ds(n * part, part)], sems.at[9 + n])
-        for n in range(pieces)
-    ]
     down_copy = fetch_one_of(mine, own_dt, other_dt, down_t, sems.at[0])
     act_copy = fetch(act_in, act, sems.at[1])
     slope_copy = fetch(slope_in, slope, sems.at[2])
     back_copy = fetch_one_of(mine, own_gut, other_gut, gate_up_t, sems.at[3])
-    for n, copy in enumerate(arriving):
+    untile(dy[...], tiles, dy_rows, send.shape[1])
+    saves = [fetch(dy_rows, dy_out, sems.at[4])]
+    down_copy.wait()
+    grad_act = jnp.dot(dy_rows[...], down_t[...], preferred_element_type=F32)
+    for copy in (act_copy, slope_copy, back_copy):
         copy.wait()
-        dy_tiles[n * part * depth : (n + 1) * part * depth, :] = (
-            dy[n * part : (n + 1) * part].astype(F32).reshape(part * depth, LANES)
-        )
-    for copy in (down_copy, act_copy, slope_copy, back_copy):
-        copy.wait()
-    grad_act = down_part(dy_tiles, dy_rows, down_t, depth)
-    saves = [fetch(dy_rows, dy_out, sems.at[4])]
     saves += back_part(
-        grad_act, act[...], slope[...], gate_up_t, dx_tiles, send, sent, sems.at[pl.ds(5, 4)]
+        grad_act, act[...], slope[...], gate_up_t, tiles, send, sent, sems.at[pl.ds(5, 4)]
     )
     for copy in saves:
         copy.wait()
+
+
+INPLACE = pl.BlockSpec(memory_space=pltpu.VMEM)
+
+
+def placed(arg, spec):
+    if spec is HBM:
+        return pltpu.with_memory_space_constraint(arg, pltpu.HBM)
+    if spec is INPLACE:
+        return pltpu.with_memory_space_constraint(arg, pltpu.VMEM)
+    return arg
 
 
 def call(kernel, args, in_specs, out_shape, out_specs, scratch, flops, moved, aliases={}):
     return pl.pallas_call(
         kernel,
         in_specs=in_specs,
-        out_shape=out_shape,
+        out_shape=tuple(
+            pltpu.HBM(out.shape, out.dtype) if spec is HBM else out
+            for out, spec in zip(out_shape, out_specs)
+        ),
         out_specs=out_specs,
         scratch_shapes=scratch,
         input_output_aliases=aliases,
-        compiler_params=pltpu.CompilerParams(vmem_limit_bytes=63 * 1024 * 1024),
+        compiler_params=pltpu.CompilerParams(vmem_limit_bytes=VMEM_MIB * 1024 * 1024),
         cost_estimate=pl.CostEstimate(flops=flops, bytes_accessed=moved, transcendentals=0),
-    )(*args)
+    )(*[placed(arg, spec) for arg, spec in zip(args, in_specs)])
 
 
 def swapped(block):
@@ -444,20 +425,19 @@
 
     tiles = pltpu.VMEM((count * depth, LANES), F32)
     rows = pltpu.VMEM((count, width), BF16)
-    part = pltpu.VMEM((experts, CAP, depth, LANES), BF16)
     flat = (count, depth, LANES)
     flat_scratch = pltpu.VMEM(flat, BF16)
     mat = 2 * count * width * hidden
     back_send, dy_rows1, activ1 = call(
         upper_kernel,
         (arrived, gate, other_gate, up, other_up, own_dt, other_dt, own_gut, other_gut),
-        [HBM] * 9,
+        [INPLACE] + [HBM] * 8,
         (shape(flat), shape((count, width)), shape((count, hidden))),
         (HBM,) * 3,
         [
-            part, part, matrix, matrix, matrix, pltpu.VMEM((2 * hidden, width), BF16), tiles,
-            tiles, tiles, rows, pltpu.VMEM((count, hidden), BF16), flat_scratch,
-            pltpu.SemaphoreType.DMA((12,)),
+            matrix, matrix, matrix, pltpu.VMEM((2 * hidden, width), BF16), tiles,
+            rows, rows, pltpu.VMEM((count, hidden), BF16), flat_scratch,
+            pltpu.SemaphoreType.DMA((10,)),
         ],
         5 * mat,
         9_000_000,
@@ -470,10 +450,14 @@
     act0, slope0, activ0 = call(
         forward_kernel,
         (arrived, gate, other_gate, up, other_up),
-        [HBM] * 5,
+        [INPLACE] + [HBM] * 4,
         (shape((count, hidden), F32), shape((count, hidden), F32), shape((count, hidden))),
-        (VMEM,) * 3,
-        [part, matrix, matrix, tiles, pltpu.SemaphoreType.DMA((3,))],
+        (HBM,) * 3,
+        [
+            pltpu.VMEM((count, hidden), F32), pltpu.VMEM((count, hidden), F32),
+            pltpu.VMEM((count, hidden), BF16), matrix, matrix, tiles, rows,
+            pltpu.SemaphoreType.DMA((5,)),
+        ],
         2 * mat,
         5_000_000,
     )
@@ -485,7 +469,7 @@
     dy_send, grad1 = call(
         relay_kernel,
         (own_slots, other_slots, own_w, other_w, back, grad_tiles),
-        [SMEM] * 4 + [VMEM] * 2,
+        [SMEM] * 4 + [INPLACE, VMEM],
         (shape(flat), shape((tokens, depth, LANES))),
         (HBM, VMEM),
         [flat_scratch, pltpu.SemaphoreType.DMA((1,))],
@@ -496,13 +480,13 @@
     back_send0, dy_rows0 = call(
         lower_kernel,
         (dy, act0, slope0, own_dt, other_dt, own_gut, other_gut),
-        [HBM] * 7,
+        [INPLACE] + [HBM] * 6,
         (shape(flat), shape((count, width))),
         (HBM,) * 2,
         [
-            flat_scratch, pltpu.VMEM((count, hidden), F32), pltpu.VMEM((count, hidden), F32),
-            matrix, pltpu.VMEM((2 * hidden, width), BF16), tiles, tiles, rows, flat_scratch,
-            pltpu.SemaphoreType.DMA((13,)),
+            pltpu.VMEM((count, hidden), F32), pltpu.VMEM((count, hidden), F32),
+            matrix, pltpu.VMEM((2 * hidden, width), BF16), tiles, rows, flat_scratch,
+            pltpu.SemaphoreType.DMA((9,)),
         ],
         3 * mat,
         8_000_000,
@@ -534,26 +518,28 @@
         (back0, rotated_grad, ekfac_scales)
     )
 
-    keep, away = call(
+    own_grads, away = call(
         finish_kernel,
         (own_slots, other_slots, back0, grad1),
-        [SMEM] * 2 + [VMEM] * 2,
-        (shape((tokens, width)), shape((tokens, width))),
-        (VMEM,) * 2,
-        [pltpu.VMEM((tile_rows, LANES), F32)] * 2,
+        [SMEM] * 2 + [INPLACE, VMEM],
+        (shape((micros, tokens, width)), shape((tokens, width))),
+        (HBM, VMEM),
+        [row_block]
+        + [pltpu.VMEM((tile_rows, LANES), F32)] * 2
+        + [pltpu.SemaphoreType.DMA((1,))],
         1_000_000,
         2_000_000,
     )
-    came = swapped(away)
-    grads = call(
+    (grads,) = call(
         join_kernel,
-        (keep, came),
-        [HBM] * 2,
-        shape((micros, tokens, width)),
-        HBM,
-        [pltpu.SemaphoreType.DMA((2,))],
+        (swapped(away), own_grads),
+        [INPLACE, HBM],
+        (shape((micros, tokens, width)),),
+        (HBM,),
+        [pltpu.SemaphoreType.DMA((1,))],
         0,
         1_000_000,
+        {1: 0},
     )
     return (grads[None], rotated_grad[None, None], ekfac_scales[None, None])
 

time: 249 us -> 229 us (0.920)
  Pallas kernels: 58 us -> 38.1 us
    pallas_call x10, Pallas kernels: 58 us -> 38.1 us  [call(): pl.pallas_call(kernel, in_specs=in_specs, out_shape=tuple((pltpu.HBM(out....]
  transfers between devices with their start and end apart: 13 -> 13, of which waited for: 10 -> 10; matrix products, arithmetic and copies ran while one was open for 4% -> 5% of each run, Pallas kernels for 6% -> 6%
where the time goes in v4:
time: 229 us; the launch traced here: 228 us
  waiting for transfers between devices  86.9 us (38%)
  starting transfers between devices  53.1 us (23%)
  Pallas kernels  38.1 us (17%)
  blocking collectives  35.4 us (15%)
  matrix products  7.57 us (3%)
  other arithmetic  3.21 us (1%)
  local copies, waits for them, and re-layouts  2.88 us (1%)
    all_to_all x3, waiting for transfers between devices, exchanged(): lax.all_to_all(block, 'expert', split_axis=0, concat_axis=0, tiled=True)  78.3 us
    pallas_call x10, Pallas kernels, call(): pl.pallas_call(kernel, in_specs=in_specs, out_shape=tuple((pltpu.HBM(out....  38.1 us
    all_to_all x1, blocking collectives, exchanged(): lax.all_to_all(block, 'expert', split_axis=0, concat_axis=0, tiled=True)  35.4 us
    all_to_all x3, starting transfers between devices, exchanged(): lax.all_to_all(block, 'expert', split_axis=0, concat_axis=0, tiled=True)  32 us
    ppermute x10, starting transfers between devices, swapped(): return lax.ppermute(block, 'segment', [(0, 1), (1, 0)])  21.2 us
    ppermute x10, waiting for transfers between devices, swapped(): return lax.ppermute(block, 'segment', [(0, 1), (1, 0)])  8.57 us
  transfers between devices with their start and end apart: 13, of which 10 were waited for; matrix products, arithmetic and copies ran while one was open for 5% of the time, Pallas kernels for 6%

profile of v4, /device:TPU:1, one launch (start us, length us, event | category | flops | bytes accessed | tf_op | source)
XLA Modules:
  0.0 228.2 jit_solution(11145678988584529421)
XLA Ops:
  0.6 1.0 dynamic-slice_bitcast_fusion
  1.6 3.3 %collective-permute-start.2 = (bf16[64,2048]{1,0:T(8,128)(2,1)S(1)}, bf16[64,2048]{1,0:T(8,128)(2,1)S(1)}, u32[]{:S(2)}, u32[]{:S(2)}) collective-permute-start(bf16[64,2048]{1,0:T(8,128)(2,1)S(1)} %dynamic-slice_bitcast_fusion), channel_id=1, source_target_pairs={{0,128},{128,0},{1,129},{129,1},{2,130},{130,2},{3,131},{131,3},{4... | collective-permute-start | bytes 786440 | tf_op jit(solution)/shard_map/ppermute | solution.py:346
  4.9 1.0 convert_reduce_fusion
  8.9 5.5 %shard_map.113 = (bf16[128,6,16,128]{3,2,1,0:T(8,128)(2,1)}, bf16[64,16,128]{2,1,0:T(8,128)(2,1)}) custom-call(s32[2,2,64]{2,1,0:T(2,128)S(1)} %minimum_add_fusion.own_slots, s32[2,2,64]{2,1,0:T(2,128)S(1)} %collective-permute-done.other_slots, f32[2,2,64]{2,1,0:T(2,128)S(1)} %bitcast.39, f32[2,2,64]{2,1,0:T(2,128)S(1)} %collective-permute-done.1.other_w, ...), custom_call_target="tpu_custom_call" | custom-call | flops 1000000 | bytes 5000000 | tf_op jit(solution)/shard_map/pallas_call | solution.py:330
  14.5 13.8 %all-to-all-start = ((bf16[128,6,16,128]{3,2,1,0:T(8,128)(2,1)}), bf16[128,6,16,128]{3,2,1,0:T(8,128)(2,1)S(1)}, u32[]{:S(2)}, u32[]{:S(2)}) async-start(bf16[128,6,16,128]{3,2,1,0:T(8,128)(2,1)} %get-tuple-element.27), calls=%async_computation | async-start | bytes 6291456 | tf_op jit(solution)/shard_map/all_to_all | solution.py:350
  28.3 4.0 %collective-permute-start.3 = (bf16[2048,384]{1,0:T(8,128)(2,1)}, bf16[2048,384]{1,0:T(8,128)(2,1)S(1)}, u32[]{:S(2)}, u32[]{:S(2)}) collective-permute-start(bf16[2048,384]{1,0:T(8,128)(2,1)} %bitcast.42), channel_id=1, source_target_pairs={{0,128},{128,0},{1,129},{129,1},{2,130},{130,2},{3,131},{131,3},{4... | collective-permute-start | bytes 4718600 | tf_op jit(solution)/shard_map/ppermute | solution.py:346
  32.7 4.6 %shard_map.114 = (bf16[768,2048]{1,0:T(8,128)(2,1)}, bf16[2048,384]{1,0:T(8,128)(2,1)}) custom-call(bf16[2048,384]{1,0:T(8,128)(2,1)} %bitcast.43, bf16[2048,384]{1,0:T(8,128)(2,1)} %bitcast.48, bf16[384,2048]{1,0:T(8,128)(2,1)} %bitcast.53, bf16[768,2048]{1,0:T(8,128)(2,1)} %get-tuple-element.28.refs_0_, ...), custom_call_target="tpu_custom_call", output_to_operand_aliasing={{0}: (3, {}), {1}: (4, {})} | custom-call | flops 1000000 | bytes 9000000 | tf_op jit(solution)/shard_map/pallas_call | solution.py:330
  37.7 2.2 collective-permute-done.5.down
  40.0 1.2 copy-done.4
  41.2 4.5 %shard_map.115 = (bf16[768,2048]{1,0:T(8,128)(2,1)}, bf16[2048,384]{1,0:T(8,128)(2,1)}) custom-call(bf16[2048,384]{1,0:T(8,128)(2,1)} %copy-done.2, bf16[2048,384]{1,0:T(8,128)(2,1)} %copy-done.3, bf16[384,2048]{1,0:T(8,128)(2,1)} %copy-done.4), custom_call_target="tpu_custom_call" | custom-call | flops 1000000 | bytes 9000000 | tf_op jit(solution)/shard_map/pallas_call | solution.py:330
  45.7 51.5 %all-to-all-done.arrived = bf16[128,6,16,128]{3,2,1,0:T(8,128)(2,1)S(1)} async-done(((bf16[128,6,16,128]{3,2,1,0:T(8,128)(2,1)}), bf16[128,6,16,128]{3,2,1,0:T(8,128)(2,1)S(1)}, u32[]{:S(2)}, u32[]{:S(2)}) %all-to-all-start) | async-done | bytes 3145760 | tf_op jit(solution)/shard_map/all_to_all | solution.py:350
  97.2 7.3 %shard_map.116 = (bf16[256,16,128]{2,1,0:T(8,128)(2,1)}, bf16[256,2048]{1,0:T(8,128)(2,1)}, bf16[256,384]{1,0:T(8,128)(2,1)}) custom-call(bf16[128,6,16,128]{3,2,1,0:T(8,128)(2,1)S(1)} %all-to-all-done.arrived, bf16[2048,384]{1,0:T(8,128)(2,1)} %bitcast.44, bf16[2048,384]{1,0:T(8,128)(2,1)} %copy-done.2, bf16[2048,384]{1,0:T(8,128)(2,1)} %bitcast.49, ...), custom_call_target="tpu_custom_call" | custom-call | flops 2013265920 | bytes 9000000 | tf_op jit(solution)/shard_map/pallas_call | solution.py:330
  104.5 35.4 %all_to_all.20 = bf16[128,2,16,128]{3,2,1,0:T(8,128)(2,1)S(1)} all-to-all(bf16[128,2,16,128]{3,2,1,0:T(8,128)(2,1)} %bitcast.57), channel_id=1, replica_groups=mesh['segment'=2,'expert'=128] {'expert'}, dimensions={0} | all-to-all | bytes 2097152 | tf_op jit(solution)/shard_map/all_to_all | solution.py:350
  139.9 2.6 %shard_map.117 = (bf16[256,16,128]{2,1,0:T(8,128)(2,1)}, bf16[64,16,128]{2,1,0:T(8,128)(2,1)S(1)}) custom-call(s32[2,2,64]{2,1,0:T(2,128)S(1)} %minimum_add_fusion.own_slots, s32[2,2,64]{2,1,0:T(2,128)S(1)} %collective-permute-done.other_slots, f32[2,2,64]{2,1,0:T(2,128)S(1)} %bitcast.40, f32[2,2,64]{2,1,0:T(2,128)S(1)} %collective-permute-done.1.other_w, ...), custom_call_target="tpu_custom_call" | custom-call | flops 1000000 | bytes 3000000 | tf_op jit(solution)/shard_map/pallas_call | solution.py:330
  142.5 9.5 %all-to-all-start.2 = ((bf16[128,2,16,128]{3,2,1,0:T(8,128)(2,1)}), bf16[128,2,16,128]{3,2,1,0:T(8,128)(2,1)}, u32[]{:S(2)}, u32[]{:S(2)}) async-start(bf16[128,2,16,128]{3,2,1,0:T(8,128)(2,1)} %bitcast.56), calls=%async_computation.2 | async-start | bytes 2097152 | tf_op jit(solution)/shard_map/all_to_all | solution.py:350
  152.0 4.0 %shard_map.118 = (f32[256,384]{1,0:T(8,128)}, f32[256,384]{1,0:T(8,128)}, bf16[256,384]{1,0:T(8,128)(2,1)}) custom-call(bf16[128,6,16,128]{3,2,1,0:T(8,128)(2,1)S(1)} %all-to-all-done.arrived, bf16[2048,384]{1,0:T(8,128)(2,1)} %bitcast.45, bf16[2048,384]{1,0:T(8,128)(2,1)} %copy-done.2, bf16[2048,384]{1,0:T(8,128)(2,1)} %bitcast.50, bf16[2048,384]{1,0:T(8,128)(2,1)} %copy-done.3), custom_call_target="tpu_custom_call" | custom-call | flops 805306368 | bytes 5000000 | tf_op jit(solution)/shard_map/pallas_call | solution.py:330
  156.0 20.2 %all-to-all-done.2 = bf16[128,2,16,128]{3,2,1,0:T(8,128)(2,1)} async-done(((bf16[128,2,16,128]{3,2,1,0:T(8,128)(2,1)}), bf16[128,2,16,128]{3,2,1,0:T(8,128)(2,1)}, u32[]{:S(2)}, u32[]{:S(2)}) %all-to-all-start.2) | async-done | bytes 1048608 | tf_op jit(solution)/shard_map/all_to_all | solution.py:350
  176.2 6.6 %shard_map.119 = (bf16[256,16,128]{2,1,0:T(8,128)(2,1)}, bf16[256,2048]{1,0:T(8,128)(2,1)}) custom-call(bf16[256,16,128]{2,1,0:T(8,128)(2,1)} %bitcast.14.dy, f32[256,384]{1,0:T(8,128)} %get-tuple-element.36.act_in, f32[256,384]{1,0:T(8,128)} %get-tuple-element.37.slope_in, bf16[2048,384]{1,0:T(8,128)(2,1)} %get-tuple-element.29.own_dt, ...), custom_call_target="tpu_custom_call" | custom-call | flops 1207959552 | bytes 8000000 | tf_op jit(solution)/shard_map/pallas_call | solution.py:330
  182.8 8.7 %all-to-all-start.3 = ((bf16[128,2,16,128]{3,2,1,0:T(8,128)(2,1)}), bf16[128,2,16,128]{3,2,1,0:T(8,128)(2,1)S(1)}, u32[]{:S(2)}, u32[]{:S(2)}) async-start(bf16[128,2,16,128]{3,2,1,0:T(8,128)(2,1)} %bitcast.55), calls=%async_computation.3 | async-start | bytes 2097152 | tf_op jit(solution)/shard_map/all_to_all | solution.py:350
  191.6 1.5 broadcast_select_fusion.1
  193.1 4.9 %collective-permute-start.8 = (bf16[256,2048]{1,0:T(8,128)(2,1)S(1)}, bf16[256,2048]{1,0:T(8,128)(2,1)S(1)}, u32[]{:S(2)}, u32[]{:S(2)}) collective-permute-start(bf16[256,2048]{1,0:T(8,128)(2,1)S(1)} %get-tuple-element.50), channel_id=1, source_target_pairs={{0,128},{128,0},{1,129},{129,1},{2,130},{130,2},{3,131},{131,3},{4... | collective-permute-start | bytes 3145736 | tf_op jit(solution)/shard_map/ppermute | solution.py:346
  198.1 2.7 %collective-permute-done.6 = bf16[384,384]{1,0:T(8,128)(2,1)S(1)} collective-permute-done((bf16[384,384]{1,0:T(8,128)(2,1)}, bf16[384,384]{1,0:T(8,128)(2,1)S(1)}, u32[]{:S(2)}, u32[]{:S(2)}) %collective-permute-start.6) | collective-permute-done | bytes 294944 | tf_op jit(solution)/shard_map/ppermute | solution.py:346
  200.8 1.3 convolution_convert_fusion
  202.2 1.4 broadcast_select_fusion.3
  204.0 1.1 collective-permute-done.7
  205.1 2.2 multiply_convert_fusion.1
  207.2 2.7 %convolution_multiply_fusion = f32[384,2048]{1,0:T(8,128)} fusion(bf16[256,2048]{1,0:T(8,128)(2,1)S(1)} %collective-permute-done.8, bf16[256,2048]{1,0:T(8,128)(2,1)S(1)} %get-tuple-element.49, bf16[256,384]{1,0:T(8,128)(2,1)S(1)} %collective-permute-done.7, bf16[256,384]{1,0:T(8,128)(2,1)S(1)} %get-tuple-element.51), kind=kOutput, calls=%fused_computation.2 | convolution fusion | flops 813563904 | bytes 5636096 | tf_op jit(solution)/shard_map/dot_general | solution.py:514
  209.9 6.5 %all-to-all-done.3 = bf16[128,2,16,128]{3,2,1,0:T(8,128)(2,1)S(1)} async-done(((bf16[128,2,16,128]{3,2,1,0:T(8,128)(2,1)}), bf16[128,2,16,128]{3,2,1,0:T(8,128)(2,1)S(1)}, u32[]{:S(2)}, u32[]{:S(2)}) %all-to-all-start.3) | async-done | bytes 1048608 | tf_op jit(solution)/shard_map/all_to_all | solution.py:350
  216.5 2.3 shard_map.120
  218.7 7.4 %collective-permute-start.9 = (bf16[64,2048]{1,0:T(8,128)(2,1)S(1)}, bf16[64,2048]{1,0:T(8,128)(2,1)S(1)}, u32[]{:S(2)}, u32[]{:S(2)}) collective-permute-start(bf16[64,2048]{1,0:T(8,128)(2,1)S(1)} %get-tuple-element.45), channel_id=1, source_target_pairs={{0,128},{128,0},{1,129},{129,1},{2,130},{130,2},{3,131},{131,3},{4... | collective-permute-start | bytes 786440 | tf_op jit(solution)/shard_map/ppermute | solution.py:346
  226.1 1.2 collective-permute-done.9.came
  227.3 0.7 shard_map.121
  (27 shorter events, 4.4 us)
Async XLA Ops:
  0.6 8.3 %copy-start.1 = (f32[1,2,64,2]{2,3,1,0:T(2,128)S(1)}, f32[1,2,64,2]{2,3,1,0:T(2,128)}, u32[]{:S(2)}) copy-start(f32[1,2,64,2]{2,3,1,0:T(2,128)} %param.12) | copy-start | bytes 3076
  1.6 6.6 %collective-permute-start.2 = (bf16[64,2048]{1,0:T(8,128)(2,1)S(1)}, bf16[64,2048]{1,0:T(8,128)(2,1)S(1)}, u32[]{:S(2)}, u32[]{:S(2)}) collective-permute-start(bf16[64,2048]{1,0:T(8,128)(2,1)S(1)} %dynamic-slice_bitcast_fusion), channel_id=1, source_target_pairs={{0,128},{128,0},{1,129},{129,1},{2,130},{130,2},{3,131},{131,3},{4... | collective-permute-start | bytes 786440 | tf_op jit(solution)/shard_map/ppermute | solution.py:346
  6.7 1.2 collective-permute-start
  6.7 1.5 collective-permute-start.1
  8.2 0.7 copy-start.6
  14.5 82.7 %all-to-all-start = ((bf16[128,6,16,128]{3,2,1,0:T(8,128)(2,1)}), bf16[128,6,16,128]{3,2,1,0:T(8,128)(2,1)S(1)}, u32[]{:S(2)}, u32[]{:S(2)}) async-start(bf16[128,6,16,128]{3,2,1,0:T(8,128)(2,1)} %get-tuple-element.27), calls=%async_computation | async-start | bytes 6291456 | tf_op jit(solution)/shard_map/all_to_all | solution.py:350
  28.3 9.1 %collective-permute-start.3 = (bf16[2048,384]{1,0:T(8,128)(2,1)}, bf16[2048,384]{1,0:T(8,128)(2,1)S(1)}, u32[]{:S(2)}, u32[]{:S(2)}) collective-permute-start(bf16[2048,384]{1,0:T(8,128)(2,1)} %bitcast.42), channel_id=1, source_target_pairs={{0,128},{128,0},{1,129},{129,1},{2,130},{130,2},{3,131},{131,3},{4... | collective-permute-start | bytes 4718600 | tf_op jit(solution)/shard_map/ppermute | solution.py:346
  32.2 5.5 %collective-permute-start.4 = (bf16[2048,384]{1,0:T(8,128)(2,1)}, bf16[2048,384]{1,0:T(8,128)(2,1)S(1)}, u32[]{:S(2)}, u32[]{:S(2)}) collective-permute-start(bf16[2048,384]{1,0:T(8,128)(2,1)} %bitcast.47), channel_id=1, source_target_pairs={{0,128},{128,0},{1,129},{129,1},{2,130},{130,2},{3,131},{131,3},{4... | collective-permute-start | bytes 4718600 | tf_op jit(solution)/shard_map/ppermute | solution.py:346
  32.3 7.6 %collective-permute-start.5 = (bf16[384,2048]{1,0:T(8,128)(2,1)}, bf16[384,2048]{1,0:T(8,128)(2,1)S(1)}, u32[]{:S(2)}, u32[]{:S(2)}) collective-permute-start(bf16[384,2048]{1,0:T(8,128)(2,1)} %bitcast.52), channel_id=1, source_target_pairs={{0,128},{128,0},{1,129},{129,1},{2,130},{130,2},{3,131},{131,3},{4... | collective-permute-start | bytes 4718600 | tf_op jit(solution)/shard_map/ppermute | solution.py:346
  37.4 2.6 %copy-start.2 = (bf16[2048,384]{1,0:T(8,128)(2,1)}, bf16[2048,384]{1,0:T(8,128)(2,1)S(1)}, u32[]{:S(2)}) copy-start(bf16[2048,384]{1,0:T(8,128)(2,1)S(1)} %collective-permute-done.3.gate.other_gate) | copy-start | bytes 4718596
  37.7 2.3 copy-start.3
  40.0 1.2 copy-start.4
  97.2 42.7 %copy-start = (bf16[64,16,128]{2,1,0:T(8,128)(2,1)S(1)}, bf16[64,16,128]{2,1,0:T(8,128)(2,1)}, u32[]{:S(2)}) copy-start(bf16[64,16,128]{2,1,0:T(8,128)(2,1)} %get-tuple-element.34.upstream) | copy-start | bytes 786436
  142.5 33.7 %all-to-all-start.2 = ((bf16[128,2,16,128]{3,2,1,0:T(8,128)(2,1)}), bf16[128,2,16,128]{3,2,1,0:T(8,128)(2,1)}, u32[]{:S(2)}, u32[]{:S(2)}) async-start(bf16[128,2,16,128]{3,2,1,0:T(8,128)(2,1)} %bitcast.56), calls=%async_computation.2 | async-start | bytes 2097152 | tf_op jit(solution)/shard_map/all_to_all | solution.py:350
  176.2 15.3 %copy-start.5 = (bf16[256,2048]{1,0:T(8,128)(2,1)S(1)}, bf16[256,2048]{1,0:T(8,128)(2,1)}, u32[]{:S(2)}) copy-start(bf16[256,2048]{1,0:T(8,128)(2,1)} %get-tuple-element.41) | copy-start | bytes 3145732
  182.8 33.6 %all-to-all-start.3 = ((bf16[128,2,16,128]{3,2,1,0:T(8,128)(2,1)}), bf16[128,2,16,128]{3,2,1,0:T(8,128)(2,1)S(1)}, u32[]{:S(2)}, u32[]{:S(2)}) async-start(bf16[128,2,16,128]{3,2,1,0:T(8,128)(2,1)} %bitcast.55), calls=%async_computation.3 | async-start | bytes 2097152 | tf_op jit(solution)/shard_map/all_to_all | solution.py:350
  193.1 12.0 %collective-permute-start.8 = (bf16[256,2048]{1,0:T(8,128)(2,1)S(1)}, bf16[256,2048]{1,0:T(8,128)(2,1)S(1)}, u32[]{:S(2)}, u32[]{:S(2)}) collective-permute-start(bf16[256,2048]{1,0:T(8,128)(2,1)S(1)} %get-tuple-element.50), channel_id=1, source_target_pairs={{0,128},{128,0},{1,129},{129,1},{2,130},{130,2},{3,131},{131,3},{4... | collective-permute-start | bytes 3145736 | tf_op jit(solution)/shard_map/ppermute | solution.py:346
  198.0 2.8 %collective-permute-start.6 = (bf16[384,384]{1,0:T(8,128)(2,1)}, bf16[384,384]{1,0:T(8,128)(2,1)S(1)}, u32[]{:S(2)}, u32[]{:S(2)}) collective-permute-start(bf16[384,384]{1,0:T(8,128)(2,1)} %bitcast.59), channel_id=1, source_target_pairs={{0,128},{128,0},{1,129},{129,1},{2,130},{130,2},{3,131},{131,3},{4... | collective-permute-start | bytes 884744 | tf_op jit(solution)/shard_map/ppermute | solution.py:346
  203.5 1.5 collective-permute-start.7
  218.7 8.6 %collective-permute-start.9 = (bf16[64,2048]{1,0:T(8,128)(2,1)S(1)}, bf16[64,2048]{1,0:T(8,128)(2,1)S(1)}, u32[]{:S(2)}, u32[]{:S(2)}) collective-permute-start(bf16[64,2048]{1,0:T(8,128)(2,1)S(1)} %get-tuple-element.45), channel_id=1, source_target_pairs={{0,128},{128,0},{1,129},{129,1},{2,130},{130,2},{3,131},{131,3},{4... | collective-permute-start | bytes 786440 | tf_op jit(solution)/shard_map/ppermute | solution.py:346

commit v5 on v4

--- a/solution.py
+++ b/solution.py
@@ -247,7 +247,7 @@
 
 
 def upper_kernel(
-    arrived, own_gate, other_gate, own_up, other_up, own_dt, other_dt, own_gut, other_gut,
+    arrived, own_gate, other_gate, own_up, other_up, own_dt, other_dt, own_gut, other_gut, after,
     sent, dy_out, act_out,
     gate, up, down_t, gate_up_t, tiles, x_rows, dy_rows, activ, send, sems,
 ):
@@ -272,25 +272,26 @@
         copy.wait()
 
 
-def forward_kernel(
-    arrived, own_gate, other_gate, own_up, other_up, act_out, slope_out, activ_out,
-    act, slope, activ, gate, up, tiles, x_rows, sems,
-):
-    mine = on_core(0)
+def forward_kernel(core, arrived, matrix_gate, matrix_up, *refs):
+    act_out, slope_out, activ_out, act, slope, activ, gate, up, tiles, x_rows, sems = refs[-11:]
     depth = arrived.shape[2]
-    gate_copy = fetch_one_of(mine, own_gate, other_gate, gate, sems.at[0])
-    up_copy = fetch_one_of(mine, own_up, other_up, up, sems.at[1])
-    untile(arrived[:, 2 * CAP :], tiles, x_rows, depth)
-    gate_copy.wait()
-    up_copy.wait()
-    act[...], slope[...], activ[...] = forward_parts(x_rows, gate, up)
-    saves = [
-        fetch(act, act_out, sems.at[2]),
-        fetch(slope, slope_out, sems.at[3]),
-        fetch(activ, activ_out, sems.at[4]),
-    ]
-    for copy in saves:
-        copy.wait()
+
+    def work():
+        gate_copy = fetch(matrix_gate, gate, sems.at[0])
+        up_copy = fetch(matrix_up, up, sems.at[1])
+        untile(arrived[:, 2 * CAP :], tiles, x_rows, depth)
+        gate_copy.wait()
+        up_copy.wait()
+        act[...], slope[...], activ[...] = forward_parts(x_rows, gate, up)
+        saves = [
+            fetch(act, act_out, sems.at[2]),
+            fetch(slope, slope_out, sems.at[3]),
+            fetch(activ, activ_out, sems.at[4]),
+        ]
+        for copy in saves:
+            copy.wait()
+
+    pl.when(on_core(core))(work)
 
 
 def lower_kernel(
@@ -428,10 +429,32 @@
     flat = (count, depth, LANES)
     flat_scratch = pltpu.VMEM(flat, BF16)
     mat = 2 * count * width * hidden
+
+    def forwarded(core, matrix_gate, matrix_up, made=()):
+        return call(
+            functools.partial(forward_kernel, core),
+            (arrived, matrix_gate, matrix_up, *made),
+            [INPLACE] + [HBM] * (2 + len(made)),
+            (shape((count, hidden), F32), shape((count, hidden), F32), shape((count, hidden))),
+            (HBM,) * 3,
+            [
+                pltpu.VMEM((count, hidden), F32), pltpu.VMEM((count, hidden), F32),
+                pltpu.VMEM((count, hidden), BF16), matrix, matrix, tiles, rows,
+                pltpu.SemaphoreType.DMA((5,)),
+            ],
+            2 * mat,
+            5_000_000,
+            {3 + n: n for n in range(len(made))},
+        )
+
+    early = forwarded(0, gate, up)
     back_send, dy_rows1, activ1 = call(
         upper_kernel,
-        (arrived, gate, other_gate, up, other_up, own_dt, other_dt, own_gut, other_gut),
-        [INPLACE] + [HBM] * 8,
+        (
+            arrived, gate, other_gate, up, other_up, own_dt, other_dt, own_gut, other_gut,
+            early[2],
+        ),
+        [INPLACE] + [HBM] * 9,
         (shape(flat), shape((count, width)), shape((count, hidden))),
         (HBM,) * 3,
         [
@@ -447,20 +470,7 @@
         return exchanged(block.reshape(experts, CAP, depth, LANES)).reshape(flat)
 
     back = returned(back_send)
-    act0, slope0, activ0 = call(
-        forward_kernel,
-        (arrived, gate, other_gate, up, other_up),
-        [INPLACE] + [HBM] * 4,
-        (shape((count, hidden), F32), shape((count, hidden), F32), shape((count, hidden))),
-        (HBM,) * 3,
-        [
-            pltpu.VMEM((count, hidden), F32), pltpu.VMEM((count, hidden), F32),
-            pltpu.VMEM((count, hidden), BF16), matrix, matrix, tiles, rows,
-            pltpu.SemaphoreType.DMA((5,)),
-        ],
-        2 * mat,
-        5_000_000,
-    )
+    act0, slope0, activ0 = forwarded(1, other_gate, other_up, early)
     basis1 = jnp.where(upper, basis, other_basis)
     basis0 = jnp.where(upper, other_basis, basis)
     rotated1 = jnp.dot(activ1, basis1, preferred_element_type=F32).astype(BF16)

time: 229 us -> 221 us (0.965)
  waiting for transfers between devices: 86.9 us -> 76.6 us
  starting transfers between devices: 53.1 us -> 61.4 us
  blocking collectives: 35.4 us -> 31.5 us
    all_to_all x3, waiting for transfers between devices: 78.3 us -> 68.2 us  [exchanged(): lax.all_to_all(block, 'expert', split_axis=0, concat_axis=0, tiled=True)]
    ppermute x10, starting transfers between devices: 21.2 us -> 29.4 us  [swapped(): return lax.ppermute(block, 'segment', [(0, 1), (1, 0)])]
    all_to_all x1, blocking collectives: 35.4 us -> 31.5 us  [exchanged(): lax.all_to_all(block, 'expert', split_axis=0, concat_axis=0, tiled=True)]
    pallas_call x10 -> x11, Pallas kernels: 38.1 us -> 38.4 us  [call(): pl.pallas_call(kernel, in_specs=in_specs, out_shape=tuple((pltpu.HBM(out....]
  transfers between devices with their start and end apart: 13 -> 13, of which waited for: 10 -> 10; matrix products, arithmetic and copies ran while one was open for 5% -> 4% of each run, Pallas kernels for 6% -> 6%
where the time goes in v5:
time: 221 us
  waiting for transfers between devices  76.6 us (35%)
  starting transfers between devices  61.4 us (28%)
  Pallas kernels  38.4 us (17%)
  blocking collectives  31.5 us (14%)
  matrix products  5.43 us (2%)
  other arithmetic  3.21 us (1%)
  local copies, waits for them, and re-layouts  2.91 us (1%)
    all_to_all x3, waiting for transfers between devices, exchanged(): lax.all_to_all(block, 'expert', split_axis=0, concat_axis=0, tiled=True)  68.2 us
    pallas_call x11, Pallas kernels, call(): pl.pallas_call(kernel, in_specs=in_specs, out_shape=tuple((pltpu.HBM(out....  38.4 us
    all_to_all x3, starting transfers between devices, exchanged(): lax.all_to_all(block, 'expert', split_axis=0, concat_axis=0, tiled=True)  31.9 us
    all_to_all x1, blocking collectives, exchanged(): lax.all_to_all(block, 'expert', split_axis=0, concat_axis=0, tiled=True)  31.5 us
    ppermute x10, starting transfers between devices, swapped(): return lax.ppermute(block, 'segment', [(0, 1), (1, 0)])  29.4 us
    ppermute x10, waiting for transfers between devices, swapped(): return lax.ppermute(block, 'segment', [(0, 1), (1, 0)])  8.43 us
  transfers between devices with their start and end apart: 13, of which 10 were waited for; matrix products, arithmetic and copies ran while one was open for 4% of the time, Pallas kernels for 6%

profile of v5, /device:TPU:1, one launch (start us, length us, event | category | flops | bytes accessed | tf_op | source)
XLA Modules:
  0.0 220.5 jit_solution(11649378599594442090)
XLA Ops:
  0.6 1.0 dynamic-slice_bitcast_fusion
  1.6 3.3 %collective-permute-start.2 = (bf16[64,2048]{1,0:T(8,128)(2,1)S(1)}, bf16[64,2048]{1,0:T(8,128)(2,1)S(1)}, u32[]{:S(2)}, u32[]{:S(2)}) collective-permute-start(bf16[64,2048]{1,0:T(8,128)(2,1)S(1)} %dynamic-slice_bitcast_fusion), channel_id=1, source_target_pairs={{0,128},{128,0},{1,129},{129,1},{2,130},{130,2},{3,131},{131,3},{4... | collective-permute-start | bytes 786440 | tf_op jit(solution)/shard_map/ppermute | solution.py:347
  4.9 1.0 convert_reduce_fusion
  6.0 0.7 minimum_add_fusion.own_slots
  7.2 0.6 collective-permute-done.other_slots
  8.2 0.7 copy-done.8
  8.9 5.6 %shard_map.113 = (bf16[128,6,16,128]{3,2,1,0:T(8,128)(2,1)}, bf16[64,16,128]{2,1,0:T(8,128)(2,1)}) custom-call(s32[2,2,64]{2,1,0:T(2,128)S(1)} %minimum_add_fusion.own_slots, s32[2,2,64]{2,1,0:T(2,128)S(1)} %collective-permute-done.other_slots, f32[2,2,64]{2,1,0:T(2,128)S(1)} %bitcast.39, f32[2,2,64]{2,1,0:T(2,128)S(1)} %collective-permute-done.1.other_w, ...), custom_call_target="tpu_custom_call" | custom-call | flops 1000000 | bytes 5000000 | tf_op jit(solution)/shard_map/pallas_call | solution.py:331
  14.5 13.8 %all-to-all-start = ((bf16[128,6,16,128]{3,2,1,0:T(8,128)(2,1)}), bf16[128,6,16,128]{3,2,1,0:T(8,128)(2,1)S(1)}, u32[]{:S(2)}, u32[]{:S(2)}) async-start(bf16[128,6,16,128]{3,2,1,0:T(8,128)(2,1)} %get-tuple-element.30), calls=%async_computation | async-start | bytes 6291456 | tf_op jit(solution)/shard_map/all_to_all | solution.py:351
  28.3 4.0 %collective-permute-start.3 = (bf16[2048,384]{1,0:T(8,128)(2,1)}, bf16[2048,384]{1,0:T(8,128)(2,1)S(1)}, u32[]{:S(2)}, u32[]{:S(2)}) collective-permute-start(bf16[2048,384]{1,0:T(8,128)(2,1)} %bitcast.42), channel_id=1, source_target_pairs={{0,128},{128,0},{1,129},{129,1},{2,130},{130,2},{3,131},{131,3},{4... | collective-permute-start | bytes 4718600 | tf_op jit(solution)/shard_map/ppermute | solution.py:347
  32.8 4.6 %shard_map.114 = (bf16[768,2048]{1,0:T(8,128)(2,1)}, bf16[2048,384]{1,0:T(8,128)(2,1)}) custom-call(bf16[2048,384]{1,0:T(8,128)(2,1)} %bitcast.43, bf16[2048,384]{1,0:T(8,128)(2,1)} %bitcast.48, bf16[384,2048]{1,0:T(8,128)(2,1)} %bitcast.53, bf16[768,2048]{1,0:T(8,128)(2,1)} %get-tuple-element.31.refs_0_, ...), custom_call_target="tpu_custom_call", output_to_operand_aliasing={{0}: (3, {}), {1}: (4, {})} | custom-call | flops 1000000 | bytes 9000000 | tf_op jit(solution)/shard_map/pallas_call | solution.py:331
  37.8 2.2 %collective-permute-done.5.down = bf16[384,2048]{1,0:T(8,128)(2,1)S(1)} collective-permute-done((bf16[384,2048]{1,0:T(8,128)(2,1)}, bf16[384,2048]{1,0:T(8,128)(2,1)S(1)}, u32[]{:S(2)}, u32[]{:S(2)}) %collective-permute-start.5) | collective-permute-done | bytes 1572896 | tf_op jit(solution)/shard_map/ppermute | solution.py:347
  40.0 1.2 copy-done.5
  41.2 4.5 %shard_map.115 = (bf16[768,2048]{1,0:T(8,128)(2,1)}, bf16[2048,384]{1,0:T(8,128)(2,1)}) custom-call(bf16[2048,384]{1,0:T(8,128)(2,1)} %copy-done.2, bf16[2048,384]{1,0:T(8,128)(2,1)} %copy-done.3, bf16[384,2048]{1,0:T(8,128)(2,1)} %copy-done.5), custom_call_target="tpu_custom_call" | custom-call | flops 1000000 | bytes 9000000 | tf_op jit(solution)/shard_map/pallas_call | solution.py:331
  45.7 51.5 %all-to-all-done.arrived = bf16[128,6,16,128]{3,2,1,0:T(8,128)(2,1)S(1)} async-done(((bf16[128,6,16,128]{3,2,1,0:T(8,128)(2,1)}), bf16[128,6,16,128]{3,2,1,0:T(8,128)(2,1)S(1)}, u32[]{:S(2)}, u32[]{:S(2)}) %all-to-all-start) | async-done | bytes 3145760 | tf_op jit(solution)/shard_map/all_to_all | solution.py:351
  97.3 7.3 %shard_map.117 = (bf16[256,16,128]{2,1,0:T(8,128)(2,1)}, bf16[256,2048]{1,0:T(8,128)(2,1)}, bf16[256,384]{1,0:T(8,128)(2,1)}) custom-call(bf16[128,6,16,128]{3,2,1,0:T(8,128)(2,1)S(1)} %all-to-all-done.arrived, bf16[2048,384]{1,0:T(8,128)(2,1)} %bitcast.45, bf16[2048,384]{1,0:T(8,128)(2,1)} %copy-done.2, bf16[2048,384]{1,0:T(8,128)(2,1)} %bitcast.50, ...), custom_call_target="tpu_custom_call" | custom-call | flops 2013265920 | bytes 9000000 | tf_op jit(solution)/shard_map/pallas_call | solution.py:331
  104.6 31.5 %all_to_all.20 = bf16[128,2,16,128]{3,2,1,0:T(8,128)(2,1)S(1)} all-to-all(bf16[128,2,16,128]{3,2,1,0:T(8,128)(2,1)} %bitcast.57), channel_id=1, replica_groups=mesh['segment'=2,'expert'=128] {'expert'}, dimensions={0} | all-to-all | bytes 2097152 | tf_op jit(solution)/shard_map/all_to_all | solution.py:351
  136.1 2.6 %shard_map.118 = (bf16[256,16,128]{2,1,0:T(8,128)(2,1)}, bf16[64,16,128]{2,1,0:T(8,128)(2,1)S(1)}) custom-call(s32[2,2,64]{2,1,0:T(2,128)S(1)} %minimum_add_fusion.own_slots, s32[2,2,64]{2,1,0:T(2,128)S(1)} %collective-permute-done.other_slots, f32[2,2,64]{2,1,0:T(2,128)S(1)} %bitcast.40, f32[2,2,64]{2,1,0:T(2,128)S(1)} %collective-permute-done.1.other_w, ...), custom_call_target="tpu_custom_call" | custom-call | flops 1000000 | bytes 3000000 | tf_op jit(solution)/shard_map/pallas_call | solution.py:331
  138.7 9.3 %all-to-all-start.2 = ((bf16[128,2,16,128]{3,2,1,0:T(8,128)(2,1)}), bf16[128,2,16,128]{3,2,1,0:T(8,128)(2,1)}, u32[]{:S(2)}, u32[]{:S(2)}) async-start(bf16[128,2,16,128]{3,2,1,0:T(8,128)(2,1)} %bitcast.56), calls=%async_computation.2 | async-start | bytes 2097152 | tf_op jit(solution)/shard_map/all_to_all | solution.py:351
  148.0 4.2 %shard_map.119 = (f32[256,384]{1,0:T(8,128)}, f32[256,384]{1,0:T(8,128)}, bf16[256,384]{1,0:T(8,128)(2,1)}) custom-call(bf16[128,6,16,128]{3,2,1,0:T(8,128)(2,1)S(1)} %all-to-all-done.arrived, bf16[2048,384]{1,0:T(8,128)(2,1)} %copy-done.2, bf16[2048,384]{1,0:T(8,128)(2,1)} %copy-done.3, ...), custom_call_target="tpu_custom_call", output_to_operand_aliasing={{0}: (3, {}), {1}: (4, {}), {2}: (5, {})} | custom-call | flops 805306368 | bytes 5000000 | tf_op jit(solution)/shard_map/pallas_call | solution.py:331
  152.2 16.2 %all-to-all-done.2 = bf16[128,2,16,128]{3,2,1,0:T(8,128)(2,1)} async-done(((bf16[128,2,16,128]{3,2,1,0:T(8,128)(2,1)}), bf16[128,2,16,128]{3,2,1,0:T(8,128)(2,1)}, u32[]{:S(2)}, u32[]{:S(2)}) %all-to-all-start.2) | async-done | bytes 1048608 | tf_op jit(solution)/shard_map/all_to_all | solution.py:351
  168.4 6.6 %shard_map.120 = (bf16[256,16,128]{2,1,0:T(8,128)(2,1)}, bf16[256,2048]{1,0:T(8,128)(2,1)}) custom-call(bf16[256,16,128]{2,1,0:T(8,128)(2,1)} %bitcast.14.dy, f32[256,384]{1,0:T(8,128)} %get-tuple-element.42.act_in, f32[256,384]{1,0:T(8,128)} %get-tuple-element.43.slope_in, bf16[2048,384]{1,0:T(8,128)(2,1)} %get-tuple-element.32.own_dt, ...), custom_call_target="tpu_custom_call" | custom-call | flops 1207959552 | bytes 8000000 | tf_op jit(solution)/shard_map/pallas_call | solution.py:331
  175.0 8.9 %all-to-all-start.3 = ((bf16[128,2,16,128]{3,2,1,0:T(8,128)(2,1)}), bf16[128,2,16,128]{3,2,1,0:T(8,128)(2,1)S(1)}, u32[]{:S(2)}, u32[]{:S(2)}) async-start(bf16[128,2,16,128]{3,2,1,0:T(8,128)(2,1)} %bitcast.55), calls=%async_computation.3 | async-start | bytes 2097152 | tf_op jit(solution)/shard_map/all_to_all | solution.py:351
  183.9 1.5 broadcast_select_fusion.1
  185.4 8.9 %collective-permute-start.8 = (bf16[256,2048]{1,0:T(8,128)(2,1)S(1)}, bf16[256,2048]{1,0:T(8,128)(2,1)S(1)}, u32[]{:S(2)}, u32[]{:S(2)}) collective-permute-start(bf16[256,2048]{1,0:T(8,128)(2,1)S(1)} %get-tuple-element.56), channel_id=1, source_target_pairs={{0,128},{128,0},{1,129},{129,1},{2,130},{130,2},{3,131},{131,3},{4... | collective-permute-start | bytes 3145736 | tf_op jit(solution)/shard_map/ppermute | solution.py:347
  194.5 2.6 %collective-permute-done.6 = bf16[384,384]{1,0:T(8,128)(2,1)S(1)} collective-permute-done((bf16[384,384]{1,0:T(8,128)(2,1)S(1)}, bf16[384,384]{1,0:T(8,128)(2,1)S(1)}, u32[]{:S(2)}, u32[]{:S(2)}) %collective-permute-start.6) | collective-permute-done | bytes 294944 | tf_op jit(solution)/shard_map/ppermute | solution.py:347
  198.1 1.1 collective-permute-done.7
  199.2 2.2 multiply_convert_fusion.1
  201.4 2.7 %convolution_multiply_fusion = f32[384,2048]{1,0:T(8,128)} fusion(bf16[256,2048]{1,0:T(8,128)(2,1)S(1)} %collective-permute-done.8, bf16[256,2048]{1,0:T(8,128)(2,1)S(1)} %get-tuple-element.55, bf16[256,384]{1,0:T(8,128)(2,1)S(1)} %collective-permute-done.7, bf16[256,384]{1,0:T(8,128)(2,1)S(1)} %get-tuple-element.57), kind=kOutput, calls=%fused_computation.2 | convolution fusion | flops 813563904 | bytes 5636096 | tf_op jit(solution)/shard_map/dot_general | solution.py:524
  204.6 2.3 %shard_map.121 = (bf16[2,64,2048]{2,1,0:T(8,128)(2,1)}, bf16[64,2048]{1,0:T(8,128)(2,1)S(1)}) custom-call(s32[2,2,64]{2,1,0:T(2,128)S(1)} %minimum_add_fusion.own_slots, s32[2,2,64]{2,1,0:T(2,128)S(1)} %collective-permute-done.other_slots, bf16[256,16,128]{2,1,0:T(8,128)(2,1)S(1)} %bitcast.36, bf16[64,16,128]{2,1,0:T(8,128)(2,1)S(1)} %get-tuple-element.50.upstream), custom_call_target="tpu_custom_call" | custom-call | flops 1000000 | bytes 2000000 | tf_op jit(solution)/shard_map/pallas_call | solution.py:331
  206.9 11.6 %collective-permute-start.9 = (bf16[64,2048]{1,0:T(8,128)(2,1)S(1)}, bf16[64,2048]{1,0:T(8,128)(2,1)S(1)}, u32[]{:S(2)}, u32[]{:S(2)}) collective-permute-start(bf16[64,2048]{1,0:T(8,128)(2,1)S(1)} %get-tuple-element.51), channel_id=1, source_target_pairs={{0,128},{128,0},{1,129},{129,1},{2,130},{130,2},{3,131},{131,3},{4... | collective-permute-start | bytes 786440 | tf_op jit(solution)/shard_map/ppermute | solution.py:347
  218.5 1.2 collective-permute-done.9.came
  219.6 0.7 shard_map.122
  (34 shorter events, 3.6 us)
Async XLA Ops:
  0.6 8.3 %copy-start.1 = (f32[1,2,64,2]{2,3,1,0:T(2,128)S(1)}, f32[1,2,64,2]{2,3,1,0:T(2,128)}, u32[]{:S(2)}) copy-start(f32[1,2,64,2]{2,3,1,0:T(2,128)} %param.12) | copy-start | bytes 3076
  1.6 6.6 %collective-permute-start.2 = (bf16[64,2048]{1,0:T(8,128)(2,1)S(1)}, bf16[64,2048]{1,0:T(8,128)(2,1)S(1)}, u32[]{:S(2)}, u32[]{:S(2)}) collective-permute-start(bf16[64,2048]{1,0:T(8,128)(2,1)S(1)} %dynamic-slice_bitcast_fusion), channel_id=1, source_target_pairs={{0,128},{128,0},{1,129},{129,1},{2,130},{130,2},{3,131},{131,3},{4... | collective-permute-start | bytes 786440 | tf_op jit(solution)/shard_map/ppermute | solution.py:347
  6.7 1.2 collective-permute-start
  6.7 1.5 collective-permute-start.1
  8.2 0.7 copy-start.8
  14.5 82.7 %all-to-all-start = ((bf16[128,6,16,128]{3,2,1,0:T(8,128)(2,1)}), bf16[128,6,16,128]{3,2,1,0:T(8,128)(2,1)S(1)}, u32[]{:S(2)}, u32[]{:S(2)}) async-start(bf16[128,6,16,128]{3,2,1,0:T(8,128)(2,1)} %get-tuple-element.30), calls=%async_computation | async-start | bytes 6291456 | tf_op jit(solution)/shard_map/all_to_all | solution.py:351
  28.3 9.1 %collective-permute-start.3 = (bf16[2048,384]{1,0:T(8,128)(2,1)}, bf16[2048,384]{1,0:T(8,128)(2,1)S(1)}, u32[]{:S(2)}, u32[]{:S(2)}) collective-permute-start(bf16[2048,384]{1,0:T(8,128)(2,1)} %bitcast.42), channel_id=1, source_target_pairs={{0,128},{128,0},{1,129},{129,1},{2,130},{130,2},{3,131},{131,3},{4... | collective-permute-start | bytes 4718600 | tf_op jit(solution)/shard_map/ppermute | solution.py:347
  32.3 5.5 %collective-permute-start.4 = (bf16[2048,384]{1,0:T(8,128)(2,1)}, bf16[2048,384]{1,0:T(8,128)(2,1)S(1)}, u32[]{:S(2)}, u32[]{:S(2)}) collective-permute-start(bf16[2048,384]{1,0:T(8,128)(2,1)} %bitcast.47), channel_id=1, source_target_pairs={{0,128},{128,0},{1,129},{129,1},{2,130},{130,2},{3,131},{131,3},{4... | collective-permute-start | bytes 4718600 | tf_op jit(solution)/shard_map/ppermute | solution.py:347
  32.4 7.6 %collective-permute-start.5 = (bf16[384,2048]{1,0:T(8,128)(2,1)}, bf16[384,2048]{1,0:T(8,128)(2,1)S(1)}, u32[]{:S(2)}, u32[]{:S(2)}) collective-permute-start(bf16[384,2048]{1,0:T(8,128)(2,1)} %bitcast.52), channel_id=1, source_target_pairs={{0,128},{128,0},{1,129},{129,1},{2,130},{130,2},{3,131},{131,3},{4... | collective-permute-start | bytes 4718600 | tf_op jit(solution)/shard_map/ppermute | solution.py:347
  37.4 2.6 %copy-start.2 = (bf16[2048,384]{1,0:T(8,128)(2,1)}, bf16[2048,384]{1,0:T(8,128)(2,1)S(1)}, u32[]{:S(2)}) copy-start(bf16[2048,384]{1,0:T(8,128)(2,1)S(1)} %collective-permute-done.3.gate.other_gate.matrix_gate) | copy-start | bytes 4718596
  37.8 2.3 %copy-start.3 = (bf16[2048,384]{1,0:T(8,128)(2,1)}, bf16[2048,384]{1,0:T(8,128)(2,1)S(1)}, u32[]{:S(2)}) copy-start(bf16[2048,384]{1,0:T(8,128)(2,1)S(1)} %collective-permute-done.4.up.other_up.matrix_up) | copy-start | bytes 4718596
  40.0 1.2 copy-start.5
  97.3 38.9 %copy-start = (bf16[64,16,128]{2,1,0:T(8,128)(2,1)S(1)}, bf16[64,16,128]{2,1,0:T(8,128)(2,1)}, u32[]{:S(2)}) copy-start(bf16[64,16,128]{2,1,0:T(8,128)(2,1)} %get-tuple-element.38.upstream) | copy-start | bytes 786436
  138.7 29.7 %all-to-all-start.2 = ((bf16[128,2,16,128]{3,2,1,0:T(8,128)(2,1)}), bf16[128,2,16,128]{3,2,1,0:T(8,128)(2,1)}, u32[]{:S(2)}, u32[]{:S(2)}) async-start(bf16[128,2,16,128]{3,2,1,0:T(8,128)(2,1)} %bitcast.56), calls=%async_computation.2 | async-start | bytes 2097152 | tf_op jit(solution)/shard_map/all_to_all | solution.py:351
  168.4 15.5 %copy-start.6 = (bf16[256,2048]{1,0:T(8,128)(2,1)S(1)}, bf16[256,2048]{1,0:T(8,128)(2,1)}, u32[]{:S(2)}) copy-start(bf16[256,2048]{1,0:T(8,128)(2,1)} %get-tuple-element.47) | copy-start | bytes 3145732
  175.0 19.4 %copy-start.7 = (bf16[1,1,384,384]{3,2,1,0:T(8,128)(2,1)S(1)}, bf16[1,1,384,384]{3,2,1,0:T(8,128)(2,1)}, u32[]{:S(2)}) copy-start(bf16[1,1,384,384]{3,2,1,0:T(8,128)(2,1)} %param.16) | copy-start | bytes 884740
  175.0 22.1 %copy-start.4 = (bf16[256,384]{1,0:T(8,128)(2,1)S(1)}, bf16[256,384]{1,0:T(8,128)(2,1)}, u32[]{:S(2)}) copy-start(bf16[256,384]{1,0:T(8,128)(2,1)} %get-tuple-element.46) | copy-start | bytes 589828
  175.0 22.3 %copy-start.9 = (bf16[256,384]{1,0:T(8,128)(2,1)S(1)}, bf16[256,384]{1,0:T(8,128)(2,1)}, u32[]{:S(2)}) copy-start(bf16[256,384]{1,0:T(8,128)(2,1)} %get-tuple-element.45) | copy-start | bytes 589828
  175.0 29.6 %all-to-all-start.3 = ((bf16[128,2,16,128]{3,2,1,0:T(8,128)(2,1)}), bf16[128,2,16,128]{3,2,1,0:T(8,128)(2,1)S(1)}, u32[]{:S(2)}, u32[]{:S(2)}) async-start(bf16[128,2,16,128]{3,2,1,0:T(8,128)(2,1)} %bitcast.55), calls=%async_computation.3 | async-start | bytes 2097152 | tf_op jit(solution)/shard_map/all_to_all | solution.py:351
  185.4 13.8 %collective-permute-start.8 = (bf16[256,2048]{1,0:T(8,128)(2,1)S(1)}, bf16[256,2048]{1,0:T(8,128)(2,1)S(1)}, u32[]{:S(2)}, u32[]{:S(2)}) collective-permute-start(bf16[256,2048]{1,0:T(8,128)(2,1)S(1)} %get-tuple-element.56), channel_id=1, source_target_pairs={{0,128},{128,0},{1,129},{129,1},{2,130},{130,2},{3,131},{131,3},{4... | collective-permute-start | bytes 3145736 | tf_op jit(solution)/shard_map/ppermute | solution.py:347
  194.4 2.7 %collective-permute-start.6 = (bf16[384,384]{1,0:T(8,128)(2,1)S(1)}, bf16[384,384]{1,0:T(8,128)(2,1)S(1)}, u32[]{:S(2)}, u32[]{:S(2)}) collective-permute-start(bf16[384,384]{1,0:T(8,128)(2,1)S(1)} %bitcast.59), channel_id=1, source_target_pairs={{0,128},{128,0},{1,129},{129,1},{2,130},{130,2},{3,131},{131,3},{4... | collective-permute-start | bytes 884744 | tf_op jit(solution)/shard_map/ppermute | solution.py:347
  197.7 1.5 collective-permute-start.7
  206.9 12.8 %collective-permute-start.9 = (bf16[64,2048]{1,0:T(8,128)(2,1)S(1)}, bf16[64,2048]{1,0:T(8,128)(2,1)S(1)}, u32[]{:S(2)}, u32[]{:S(2)}) collective-permute-start(bf16[64,2048]{1,0:T(8,128)(2,1)S(1)} %get-tuple-element.51), channel_id=1, source_target_pairs={{0,128},{128,0},{1,129},{129,1},{2,130},{130,2},{3,131},{131,3},{4... | collective-permute-start | bytes 786440 | tf_op jit(solution)/shard_map/ppermute | solution.py:347

commit v6 on v5

--- a/solution.py
+++ b/solution.py
@@ -73,7 +73,7 @@
 
 def dispatch_kernel(
     own_slots, other_slots, own_w, other_w, own_x, other_x, grads, after, sent, tiles_out,
-    send, grad_tiles, own, other, grad, x_upper, x_lower, g_tiles, sems,
+    send, grad_tiles, own, grad, x_upper, x_lower, g_tiles, sems,
 ):
     tokens, width = grad.shape
     depth = width // LANES
@@ -82,13 +82,12 @@
     slot = slot_reader(own_slots, other_slots)
     copies = [
         fetch(own_x.at[segment], own, sems.at[0]),
-        fetch(other_x, other, sems.at[1]),
         fetch(grads.at[segment], grad, sems.at[2]),
     ]
     clear(send, send.shape[0])
     for copy in copies:
         copy.wait()
-    mine, theirs = own[...].astype(F32), other[...].astype(F32)
+    mine, theirs = own[...].astype(F32), other_x[...].astype(F32)
     rows_to_tiles(jnp.where(upper, mine, theirs), x_upper, tokens, depth)
     saves = []
 
@@ -135,7 +134,7 @@
 
 
 def relay_kernel(
-    own_slots, other_slots, own_w, other_w, back, upstream, sent, grad_out, send, sems
+    own_slots, other_slots, own_w, other_w, back, upstream, sent, grad_out, send, grads, sems
 ):
     tokens = upstream.shape[0]
     segment = lax.axis_index("segment")
@@ -148,7 +147,7 @@
         for k in range(2):
             total = total + back[slot(1, k, t)].astype(F32)
         rounded = total.astype(BF16)
-        grad_out[t] = rounded
+        grads[t] = rounded
         g = rounded.astype(F32)
         for k in range(2):
             weight = jnp.where(upper, other_w[segment, k, t], own_w[segment, k, t])
@@ -156,32 +155,52 @@
         return carry
 
     lax.fori_loop(0, tokens, token, 0, unroll=4)
-    fetch(send, sent, sems.at[0]).wait()
-
-
-def finish_kernel(own_slots, other_slots, back, upstream, out, away, keep, low, up, sems):
-    tokens, depth = upstream.shape[0], upstream.shape[1]
-    upper = on_core(1)
-    slot = slot_reader(own_slots, other_slots)
-
-    def token(t, carry):
-        at = pl.ds(pl.multiple_of(t * depth, depth), depth)
-        g = upstream[t].astype(F32)
-        up[at, :] = g
-        total = g
-        for k in range(2):
-            total = total + back[slot(0, k, t)].astype(F32)
-        low[at, :] = total
-        return carry
-
-    lax.fori_loop(0, tokens, token, 0, unroll=4)
-    for j in range(depth):
-        columns = slice(j * LANES, (j + 1) * LANES)
-        high = up[pl.ds(j, tokens, stride=depth), :]
-        down = low[pl.ds(j, tokens, stride=depth), :]
-        keep[:, columns] = jnp.where(upper, high, down).astype(BF16)
-        away[:, columns] = jnp.where(upper, down, high).astype(BF16)
-    fetch(keep, out.at[lax.axis_index("segment")], sems.at[0]).wait()
+    saves = [fetch(send, sent, sems.at[0]), fetch(grads, grad_out, sems.at[1])]
+    for copy in saves:
+        copy.wait()
+
+
+def stow_kernel(upstream, out, away, block, tiles, rows, sems):
+    tokens, depth = block.shape[:2]
+    fetch(upstream, block, sems.at[0]).wait()
+    tiles[...] = block[...].astype(F32).reshape(tiles.shape)
+    tiles_to_rows(tiles, rows, tokens, depth)
+
+    @pl.when(on_core(1))
+    def _():
+        fetch(rows, out.at[1], sems.at[1]).wait()
+
+    @pl.when(on_core(0))
+    def _():
+        fetch(rows, away, sems.at[1]).wait()
+
+
+def finish_kernel(core, own_in, other_in, back, upstream, made, out, *scratch):
+    own_slots, other_slots, block, tiles, rows, sems = scratch
+    tokens, depth = block.shape[:2]
+
+    def work():
+        copies = [
+            fetch(own_in, own_slots, sems.at[0]),
+            fetch(other_in, other_slots, sems.at[1]),
+            fetch(upstream, block, sems.at[2]),
+        ]
+        for copy in copies:
+            copy.wait()
+        slots = own_slots if core == 0 else other_slots
+
+        def token(t, carry):
+            total = block[t].astype(F32)
+            for k in range(2):
+                total = total + back[slots[core, k, t]].astype(F32)
+            tiles[pl.ds(pl.multiple_of(t * depth, depth), depth), :] = total
+            return carry
+
+        lax.fori_loop(0, tokens, token, 0, unroll=4)
+        tiles_to_rows(tiles, rows, tokens, depth)
+        fetch(rows, out if core == 1 else out.at[0], sems.at[3]).wait()
+
+    pl.when(on_core(core))(work)
 
 
 def join_kernel(came, partial, out, sems):
@@ -295,15 +314,27 @@
 
 
 def lower_kernel(
-    dy, act_in, slope_in, own_dt, other_dt, own_gut, other_gut, sent, dy_out,
-    act, slope, down_t, gate_up_t, tiles, dy_rows, send, sems,
+    dy_in, act_in, slope_in, own_dt, other_dt, own_gut, other_gut, sent, dy_out,
+    dy, act, slope, down_t, gate_up_t, tiles, dy_rows, send, sems,
 ):
     mine = on_core(0)
+    count, depth = send.shape[:2]
+    pieces = 4
+    part = count // pieces
+    arriving = [
+        fetch(dy_in.at[pl.ds(n * part, part)], dy.at[pl.ds(n * part, part)], sems.at[9 + n])
+        for n in range(pieces)
+    ]
     down_copy = fetch_one_of(mine, own_dt, other_dt, down_t, sems.at[0])
     act_copy = fetch(act_in, act, sems.at[1])
     slope_copy = fetch(slope_in, slope, sems.at[2])
     back_copy = fetch_one_of(mine, own_gut, other_gut, gate_up_t, sems.at[3])
-    untile(dy[...], tiles, dy_rows, send.shape[1])
+    for n, copy in enumerate(arriving):
+        copy.wait()
+        tiles[n * part * depth : (n + 1) * part * depth, :] = (
+            dy[n * part : (n + 1) * part].astype(F32).reshape(part * depth, LANES)
+        )
+    tiles_to_rows(tiles, dy_rows, count, depth)
     saves = [fetch(dy_rows, dy_out, sems.at[4])]
     down_copy.wait()
     grad_act = jnp.dot(dy_rows[...], down_t[...], preferred_element_type=F32)
@@ -404,14 +435,14 @@
     send, grad_tiles = call(
         dispatch_kernel,
         (own_slots, other_slots, own_w, other_w, saved_input[0], other_x, out_grad, early_dt),
-        [SMEM] * 4 + [HBM] * 4,
+        [SMEM] * 4 + [HBM, INPLACE, HBM, HBM],
         (shape((experts, 3 * CAP, depth, LANES)), shape((tokens, depth, LANES))),
         (HBM,) * 2,
         [
             pltpu.VMEM((experts, 3 * CAP, depth, LANES), BF16),
             pltpu.VMEM((tokens, depth, LANES), BF16),
         ]
-        + [row_block] * 3
+        + [row_block] * 2
         + [pltpu.VMEM((tile_rows, LANES), F32)] * 3
         + [pltpu.SemaphoreType.DMA((7,))],
         1_000_000,
@@ -481,22 +512,38 @@
         (own_slots, other_slots, own_w, other_w, back, grad_tiles),
         [SMEM] * 4 + [INPLACE, VMEM],
         (shape(flat), shape((tokens, depth, LANES))),
-        (HBM, VMEM),
-        [flat_scratch, pltpu.SemaphoreType.DMA((1,))],
+        (HBM, HBM),
+        [
+            flat_scratch, pltpu.VMEM((tokens, depth, LANES), BF16),
+            pltpu.SemaphoreType.DMA((2,)),
+        ],
         1_000_000,
         3_000_000,
+    )
+    own_grads, away = call(
+        stow_kernel,
+        (grad1,),
+        [HBM],
+        (shape((micros, tokens, width)), shape((tokens, width))),
+        (HBM,) * 2,
+        [
+            pltpu.VMEM((tokens, depth, LANES), BF16), pltpu.VMEM((tile_rows, LANES), F32),
+            row_block, pltpu.SemaphoreType.DMA((2,)),
+        ],
+        1_000_000,
+        1_000_000,
     )
     dy = returned(dy_send)
     back_send0, dy_rows0 = call(
         lower_kernel,
         (dy, act0, slope0, own_dt, other_dt, own_gut, other_gut),
-        [INPLACE] + [HBM] * 6,
+        [HBM] * 7,
         (shape(flat), shape((count, width))),
         (HBM,) * 2,
         [
-            pltpu.VMEM((count, hidden), F32), pltpu.VMEM((count, hidden), F32),
+            flat_scratch, pltpu.VMEM((count, hidden), F32), pltpu.VMEM((count, hidden), F32),
             matrix, pltpu.VMEM((2 * hidden, width), BF16), tiles, rows, flat_scratch,
-            pltpu.SemaphoreType.DMA((9,)),
+            pltpu.SemaphoreType.DMA((13,)),
         ],
         3 * mat,
         8_000_000,
@@ -528,21 +575,32 @@
         (back0, rotated_grad, ekfac_scales)
     )
 
-    own_grads, away = call(
-        finish_kernel,
-        (own_slots, other_slots, back0, grad1),
-        [SMEM] * 2 + [INPLACE, VMEM],
-        (shape((micros, tokens, width)), shape((tokens, width))),
-        (HBM, VMEM),
-        [row_block]
-        + [pltpu.VMEM((tile_rows, LANES), F32)] * 2
-        + [pltpu.SemaphoreType.DMA((1,))],
-        1_000_000,
-        2_000_000,
-    )
+    def finished(core, made):
+        (out,) = call(
+            functools.partial(finish_kernel, core),
+            (own_slots, other_slots, back0, grad1, made),
+            [HBM, HBM, INPLACE, HBM, HBM],
+            (shape(made.shape),),
+            (HBM,),
+            [
+                pltpu.SMEM((micros, 2, tokens), jnp.int32),
+                pltpu.SMEM((micros, 2, tokens), jnp.int32),
+                pltpu.VMEM((tokens, depth, LANES), BF16),
+                pltpu.VMEM((tile_rows, LANES), F32),
+                row_block,
+                pltpu.SemaphoreType.DMA((4,)),
+            ],
+            3_000_000_000,
+            2_000_000,
+            {4: 0},
+        )
+        return out
+
+    came = swapped(finished(1, away))
+    own_grads = finished(0, own_grads)
     (grads,) = call(
         join_kernel,
-        (swapped(away), own_grads),
+        (came, own_grads),
         [INPLACE, HBM],
         (shape((micros, tokens, width)),),
         (HBM,),

time: 221 us -> 217 us (0.982)
    ppermute x10, starting transfers between devices: 29.4 us -> 27.2 us  [swapped(): return lax.ppermute(block, 'segment', [(0, 1), (1, 0)])]
    pallas_call x11 -> x13, Pallas kernels: 38.4 us -> 39.1 us  [call(): pl.pallas_call(kernel, in_specs=in_specs, out_shape=tuple((pltpu.HBM(out....]
  transfers between devices with their start and end apart: 13 -> 13, of which waited for: 10 -> 8; matrix products, arithmetic and copies ran while one was open for 4% -> 4% of each run, Pallas kernels for 6% -> 7%
where the time goes in v6:
time: 217 us
  waiting for transfers between devices  75 us (35%)
  starting transfers between devices  59.2 us (27%)
  Pallas kernels  39.1 us (18%)
  blocking collectives  31.6 us (15%)
  matrix products  5.41 us (2%)
  other arithmetic  3.08 us (1%)
  local copies, waits for them, and re-layouts  2.21 us (1%)
    all_to_all x3, waiting for transfers between devices, exchanged(): lax.all_to_all(block, 'expert', split_axis=0, concat_axis=0, tiled=True)  67.5 us
    pallas_call x13, Pallas kernels, call(): pl.pallas_call(kernel, in_specs=in_specs, out_shape=tuple((pltpu.HBM(out....  39.1 us
    all_to_all x3, starting transfers between devices, exchanged(): lax.all_to_all(block, 'expert', split_axis=0, concat_axis=0, tiled=True)  31.9 us
    all_to_all x1, blocking collectives, exchanged(): lax.all_to_all(block, 'expert', split_axis=0, concat_axis=0, tiled=True)  31.6 us
    ppermute x10, starting transfers between devices, swapped(): return lax.ppermute(block, 'segment', [(0, 1), (1, 0)])  27.2 us
    ppermute x10, waiting for transfers between devices, swapped(): return lax.ppermute(block, 'segment', [(0, 1), (1, 0)])  7.52 us
  transfers between devices with their start and end apart: 13, of which 8 were waited for; matrix products, arithmetic and copies ran while one was open for 4% of the time, Pallas kernels for 7%

profile of v6, /device:TPU:1, one launch (start us, length us, event | category | flops | bytes accessed | tf_op | source)
XLA Modules:
  0.0 216.7 jit_solution(455623528659461351)
XLA Ops:
  0.6 1.0 dynamic-slice_bitcast_fusion
  1.6 3.3 %collective-permute-start.2 = (bf16[64,2048]{1,0:T(8,128)(2,1)S(1)}, bf16[64,2048]{1,0:T(8,128)(2,1)S(1)}, u32[]{:S(2)}, u32[]{:S(2)}) collective-permute-start(bf16[64,2048]{1,0:T(8,128)(2,1)S(1)} %dynamic-slice_bitcast_fusion), channel_id=1, source_target_pairs={{0,128},{128,0},{1,129},{129,1},{2,130},{130,2},{3,131},{131,3},{4... | collective-permute-start | bytes 786440 | tf_op jit(solution)/shard_map/ppermute | solution.py:378
  4.9 1.0 convert_reduce_fusion
  6.0 0.7 minimum_add_fusion.own_slots.own_in
  6.7 0.5 collective-permute-start.1
  7.2 0.6 collective-permute-done.other_slots.other_in
  8.2 5.6 %shard_map.113 = (bf16[128,6,16,128]{3,2,1,0:T(8,128)(2,1)}, bf16[64,16,128]{2,1,0:T(8,128)(2,1)}) custom-call(s32[2,2,64]{2,1,0:T(2,128)S(1)} %minimum_add_fusion.own_slots.own_in, s32[2,2,64]{2,1,0:T(2,128)S(1)} %collective-permute-done.other_slots.other_in, f32[2,2,64]{2,1,0:T(2,128)S(1)} %bitcast.40, f32[2,2,64]{2,1,0:T(2,128)S(1)} %collective-permute-done.1.other_w, ...), custom_call_target="tpu_custom_call" | custom-call | flops 1000000 | bytes 5000000 | tf_op jit(solution)/shard_map/pallas_call | solution.py:362
  13.8 13.8 %all-to-all-start = ((bf16[128,6,16,128]{3,2,1,0:T(8,128)(2,1)}), bf16[128,6,16,128]{3,2,1,0:T(8,128)(2,1)S(1)}, u32[]{:S(2)}, u32[]{:S(2)}) async-start(bf16[128,6,16,128]{3,2,1,0:T(8,128)(2,1)} %get-tuple-element.30), calls=%async_computation | async-start | bytes 6291456 | tf_op jit(solution)/shard_map/all_to_all | solution.py:382
  27.6 4.1 %collective-permute-start.3 = (bf16[2048,384]{1,0:T(8,128)(2,1)}, bf16[2048,384]{1,0:T(8,128)(2,1)S(1)}, u32[]{:S(2)}, u32[]{:S(2)}) collective-permute-start(bf16[2048,384]{1,0:T(8,128)(2,1)} %bitcast.43), channel_id=1, source_target_pairs={{0,128},{128,0},{1,129},{129,1},{2,130},{130,2},{3,131},{131,3},{4... | collective-permute-start | bytes 4718600 | tf_op jit(solution)/shard_map/ppermute | solution.py:378
  32.2 4.6 %shard_map.114 = (bf16[768,2048]{1,0:T(8,128)(2,1)}, bf16[2048,384]{1,0:T(8,128)(2,1)}) custom-call(bf16[2048,384]{1,0:T(8,128)(2,1)} %bitcast.44, bf16[2048,384]{1,0:T(8,128)(2,1)} %bitcast.49, bf16[384,2048]{1,0:T(8,128)(2,1)} %bitcast.54, bf16[768,2048]{1,0:T(8,128)(2,1)} %get-tuple-element.31.refs_0_, ...), custom_call_target="tpu_custom_call", output_to_operand_aliasing={{0}: (3, {}), {1}: (4, {})} | custom-call | flops 1000000 | bytes 9000000 | tf_op jit(solution)/shard_map/pallas_call | solution.py:362
  37.2 2.2 %collective-permute-done.5.down = bf16[384,2048]{1,0:T(8,128)(2,1)S(1)} collective-permute-done((bf16[384,2048]{1,0:T(8,128)(2,1)}, bf16[384,2048]{1,0:T(8,128)(2,1)S(1)}, u32[]{:S(2)}, u32[]{:S(2)}) %collective-permute-start.5) | collective-permute-done | bytes 1572896 | tf_op jit(solution)/shard_map/ppermute | solution.py:378
  39.4 1.2 copy-done.7
  40.6 4.5 %shard_map.115 = (bf16[768,2048]{1,0:T(8,128)(2,1)}, bf16[2048,384]{1,0:T(8,128)(2,1)}) custom-call(bf16[2048,384]{1,0:T(8,128)(2,1)} %copy-done.4, bf16[2048,384]{1,0:T(8,128)(2,1)} %copy-done.5, bf16[384,2048]{1,0:T(8,128)(2,1)} %copy-done.7), custom_call_target="tpu_custom_call" | custom-call | flops 1000000 | bytes 9000000 | tf_op jit(solution)/shard_map/pallas_call | solution.py:362
  45.1 51.3 %all-to-all-done.arrived = bf16[128,6,16,128]{3,2,1,0:T(8,128)(2,1)S(1)} async-done(((bf16[128,6,16,128]{3,2,1,0:T(8,128)(2,1)}), bf16[128,6,16,128]{3,2,1,0:T(8,128)(2,1)S(1)}, u32[]{:S(2)}, u32[]{:S(2)}) %all-to-all-start) | async-done | bytes 3145760 | tf_op jit(solution)/shard_map/all_to_all | solution.py:382
  96.5 7.3 %shard_map.117 = (bf16[256,16,128]{2,1,0:T(8,128)(2,1)}, bf16[256,2048]{1,0:T(8,128)(2,1)}, bf16[256,384]{1,0:T(8,128)(2,1)}) custom-call(bf16[128,6,16,128]{3,2,1,0:T(8,128)(2,1)S(1)} %all-to-all-done.arrived, bf16[2048,384]{1,0:T(8,128)(2,1)} %bitcast.46, bf16[2048,384]{1,0:T(8,128)(2,1)} %copy-done.4, bf16[2048,384]{1,0:T(8,128)(2,1)} %bitcast.51, ...), custom_call_target="tpu_custom_call" | custom-call | flops 2013265920 | bytes 9000000 | tf_op jit(solution)/shard_map/pallas_call | solution.py:362
  103.8 31.6 %all_to_all.20 = bf16[128,2,16,128]{3,2,1,0:T(8,128)(2,1)S(1)} all-to-all(bf16[128,2,16,128]{3,2,1,0:T(8,128)(2,1)} %bitcast.58), channel_id=1, replica_groups=mesh['segment'=2,'expert'=128] {'expert'}, dimensions={0} | all-to-all | bytes 2097152 | tf_op jit(solution)/shard_map/all_to_all | solution.py:382
  135.4 2.6 %shard_map.118 = (bf16[256,16,128]{2,1,0:T(8,128)(2,1)}, bf16[64,16,128]{2,1,0:T(8,128)(2,1)}) custom-call(s32[2,2,64]{2,1,0:T(2,128)S(1)} %minimum_add_fusion.own_slots.own_in, s32[2,2,64]{2,1,0:T(2,128)S(1)} %collective-permute-done.other_slots.other_in, f32[2,2,64]{2,1,0:T(2,128)S(1)} %bitcast.41, f32[2,2,64]{2,1,0:T(2,128)S(1)} %collective-permute-done.1.other_w, ...), custom_call_target="tpu_custom_call" | custom-call | flops 1000000 | bytes 3000000 | tf_op jit(solution)/shard_map/pallas_call | solution.py:362
  138.1 9.3 %all-to-all-start.2 = ((bf16[128,2,16,128]{3,2,1,0:T(8,128)(2,1)}), bf16[128,2,16,128]{3,2,1,0:T(8,128)(2,1)}, u32[]{:S(2)}, u32[]{:S(2)}) async-start(bf16[128,2,16,128]{3,2,1,0:T(8,128)(2,1)} %bitcast.57), calls=%async_computation.2 | async-start | bytes 2097152 | tf_op jit(solution)/shard_map/all_to_all | solution.py:382
  147.4 4.2 %shard_map.119 = (f32[256,384]{1,0:T(8,128)}, f32[256,384]{1,0:T(8,128)}, bf16[256,384]{1,0:T(8,128)(2,1)}) custom-call(bf16[128,6,16,128]{3,2,1,0:T(8,128)(2,1)S(1)} %all-to-all-done.arrived, bf16[2048,384]{1,0:T(8,128)(2,1)} %copy-done.4, bf16[2048,384]{1,0:T(8,128)(2,1)} %copy-done.5, ...), custom_call_target="tpu_custom_call", output_to_operand_aliasing={{0}: (3, {}), {1}: (4, {}), {2}: (5, {})} | custom-call | flops 805306368 | bytes 5000000 | tf_op jit(solution)/shard_map/pallas_call | solution.py:362
  151.6 16.2 %all-to-all-done.2 = bf16[128,2,16,128]{3,2,1,0:T(8,128)(2,1)} async-done(((bf16[128,2,16,128]{3,2,1,0:T(8,128)(2,1)}), bf16[128,2,16,128]{3,2,1,0:T(8,128)(2,1)}, u32[]{:S(2)}, u32[]{:S(2)}) %all-to-all-start.2) | async-done | bytes 1048608 | tf_op jit(solution)/shard_map/all_to_all | solution.py:382
  167.8 5.4 %shard_map.120 = (bf16[256,16,128]{2,1,0:T(8,128)(2,1)}, bf16[256,2048]{1,0:T(8,128)(2,1)}) custom-call(bf16[256,16,128]{2,1,0:T(8,128)(2,1)} %bitcast.14.dy_in, f32[256,384]{1,0:T(8,128)} %get-tuple-element.42.act_in, f32[256,384]{1,0:T(8,128)} %get-tuple-element.43.slope_in, bf16[2048,384]{1,0:T(8,128)(2,1)} %get-tuple-element.32.own_dt, ...), custom_call_target="tpu_custom_call" | custom-call | flops 1207959552 | bytes 8000000 | tf_op jit(solution)/shard_map/pallas_call | solution.py:362
  173.2 8.9 %all-to-all-start.3 = ((bf16[128,2,16,128]{3,2,1,0:T(8,128)(2,1)}), bf16[128,2,16,128]{3,2,1,0:T(8,128)(2,1)S(1)}, u32[]{:S(2)}, u32[]{:S(2)}) async-start(bf16[128,2,16,128]{3,2,1,0:T(8,128)(2,1)} %bitcast.56), calls=%async_computation.3 | async-start | bytes 2097152 | tf_op jit(solution)/shard_map/all_to_all | solution.py:382
  182.1 1.4 broadcast_select_fusion.1
  183.4 9.0 %collective-permute-start.8 = (bf16[256,2048]{1,0:T(8,128)(2,1)S(1)}, bf16[256,2048]{1,0:T(8,128)(2,1)S(1)}, u32[]{:S(2)}, u32[]{:S(2)}) collective-permute-start(bf16[256,2048]{1,0:T(8,128)(2,1)S(1)} %get-tuple-element.56), channel_id=1, source_target_pairs={{0,128},{128,0},{1,129},{129,1},{2,130},{130,2},{3,131},{131,3},{4... | collective-permute-start | bytes 3145736 | tf_op jit(solution)/shard_map/ppermute | solution.py:378
  192.5 2.6 %collective-permute-done.6 = bf16[384,384]{1,0:T(8,128)(2,1)S(1)} collective-permute-done((bf16[384,384]{1,0:T(8,128)(2,1)S(1)}, bf16[384,384]{1,0:T(8,128)(2,1)S(1)}, u32[]{:S(2)}, u32[]{:S(2)}) %collective-permute-start.6) | collective-permute-done | bytes 294944 | tf_op jit(solution)/shard_map/ppermute | solution.py:378
  196.2 1.9 shard_map.121
  198.1 2.2 multiply_convert_fusion.1
  200.2 2.7 %convolution_multiply_fusion = f32[384,2048]{1,0:T(8,128)} fusion(bf16[256,2048]{1,0:T(8,128)(2,1)S(1)} %collective-permute-done.8, bf16[256,2048]{1,0:T(8,128)(2,1)S(1)} %get-tuple-element.55, bf16[256,384]{1,0:T(8,128)(2,1)S(1)} %collective-permute-done.7, bf16[256,384]{1,0:T(8,128)(2,1)S(1)} %get-tuple-element.57), kind=kOutput, calls=%fused_computation.2 | convolution fusion | flops 813563904 | bytes 5636096 | tf_op jit(solution)/shard_map/dot_general | solution.py:571
  202.9 2.2 %shard_map.122 = bf16[64,2048]{1,0:T(8,128)(2,1)} custom-call(s32[2,2,64]{2,1,0:T(2,128)} %copy-done.1, s32[2,2,64]{2,1,0:T(2,128)} %copy-done.3, bf16[256,16,128]{2,1,0:T(8,128)(2,1)S(1)} %bitcast.37, bf16[64,16,128]{2,1,0:T(8,128)(2,1)} %get-tuple-element.50.upstream, bf16[64,2048]{1,0:T(8,128)(2,1)} %get-tuple-element.51.made), custom_call_target="tpu_custom_call", output_to_operand_aliasing={{}: (4, {})} | custom-call | flops 3000000000 | bytes 2000000 | tf_op jit(solution)/shard_map/pallas_call | solution.py:362
  205.1 9.3 %collective-permute-start.9 = (bf16[64,2048]{1,0:T(8,128)(2,1)}, bf16[64,2048]{1,0:T(8,128)(2,1)S(1)}, u32[]{:S(2)}, u32[]{:S(2)}) collective-permute-start(bf16[64,2048]{1,0:T(8,128)(2,1)} %shard_map.122), channel_id=1, source_target_pairs={{0,128},{128,0},{1,129},{129,1},{2,130},{130,2},{3,131},{131,3},{4... | collective-permute-start | bytes 786440 | tf_op jit(solution)/shard_map/ppermute | solution.py:378
  214.5 1.3 collective-permute-done.9.came
  215.8 0.7 shard_map.124
  (38 shorter events, 2.6 us)
Async XLA Ops:
  0.6 7.6 %copy-start.2 = (f32[1,2,64,2]{2,3,1,0:T(2,128)S(1)}, f32[1,2,64,2]{2,3,1,0:T(2,128)}, u32[]{:S(2)}) copy-start(f32[1,2,64,2]{2,3,1,0:T(2,128)} %param.12) | copy-start | bytes 3076
  1.6 6.6 %collective-permute-start.2 = (bf16[64,2048]{1,0:T(8,128)(2,1)S(1)}, bf16[64,2048]{1,0:T(8,128)(2,1)S(1)}, u32[]{:S(2)}, u32[]{:S(2)}) collective-permute-start(bf16[64,2048]{1,0:T(8,128)(2,1)S(1)} %dynamic-slice_bitcast_fusion), channel_id=1, source_target_pairs={{0,128},{128,0},{1,129},{129,1},{2,130},{130,2},{3,131},{131,3},{4... | collective-permute-start | bytes 786440 | tf_op jit(solution)/shard_map/ppermute | solution.py:378
  6.7 128.8 %copy-start.1 = (s32[2,2,64]{2,1,0:T(2,128)}, s32[2,2,64]{2,1,0:T(2,128)S(1)}, u32[]{:S(2)}) copy-start(s32[2,2,64]{2,1,0:T(2,128)S(1)} %minimum_add_fusion.own_slots.own_in) | copy-start | bytes 3076
  6.7 1.2 collective-permute-start
  6.7 1.5 collective-permute-start.1
  7.8 127.6 %copy-start.3 = (s32[2,2,64]{2,1,0:T(2,128)}, s32[2,2,64]{2,1,0:T(2,128)S(1)}, u32[]{:S(2)}) copy-start(s32[2,2,64]{2,1,0:T(2,128)S(1)} %collective-permute-done.other_slots.other_in) | copy-start | bytes 3076
  13.8 82.7 %all-to-all-start = ((bf16[128,6,16,128]{3,2,1,0:T(8,128)(2,1)}), bf16[128,6,16,128]{3,2,1,0:T(8,128)(2,1)S(1)}, u32[]{:S(2)}, u32[]{:S(2)}) async-start(bf16[128,6,16,128]{3,2,1,0:T(8,128)(2,1)} %get-tuple-element.30), calls=%async_computation | async-start | bytes 6291456 | tf_op jit(solution)/shard_map/all_to_all | solution.py:382
  27.6 9.2 %collective-permute-start.3 = (bf16[2048,384]{1,0:T(8,128)(2,1)}, bf16[2048,384]{1,0:T(8,128)(2,1)S(1)}, u32[]{:S(2)}, u32[]{:S(2)}) collective-permute-start(bf16[2048,384]{1,0:T(8,128)(2,1)} %bitcast.43), channel_id=1, source_target_pairs={{0,128},{128,0},{1,129},{129,1},{2,130},{130,2},{3,131},{131,3},{4... | collective-permute-start | bytes 4718600 | tf_op jit(solution)/shard_map/ppermute | solution.py:378
  31.7 5.5 %collective-permute-start.4 = (bf16[2048,384]{1,0:T(8,128)(2,1)}, bf16[2048,384]{1,0:T(8,128)(2,1)S(1)}, u32[]{:S(2)}, u32[]{:S(2)}) collective-permute-start(bf16[2048,384]{1,0:T(8,128)(2,1)} %bitcast.48), channel_id=1, source_target_pairs={{0,128},{128,0},{1,129},{129,1},{2,130},{130,2},{3,131},{131,3},{4... | collective-permute-start | bytes 4718600 | tf_op jit(solution)/shard_map/ppermute | solution.py:378
  31.8 7.6 %collective-permute-start.5 = (bf16[384,2048]{1,0:T(8,128)(2,1)}, bf16[384,2048]{1,0:T(8,128)(2,1)S(1)}, u32[]{:S(2)}, u32[]{:S(2)}) collective-permute-start(bf16[384,2048]{1,0:T(8,128)(2,1)} %bitcast.53), channel_id=1, source_target_pairs={{0,128},{128,0},{1,129},{129,1},{2,130},{130,2},{3,131},{131,3},{4... | collective-permute-start | bytes 4718600 | tf_op jit(solution)/shard_map/ppermute | solution.py:378
  36.8 2.6 %copy-start.4 = (bf16[2048,384]{1,0:T(8,128)(2,1)}, bf16[2048,384]{1,0:T(8,128)(2,1)S(1)}, u32[]{:S(2)}) copy-start(bf16[2048,384]{1,0:T(8,128)(2,1)S(1)} %collective-permute-done.3.gate.other_gate.matrix_gate) | copy-start | bytes 4718596
  37.2 2.3 %copy-start.5 = (bf16[2048,384]{1,0:T(8,128)(2,1)}, bf16[2048,384]{1,0:T(8,128)(2,1)S(1)}, u32[]{:S(2)}) copy-start(bf16[2048,384]{1,0:T(8,128)(2,1)S(1)} %collective-permute-done.4.up.other_up.matrix_up) | copy-start | bytes 4718596
  39.4 1.2 copy-start.7
  96.5 38.9 %copy-start = (bf16[64,16,128]{2,1,0:T(8,128)(2,1)S(1)}, bf16[64,16,128]{2,1,0:T(8,128)(2,1)}, u32[]{:S(2)}) copy-start(bf16[64,16,128]{2,1,0:T(8,128)(2,1)} %get-tuple-element.38.upstream) | copy-start | bytes 786436
  138.1 29.7 %all-to-all-start.2 = ((bf16[128,2,16,128]{3,2,1,0:T(8,128)(2,1)}), bf16[128,2,16,128]{3,2,1,0:T(8,128)(2,1)}, u32[]{:S(2)}, u32[]{:S(2)}) async-start(bf16[128,2,16,128]{3,2,1,0:T(8,128)(2,1)} %bitcast.57), calls=%async_computation.2 | async-start | bytes 2097152 | tf_op jit(solution)/shard_map/all_to_all | solution.py:382
  167.8 14.3 %copy-start.8 = (bf16[256,2048]{1,0:T(8,128)(2,1)S(1)}, bf16[256,2048]{1,0:T(8,128)(2,1)}, u32[]{:S(2)}) copy-start(bf16[256,2048]{1,0:T(8,128)(2,1)} %get-tuple-element.47) | copy-start | bytes 3145732
  173.2 19.2 %copy-start.9 = (bf16[1,1,384,384]{3,2,1,0:T(8,128)(2,1)S(1)}, bf16[1,1,384,384]{3,2,1,0:T(8,128)(2,1)}, u32[]{:S(2)}) copy-start(bf16[1,1,384,384]{3,2,1,0:T(8,128)(2,1)} %param.16) | copy-start | bytes 884740
  173.2 21.9 %copy-start.6 = (bf16[256,384]{1,0:T(8,128)(2,1)S(1)}, bf16[256,384]{1,0:T(8,128)(2,1)}, u32[]{:S(2)}) copy-start(bf16[256,384]{1,0:T(8,128)(2,1)} %get-tuple-element.46) | copy-start | bytes 589828
  173.2 22.2 %copy-start.10 = (bf16[256,384]{1,0:T(8,128)(2,1)S(1)}, bf16[256,384]{1,0:T(8,128)(2,1)}, u32[]{:S(2)}) copy-start(bf16[256,384]{1,0:T(8,128)(2,1)} %get-tuple-element.45) | copy-start | bytes 589828
  173.2 29.7 %all-to-all-start.3 = ((bf16[128,2,16,128]{3,2,1,0:T(8,128)(2,1)}), bf16[128,2,16,128]{3,2,1,0:T(8,128)(2,1)S(1)}, u32[]{:S(2)}, u32[]{:S(2)}) async-start(bf16[128,2,16,128]{3,2,1,0:T(8,128)(2,1)} %bitcast.56), calls=%async_computation.3 | async-start | bytes 2097152 | tf_op jit(solution)/shard_map/all_to_all | solution.py:382
  183.4 14.6 %collective-permute-start.8 = (bf16[256,2048]{1,0:T(8,128)(2,1)S(1)}, bf16[256,2048]{1,0:T(8,128)(2,1)S(1)}, u32[]{:S(2)}, u32[]{:S(2)}) collective-permute-start(bf16[256,2048]{1,0:T(8,128)(2,1)S(1)} %get-tuple-element.56), channel_id=1, source_target_pairs={{0,128},{128,0},{1,129},{129,1},{2,130},{130,2},{3,131},{131,3},{4... | collective-permute-start | bytes 3145736 | tf_op jit(solution)/shard_map/ppermute | solution.py:378
  192.4 2.7 %collective-permute-start.6 = (bf16[384,384]{1,0:T(8,128)(2,1)S(1)}, bf16[384,384]{1,0:T(8,128)(2,1)S(1)}, u32[]{:S(2)}, u32[]{:S(2)}) collective-permute-start(bf16[384,384]{1,0:T(8,128)(2,1)S(1)} %bitcast.60), channel_id=1, source_target_pairs={{0,128},{128,0},{1,129},{129,1},{2,130},{130,2},{3,131},{131,3},{4... | collective-permute-start | bytes 884744 | tf_op jit(solution)/shard_map/ppermute | solution.py:378
  195.7 2.3 %collective-permute-start.7 = (bf16[256,384]{1,0:T(8,128)(2,1)S(1)}, bf16[256,384]{1,0:T(8,128)(2,1)S(1)}, u32[]{:S(2)}, u32[]{:S(2)}) collective-permute-start(bf16[256,384]{1,0:T(8,128)(2,1)S(1)} %get-tuple-element.58), channel_id=1, source_target_pairs={{0,128},{128,0},{1,129},{129,1},{2,130},{130,2},{3,131},{131,3},{4... | collective-permute-start | bytes 589832 | tf_op jit(solution)/shard_map/ppermute | solution.py:378
  205.1 10.7 %collective-permute-start.9 = (bf16[64,2048]{1,0:T(8,128)(2,1)}, bf16[64,2048]{1,0:T(8,128)(2,1)S(1)}, u32[]{:S(2)}, u32[]{:S(2)}) collective-permute-start(bf16[64,2048]{1,0:T(8,128)(2,1)} %shard_map.122), channel_id=1, source_target_pairs={{0,128},{128,0},{1,129},{129,1},{2,130},{130,2},{3,131},{131,3},{4... | collective-permute-start | bytes 786440 | tf_op jit(solution)/shard_map/ppermute | solution.py:378

commit v7 on v6

--- a/solution.py
+++ b/solution.py
@@ -154,7 +154,7 @@
             send[slot(0, k, t)] = (weight * g).astype(BF16)
         return carry
 
-    lax.fori_loop(0, tokens, token, 0, unroll=4)
+    lax.fori_loop(0, tokens, token, 0, unroll=8)
     saves = [fetch(send, sent, sems.at[0]), fetch(grads, grad_out, sems.at[1])]
     for copy in saves:
         copy.wait()
@@ -274,11 +274,11 @@
     depth = send.shape[1]
     gate_copy = fetch_one_of(mine, own_gate, other_gate, gate, sems.at[0])
     up_copy = fetch_one_of(mine, own_up, other_up, up, sems.at[1])
-    down_copy = fetch_one_of(mine, own_dt, other_dt, down_t, sems.at[2])
-    back_copy = fetch_one_of(mine, own_gut, other_gut, gate_up_t, sems.at[3])
     untile(arrived[:, :CAP], tiles, x_rows, depth)
     gate_copy.wait()
     up_copy.wait()
+    down_copy = fetch_one_of(mine, own_dt, other_dt, down_t, sems.at[2])
+    back_copy = fetch_one_of(mine, own_gut, other_gut, gate_up_t, sems.at[3])
     act, slope, rounded = forward_parts(x_rows, gate, up)
     activ[...] = rounded
     untile(arrived[:, CAP : 2 * CAP], tiles, dy_rows, depth)
@@ -326,11 +326,12 @@
         for n in range(pieces)
     ]
     down_copy = fetch_one_of(mine, own_dt, other_dt, down_t, sems.at[0])
-    act_copy = fetch(act_in, act, sems.at[1])
-    slope_copy = fetch(slope_in, slope, sems.at[2])
-    back_copy = fetch_one_of(mine, own_gut, other_gut, gate_up_t, sems.at[3])
     for n, copy in enumerate(arriving):
         copy.wait()
+        if n == 1:
+            act_copy = fetch(act_in, act, sems.at[1])
+            slope_copy = fetch(slope_in, slope, sems.at[2])
+            back_copy = fetch_one_of(mine, own_gut, other_gut, gate_up_t, sems.at[3])
         tiles[n * part * depth : (n + 1) * part * depth, :] = (
             dy[n * part : (n + 1) * part].astype(F32).reshape(part * depth, LANES)
         )

time: 217 us -> 218 us (level)
  no operation moved by 1% of the time
where the time goes in v7:
time: 218 us; the launch traced here: 217 us
  waiting for transfers between devices  75 us (34%)
  starting transfers between devices  59.2 us (27%)
  Pallas kernels  39.7 us (18%)
  blocking collectives  31.6 us (14%)
  matrix products  5.41 us (2%)
  other arithmetic  3.08 us (1%)
  local copies, waits for them, and re-layouts  2.21 us (1%)
    all_to_all x3, waiting for transfers between devices, exchanged(): lax.all_to_all(block, 'expert', split_axis=0, concat_axis=0, tiled=True)  67.5 us
    pallas_call x13, Pallas kernels, call(): pl.pallas_call(kernel, in_specs=in_specs, out_shape=tuple((pltpu.HBM(out....  39.7 us
    all_to_all x3, starting transfers between devices, exchanged(): lax.all_to_all(block, 'expert', split_axis=0, concat_axis=0, tiled=True)  31.9 us
    all_to_all x1, blocking collectives, exchanged(): lax.all_to_all(block, 'expert', split_axis=0, concat_axis=0, tiled=True)  31.6 us
    ppermute x10, starting transfers between devices, swapped(): return lax.ppermute(block, 'segment', [(0, 1), (1, 0)])  27.2 us
    ppermute x10, waiting for transfers between devices, swapped(): return lax.ppermute(block, 'segment', [(0, 1), (1, 0)])  7.52 us
  transfers between devices with their start and end apart: 13, of which 8 were waited for; matrix products, arithmetic and copies ran while one was open for 4% of the time, Pallas kernels for 7%

profile of v7, /device:TPU:1, one launch (start us, length us, event | category | flops | bytes accessed | tf_op | source)
XLA Modules:
  0.0 217.2 jit_solution(10554671540538896737)
XLA Ops:
  0.6 1.0 dynamic-slice_bitcast_fusion
  1.6 3.3 %collective-permute-start.2 = (bf16[64,2048]{1,0:T(8,128)(2,1)S(1)}, bf16[64,2048]{1,0:T(8,128)(2,1)S(1)}, u32[]{:S(2)}, u32[]{:S(2)}) collective-permute-start(bf16[64,2048]{1,0:T(8,128)(2,1)S(1)} %dynamic-slice_bitcast_fusion), channel_id=1, source_target_pairs={{0,128},{128,0},{1,129},{129,1},{2,130},{130,2},{3,131},{131,3},{4... | collective-permute-start | bytes 786440 | tf_op jit(solution)/shard_map/ppermute | solution.py:379
  4.9 1.0 convert_reduce_fusion
  6.0 0.7 minimum_add_fusion.own_slots.own_in
  6.7 0.5 collective-permute-start.1
  7.2 0.6 collective-permute-done.other_slots.other_in
  8.2 5.6 %shard_map.113 = (bf16[128,6,16,128]{3,2,1,0:T(8,128)(2,1)}, bf16[64,16,128]{2,1,0:T(8,128)(2,1)}) custom-call(s32[2,2,64]{2,1,0:T(2,128)S(1)} %minimum_add_fusion.own_slots.own_in, s32[2,2,64]{2,1,0:T(2,128)S(1)} %collective-permute-done.other_slots.other_in, f32[2,2,64]{2,1,0:T(2,128)S(1)} %bitcast.40, f32[2,2,64]{2,1,0:T(2,128)S(1)} %collective-permute-done.1.other_w, ...), custom_call_target="tpu_custom_call" | custom-call | flops 1000000 | bytes 5000000 | tf_op jit(solution)/shard_map/pallas_call | solution.py:363
  13.8 13.8 %all-to-all-start = ((bf16[128,6,16,128]{3,2,1,0:T(8,128)(2,1)}), bf16[128,6,16,128]{3,2,1,0:T(8,128)(2,1)S(1)}, u32[]{:S(2)}, u32[]{:S(2)}) async-start(bf16[128,6,16,128]{3,2,1,0:T(8,128)(2,1)} %get-tuple-element.30), calls=%async_computation | async-start | bytes 6291456 | tf_op jit(solution)/shard_map/all_to_all | solution.py:383
  27.6 4.1 %collective-permute-start.3 = (bf16[2048,384]{1,0:T(8,128)(2,1)}, bf16[2048,384]{1,0:T(8,128)(2,1)S(1)}, u32[]{:S(2)}, u32[]{:S(2)}) collective-permute-start(bf16[2048,384]{1,0:T(8,128)(2,1)} %bitcast.43), channel_id=1, source_target_pairs={{0,128},{128,0},{1,129},{129,1},{2,130},{130,2},{3,131},{131,3},{4... | collective-permute-start | bytes 4718600 | tf_op jit(solution)/shard_map/ppermute | solution.py:379
  32.2 4.6 %shard_map.114 = (bf16[768,2048]{1,0:T(8,128)(2,1)}, bf16[2048,384]{1,0:T(8,128)(2,1)}) custom-call(bf16[2048,384]{1,0:T(8,128)(2,1)} %bitcast.44, bf16[2048,384]{1,0:T(8,128)(2,1)} %bitcast.49, bf16[384,2048]{1,0:T(8,128)(2,1)} %bitcast.54, bf16[768,2048]{1,0:T(8,128)(2,1)} %get-tuple-element.31.refs_0_, ...), custom_call_target="tpu_custom_call", output_to_operand_aliasing={{0}: (3, {}), {1}: (4, {})} | custom-call | flops 1000000 | bytes 9000000 | tf_op jit(solution)/shard_map/pallas_call | solution.py:363
  37.2 2.2 %collective-permute-done.5.down = bf16[384,2048]{1,0:T(8,128)(2,1)S(1)} collective-permute-done((bf16[384,2048]{1,0:T(8,128)(2,1)}, bf16[384,2048]{1,0:T(8,128)(2,1)S(1)}, u32[]{:S(2)}, u32[]{:S(2)}) %collective-permute-start.5) | collective-permute-done | bytes 1572896 | tf_op jit(solution)/shard_map/ppermute | solution.py:379
  39.4 1.2 copy-done.7
  40.6 4.5 %shard_map.115 = (bf16[768,2048]{1,0:T(8,128)(2,1)}, bf16[2048,384]{1,0:T(8,128)(2,1)}) custom-call(bf16[2048,384]{1,0:T(8,128)(2,1)} %copy-done.4, bf16[2048,384]{1,0:T(8,128)(2,1)} %copy-done.5, bf16[384,2048]{1,0:T(8,128)(2,1)} %copy-done.7), custom_call_target="tpu_custom_call" | custom-call | flops 1000000 | bytes 9000000 | tf_op jit(solution)/shard_map/pallas_call | solution.py:363
  45.1 51.3 %all-to-all-done.arrived = bf16[128,6,16,128]{3,2,1,0:T(8,128)(2,1)S(1)} async-done(((bf16[128,6,16,128]{3,2,1,0:T(8,128)(2,1)}), bf16[128,6,16,128]{3,2,1,0:T(8,128)(2,1)S(1)}, u32[]{:S(2)}, u32[]{:S(2)}) %all-to-all-start) | async-done | bytes 3145760 | tf_op jit(solution)/shard_map/all_to_all | solution.py:383
  96.5 7.3 %shard_map.117 = (bf16[256,16,128]{2,1,0:T(8,128)(2,1)}, bf16[256,2048]{1,0:T(8,128)(2,1)}, bf16[256,384]{1,0:T(8,128)(2,1)}) custom-call(bf16[128,6,16,128]{3,2,1,0:T(8,128)(2,1)S(1)} %all-to-all-done.arrived, bf16[2048,384]{1,0:T(8,128)(2,1)} %bitcast.46, bf16[2048,384]{1,0:T(8,128)(2,1)} %copy-done.4, bf16[2048,384]{1,0:T(8,128)(2,1)} %bitcast.51, ...), custom_call_target="tpu_custom_call" | custom-call | flops 2013265920 | bytes 9000000 | tf_op jit(solution)/shard_map/pallas_call | solution.py:363
  103.9 31.6 %all_to_all.20 = bf16[128,2,16,128]{3,2,1,0:T(8,128)(2,1)S(1)} all-to-all(bf16[128,2,16,128]{3,2,1,0:T(8,128)(2,1)} %bitcast.58), channel_id=1, replica_groups=mesh['segment'=2,'expert'=128] {'expert'}, dimensions={0} | all-to-all | bytes 2097152 | tf_op jit(solution)/shard_map/all_to_all | solution.py:383
  135.5 2.7 %shard_map.118 = (bf16[256,16,128]{2,1,0:T(8,128)(2,1)}, bf16[64,16,128]{2,1,0:T(8,128)(2,1)}) custom-call(s32[2,2,64]{2,1,0:T(2,128)S(1)} %minimum_add_fusion.own_slots.own_in, s32[2,2,64]{2,1,0:T(2,128)S(1)} %collective-permute-done.other_slots.other_in, f32[2,2,64]{2,1,0:T(2,128)S(1)} %bitcast.41, f32[2,2,64]{2,1,0:T(2,128)S(1)} %collective-permute-done.1.other_w, ...), custom_call_target="tpu_custom_call" | custom-call | flops 1000000 | bytes 3000000 | tf_op jit(solution)/shard_map/pallas_call | solution.py:363
  138.2 9.3 %all-to-all-start.2 = ((bf16[128,2,16,128]{3,2,1,0:T(8,128)(2,1)}), bf16[128,2,16,128]{3,2,1,0:T(8,128)(2,1)}, u32[]{:S(2)}, u32[]{:S(2)}) async-start(bf16[128,2,16,128]{3,2,1,0:T(8,128)(2,1)} %bitcast.57), calls=%async_computation.2 | async-start | bytes 2097152 | tf_op jit(solution)/shard_map/all_to_all | solution.py:383
  147.5 4.2 %shard_map.119 = (f32[256,384]{1,0:T(8,128)}, f32[256,384]{1,0:T(8,128)}, bf16[256,384]{1,0:T(8,128)(2,1)}) custom-call(bf16[128,6,16,128]{3,2,1,0:T(8,128)(2,1)S(1)} %all-to-all-done.arrived, bf16[2048,384]{1,0:T(8,128)(2,1)} %copy-done.4, bf16[2048,384]{1,0:T(8,128)(2,1)} %copy-done.5, ...), custom_call_target="tpu_custom_call", output_to_operand_aliasing={{0}: (3, {}), {1}: (4, {}), {2}: (5, {})} | custom-call | flops 805306368 | bytes 5000000 | tf_op jit(solution)/shard_map/pallas_call | solution.py:363
  151.7 16.2 %all-to-all-done.2 = bf16[128,2,16,128]{3,2,1,0:T(8,128)(2,1)} async-done(((bf16[128,2,16,128]{3,2,1,0:T(8,128)(2,1)}), bf16[128,2,16,128]{3,2,1,0:T(8,128)(2,1)}, u32[]{:S(2)}, u32[]{:S(2)}) %all-to-all-start.2) | async-done | bytes 1048608 | tf_op jit(solution)/shard_map/all_to_all | solution.py:383
  167.9 5.8 %shard_map.120 = (bf16[256,16,128]{2,1,0:T(8,128)(2,1)}, bf16[256,2048]{1,0:T(8,128)(2,1)}) custom-call(bf16[256,16,128]{2,1,0:T(8,128)(2,1)} %bitcast.14.dy_in, f32[256,384]{1,0:T(8,128)} %get-tuple-element.42.act_in, f32[256,384]{1,0:T(8,128)} %get-tuple-element.43.slope_in, bf16[2048,384]{1,0:T(8,128)(2,1)} %get-tuple-element.32.own_dt, ...), custom_call_target="tpu_custom_call" | custom-call | flops 1207959552 | bytes 8000000 | tf_op jit(solution)/shard_map/pallas_call | solution.py:363
  173.7 8.9 %all-to-all-start.3 = ((bf16[128,2,16,128]{3,2,1,0:T(8,128)(2,1)}), bf16[128,2,16,128]{3,2,1,0:T(8,128)(2,1)S(1)}, u32[]{:S(2)}, u32[]{:S(2)}) async-start(bf16[128,2,16,128]{3,2,1,0:T(8,128)(2,1)} %bitcast.56), calls=%async_computation.3 | async-start | bytes 2097152 | tf_op jit(solution)/shard_map/all_to_all | solution.py:383
  182.6 1.4 broadcast_select_fusion.1
  184.0 8.9 %collective-permute-start.8 = (bf16[256,2048]{1,0:T(8,128)(2,1)S(1)}, bf16[256,2048]{1,0:T(8,128)(2,1)S(1)}, u32[]{:S(2)}, u32[]{:S(2)}) collective-permute-start(bf16[256,2048]{1,0:T(8,128)(2,1)S(1)} %get-tuple-element.56), channel_id=1, source_target_pairs={{0,128},{128,0},{1,129},{129,1},{2,130},{130,2},{3,131},{131,3},{4... | collective-permute-start | bytes 3145736 | tf_op jit(solution)/shard_map/ppermute | solution.py:379
  193.0 2.6 %collective-permute-done.6 = bf16[384,384]{1,0:T(8,128)(2,1)S(1)} collective-permute-done((bf16[384,384]{1,0:T(8,128)(2,1)S(1)}, bf16[384,384]{1,0:T(8,128)(2,1)S(1)}, u32[]{:S(2)}, u32[]{:S(2)}) %collective-permute-start.6) | collective-permute-done | bytes 294944 | tf_op jit(solution)/shard_map/ppermute | solution.py:379
  196.7 1.9 shard_map.121
  198.6 2.2 multiply_convert_fusion.1
  200.8 2.7 %convolution_multiply_fusion = f32[384,2048]{1,0:T(8,128)} fusion(bf16[256,2048]{1,0:T(8,128)(2,1)S(1)} %collective-permute-done.8, bf16[256,2048]{1,0:T(8,128)(2,1)S(1)} %get-tuple-element.55, bf16[256,384]{1,0:T(8,128)(2,1)S(1)} %collective-permute-done.7, bf16[256,384]{1,0:T(8,128)(2,1)S(1)} %get-tuple-element.57), kind=kOutput, calls=%fused_computation.2 | convolution fusion | flops 813563904 | bytes 5636096 | tf_op jit(solution)/shard_map/dot_general | solution.py:572
  203.5 2.2 %shard_map.122 = bf16[64,2048]{1,0:T(8,128)(2,1)} custom-call(s32[2,2,64]{2,1,0:T(2,128)} %copy-done.1, s32[2,2,64]{2,1,0:T(2,128)} %copy-done.3, bf16[256,16,128]{2,1,0:T(8,128)(2,1)S(1)} %bitcast.37, bf16[64,16,128]{2,1,0:T(8,128)(2,1)} %get-tuple-element.50.upstream, bf16[64,2048]{1,0:T(8,128)(2,1)} %get-tuple-element.51.made), custom_call_target="tpu_custom_call", output_to_operand_aliasing={{}: (4, {})} | custom-call | flops 3000000000 | bytes 2000000 | tf_op jit(solution)/shard_map/pallas_call | solution.py:363
  205.7 9.3 %collective-permute-start.9 = (bf16[64,2048]{1,0:T(8,128)(2,1)}, bf16[64,2048]{1,0:T(8,128)(2,1)S(1)}, u32[]{:S(2)}, u32[]{:S(2)}) collective-permute-start(bf16[64,2048]{1,0:T(8,128)(2,1)} %shard_map.122), channel_id=1, source_target_pairs={{0,128},{128,0},{1,129},{129,1},{2,130},{130,2},{3,131},{131,3},{4... | collective-permute-start | bytes 786440 | tf_op jit(solution)/shard_map/ppermute | solution.py:379
  215.0 1.3 collective-permute-done.9.came
  216.3 0.7 shard_map.124
  (38 shorter events, 2.6 us)
Async XLA Ops:
  0.6 7.6 %copy-start.2 = (f32[1,2,64,2]{2,3,1,0:T(2,128)S(1)}, f32[1,2,64,2]{2,3,1,0:T(2,128)}, u32[]{:S(2)}) copy-start(f32[1,2,64,2]{2,3,1,0:T(2,128)} %param.12) | copy-start | bytes 3076
  1.6 6.6 %collective-permute-start.2 = (bf16[64,2048]{1,0:T(8,128)(2,1)S(1)}, bf16[64,2048]{1,0:T(8,128)(2,1)S(1)}, u32[]{:S(2)}, u32[]{:S(2)}) collective-permute-start(bf16[64,2048]{1,0:T(8,128)(2,1)S(1)} %dynamic-slice_bitcast_fusion), channel_id=1, source_target_pairs={{0,128},{128,0},{1,129},{129,1},{2,130},{130,2},{3,131},{131,3},{4... | collective-permute-start | bytes 786440 | tf_op jit(solution)/shard_map/ppermute | solution.py:379
  6.7 128.8 %copy-start.1 = (s32[2,2,64]{2,1,0:T(2,128)}, s32[2,2,64]{2,1,0:T(2,128)S(1)}, u32[]{:S(2)}) copy-start(s32[2,2,64]{2,1,0:T(2,128)S(1)} %minimum_add_fusion.own_slots.own_in) | copy-start | bytes 3076
  6.7 1.2 collective-permute-start
  6.7 1.5 collective-permute-start.1
  7.8 127.7 %copy-start.3 = (s32[2,2,64]{2,1,0:T(2,128)}, s32[2,2,64]{2,1,0:T(2,128)S(1)}, u32[]{:S(2)}) copy-start(s32[2,2,64]{2,1,0:T(2,128)S(1)} %collective-permute-done.other_slots.other_in) | copy-start | bytes 3076
  13.8 82.7 %all-to-all-start = ((bf16[128,6,16,128]{3,2,1,0:T(8,128)(2,1)}), bf16[128,6,16,128]{3,2,1,0:T(8,128)(2,1)S(1)}, u32[]{:S(2)}, u32[]{:S(2)}) async-start(bf16[128,6,16,128]{3,2,1,0:T(8,128)(2,1)} %get-tuple-element.30), calls=%async_computation | async-start | bytes 6291456 | tf_op jit(solution)/shard_map/all_to_all | solution.py:383
  27.6 9.2 %collective-permute-start.3 = (bf16[2048,384]{1,0:T(8,128)(2,1)}, bf16[2048,384]{1,0:T(8,128)(2,1)S(1)}, u32[]{:S(2)}, u32[]{:S(2)}) collective-permute-start(bf16[2048,384]{1,0:T(8,128)(2,1)} %bitcast.43), channel_id=1, source_target_pairs={{0,128},{128,0},{1,129},{129,1},{2,130},{130,2},{3,131},{131,3},{4... | collective-permute-start | bytes 4718600 | tf_op jit(solution)/shard_map/ppermute | solution.py:379
  31.7 5.5 %collective-permute-start.4 = (bf16[2048,384]{1,0:T(8,128)(2,1)}, bf16[2048,384]{1,0:T(8,128)(2,1)S(1)}, u32[]{:S(2)}, u32[]{:S(2)}) collective-permute-start(bf16[2048,384]{1,0:T(8,128)(2,1)} %bitcast.48), channel_id=1, source_target_pairs={{0,128},{128,0},{1,129},{129,1},{2,130},{130,2},{3,131},{131,3},{4... | collective-permute-start | bytes 4718600 | tf_op jit(solution)/shard_map/ppermute | solution.py:379
  31.8 7.6 %collective-permute-start.5 = (bf16[384,2048]{1,0:T(8,128)(2,1)}, bf16[384,2048]{1,0:T(8,128)(2,1)S(1)}, u32[]{:S(2)}, u32[]{:S(2)}) collective-permute-start(bf16[384,2048]{1,0:T(8,128)(2,1)} %bitcast.53), channel_id=1, source_target_pairs={{0,128},{128,0},{1,129},{129,1},{2,130},{130,2},{3,131},{131,3},{4... | collective-permute-start | bytes 4718600 | tf_op jit(solution)/shard_map/ppermute | solution.py:379
  36.8 2.6 %copy-start.4 = (bf16[2048,384]{1,0:T(8,128)(2,1)}, bf16[2048,384]{1,0:T(8,128)(2,1)S(1)}, u32[]{:S(2)}) copy-start(bf16[2048,384]{1,0:T(8,128)(2,1)S(1)} %collective-permute-done.3.gate.other_gate.matrix_gate) | copy-start | bytes 4718596
  37.2 2.3 %copy-start.5 = (bf16[2048,384]{1,0:T(8,128)(2,1)}, bf16[2048,384]{1,0:T(8,128)(2,1)S(1)}, u32[]{:S(2)}) copy-start(bf16[2048,384]{1,0:T(8,128)(2,1)S(1)} %collective-permute-done.4.up.other_up.matrix_up) | copy-start | bytes 4718596
  39.4 1.2 copy-start.7
  96.5 39.0 %copy-start = (bf16[64,16,128]{2,1,0:T(8,128)(2,1)S(1)}, bf16[64,16,128]{2,1,0:T(8,128)(2,1)}, u32[]{:S(2)}) copy-start(bf16[64,16,128]{2,1,0:T(8,128)(2,1)} %get-tuple-element.38.upstream) | copy-start | bytes 786436
  138.2 29.7 %all-to-all-start.2 = ((bf16[128,2,16,128]{3,2,1,0:T(8,128)(2,1)}), bf16[128,2,16,128]{3,2,1,0:T(8,128)(2,1)}, u32[]{:S(2)}, u32[]{:S(2)}) async-start(bf16[128,2,16,128]{3,2,1,0:T(8,128)(2,1)} %bitcast.57), calls=%async_computation.2 | async-start | bytes 2097152 | tf_op jit(solution)/shard_map/all_to_all | solution.py:383
  167.9 14.7 %copy-start.8 = (bf16[256,2048]{1,0:T(8,128)(2,1)S(1)}, bf16[256,2048]{1,0:T(8,128)(2,1)}, u32[]{:S(2)}) copy-start(bf16[256,2048]{1,0:T(8,128)(2,1)} %get-tuple-element.47) | copy-start | bytes 3145732
  173.7 19.2 %copy-start.9 = (bf16[1,1,384,384]{3,2,1,0:T(8,128)(2,1)S(1)}, bf16[1,1,384,384]{3,2,1,0:T(8,128)(2,1)}, u32[]{:S(2)}) copy-start(bf16[1,1,384,384]{3,2,1,0:T(8,128)(2,1)} %param.16) | copy-start | bytes 884740
  173.7 21.9 %copy-start.6 = (bf16[256,384]{1,0:T(8,128)(2,1)S(1)}, bf16[256,384]{1,0:T(8,128)(2,1)}, u32[]{:S(2)}) copy-start(bf16[256,384]{1,0:T(8,128)(2,1)} %get-tuple-element.46) | copy-start | bytes 589828
  173.7 22.2 %copy-start.10 = (bf16[256,384]{1,0:T(8,128)(2,1)S(1)}, bf16[256,384]{1,0:T(8,128)(2,1)}, u32[]{:S(2)}) copy-start(bf16[256,384]{1,0:T(8,128)(2,1)} %get-tuple-element.45) | copy-start | bytes 589828
  173.7 29.7 %all-to-all-start.3 = ((bf16[128,2,16,128]{3,2,1,0:T(8,128)(2,1)}), bf16[128,2,16,128]{3,2,1,0:T(8,128)(2,1)S(1)}, u32[]{:S(2)}, u32[]{:S(2)}) async-start(bf16[128,2,16,128]{3,2,1,0:T(8,128)(2,1)} %bitcast.56), calls=%async_computation.3 | async-start | bytes 2097152 | tf_op jit(solution)/shard_map/all_to_all | solution.py:383
  184.0 14.6 %collective-permute-start.8 = (bf16[256,2048]{1,0:T(8,128)(2,1)S(1)}, bf16[256,2048]{1,0:T(8,128)(2,1)S(1)}, u32[]{:S(2)}, u32[]{:S(2)}) collective-permute-start(bf16[256,2048]{1,0:T(8,128)(2,1)S(1)} %get-tuple-element.56), channel_id=1, source_target_pairs={{0,128},{128,0},{1,129},{129,1},{2,130},{130,2},{3,131},{131,3},{4... | collective-permute-start | bytes 3145736 | tf_op jit(solution)/shard_map/ppermute | solution.py:379
  192.9 2.7 %collective-permute-start.6 = (bf16[384,384]{1,0:T(8,128)(2,1)S(1)}, bf16[384,384]{1,0:T(8,128)(2,1)S(1)}, u32[]{:S(2)}, u32[]{:S(2)}) collective-permute-start(bf16[384,384]{1,0:T(8,128)(2,1)S(1)} %bitcast.60), channel_id=1, source_target_pairs={{0,128},{128,0},{1,129},{129,1},{2,130},{130,2},{3,131},{131,3},{4... | collective-permute-start | bytes 884744 | tf_op jit(solution)/shard_map/ppermute | solution.py:379
  196.2 2.4 %collective-permute-start.7 = (bf16[256,384]{1,0:T(8,128)(2,1)S(1)}, bf16[256,384]{1,0:T(8,128)(2,1)S(1)}, u32[]{:S(2)}, u32[]{:S(2)}) collective-permute-start(bf16[256,384]{1,0:T(8,128)(2,1)S(1)} %get-tuple-element.58), channel_id=1, source_target_pairs={{0,128},{128,0},{1,129},{129,1},{2,130},{130,2},{3,131},{131,3},{4... | collective-permute-start | bytes 589832 | tf_op jit(solution)/shard_map/ppermute | solution.py:379
  205.7 10.7 %collective-permute-start.9 = (bf16[64,2048]{1,0:T(8,128)(2,1)}, bf16[64,2048]{1,0:T(8,128)(2,1)S(1)}, u32[]{:S(2)}, u32[]{:S(2)}) collective-permute-start(bf16[64,2048]{1,0:T(8,128)(2,1)} %shard_map.122), channel_id=1, source_target_pairs={{0,128},{128,0},{1,129},{129,1},{2,130},{130,2},{3,131},{131,3},{4... | collective-permute-start | bytes 786440 | tf_op jit(solution)/shard_map/ppermute | solution.py:379
